TPU v7x, 32 devices: a whole 2x2x4 slice. The times are simulated.
32 devices in a mesh: grp: 4 (over y, core), fsdp: 8 (over z, x).
Axes of the slice: x: 2, y: 2, z: 4, core: 2. Of those that a mesh axis runs over, the one named last changes fastest.
Arguments:
- tokens: bfloat16 [64, 512, 768], P('grp', 'fsdp'), may hold values from -6 to 6
- frames: bfloat16 [64, 1536, 768], P('grp', 'fsdp'), may hold values from -6 to 6
- lengths: int32 [64], P('grp'), may hold values from 1 to 448, as said below
- cotangent: bfloat16 [64, 512, 768], P('grp', 'fsdp'), may hold values from -6 to 6
- self_in: bfloat16 [768, 2304], P(('grp', 'fsdp')), may hold values from -0.21875 to 0.21875
- self_out: bfloat16 [768, 768], P(('grp', 'fsdp')), may hold values from -1.75 to 1.75
- cross_q: bfloat16 [768, 768], P(('grp', 'fsdp')), may hold values from -0.21875 to 0.21875
- cross_kv: bfloat16 [768, 1536], P(('grp', 'fsdp')), may hold values from -0.21875 to 0.21875
- cross_out: bfloat16 [768, 768], P(('grp', 'fsdp')), may hold values from -1.75 to 1.75
- fc_in: bfloat16 [768, 3072], P(('grp', 'fsdp')), may hold values from -0.21875 to 0.21875
- fc_out: bfloat16 [3072, 768], P(('grp', 'fsdp')), may hold values from -0.109375 to 0.109375
- norm_gain: bfloat16 [768, 4], P(('grp', 'fsdp')), may hold values from 0.25 to 1.75
- norm_bias: bfloat16 [768, 4], P(('grp', 'fsdp')), may hold values from -3 to 3
Outputs:
- output: bfloat16 [64, 512, 768], P('grp', 'fsdp')
- grad_tokens: bfloat16 [64, 512, 768], P('grp', 'fsdp')
- grad_frames: bfloat16 [64, 1536, 768], P('grp', 'fsdp')
- grad_self_in: float32 [768, 2304], P(('grp', 'fsdp'))
- grad_self_out: float32 [768, 768], P(('grp', 'fsdp'))
- grad_cross_q: float32 [768, 768], P(('grp', 'fsdp'))
- grad_cross_kv: float32 [768, 1536], P(('grp', 'fsdp'))
- grad_cross_out: float32 [768, 768], P(('grp', 'fsdp'))
- grad_fc_in: float32 [768, 3072], P(('grp', 'fsdp'))
- grad_fc_out: float32 [3072, 768], P(('grp', 'fsdp'))
- grad_norm_gain: float32 [768, 4], P(('grp', 'fsdp'))
- grad_norm_bias: float32 [768, 4], P(('grp', 'fsdp'))
Inputs may be any that keep to these rules, and one draw needn't show every extreme that they name: `lengths`: each group of 16 sequences that one index of grp holds has one sequence of exactly 448 tokens; slots from a sequence's length on are padding.
All inputs are finite; a program needn't handle non-finite values.
Results may differ from a plain program's by a relative error of at most 0.02.
Values may be sent and summed in bfloat16 or wider, within the bound.
No kernel may reach another device: no remote copies, remote signals or barrier semaphores. Data moves between devices by JAX's collectives and lax.ppermute only.
A program may use at most 512 MiB of HBM per device.

v0:
```python
import jax
import jax.numpy as jnp
import numpy as np
from jax import lax
from jax.sharding import PartitionSpec as P

D = 768
HEAD_DIM = 64
FRAMES = 1500


eps_norm = 1e-05
neg_big = -1e30
head_scale = 0.125


def layer_norm(inputs, gain_vec, shift_vec):
    average = jnp.mean(inputs, axis=-1, keepdims=True)
    centered = inputs - average
    variance = jnp.mean(centered * centered, axis=-1, keepdims=True)
    return centered * lax.rsqrt(variance + eps_norm) * gain_vec + shift_vec


def exact_gelu(inputs):
    return jax.nn.gelu(inputs, approximate=False)


def seen_keys(row_start, block_rows, key_count, key_limit, causal):
    row_ids = row_start + lax.broadcasted_iota(jnp.int32, (block_rows, key_count), 0)
    col_ids = lax.broadcasted_iota(jnp.int32, (block_rows, key_count), 1)
    allowed = col_ids < key_limit
    if causal:
        allowed = allowed & (col_ids <= row_ids)
    return allowed


def attend_forward(queries, key_vecs, value_vecs, key_limit, causal):
    query_count = queries.shape[0]
    key_count = key_vecs.shape[0]
    block_rows = min(512, query_count)
    head_count = queries.shape[1] // HEAD_DIM
    key_heads = key_vecs.reshape(key_count, head_count, HEAD_DIM)
    value_heads = value_vecs.reshape(key_count, head_count, HEAD_DIM)

    def per_block(block_id):
        row_start = block_id * block_rows
        query_heads = lax.dynamic_slice_in_dim(queries, row_start, block_rows, 0).reshape(
            block_rows, head_count, HEAD_DIM
        )
        scores = jnp.einsum(
            "qhd,khd->hqk", query_heads, key_heads, preferred_element_type=jnp.float32
        )
        scores = jnp.where(
            seen_keys(row_start, block_rows, key_count, key_limit, causal)[None], scores, neg_big
        )
        peak_score = jnp.max(scores, axis=-1, keepdims=True)
        exp_scores = jnp.exp(scores - peak_score)
        exp_total = jnp.sum(exp_scores, axis=-1, keepdims=True)
        softmaxed = (exp_scores / exp_total).astype(jnp.bfloat16)
        mixture = jnp.einsum(
            "hqk,khd->qhd", softmaxed, value_heads, preferred_element_type=jnp.float32
        )
        return (
            mixture.reshape(block_rows, head_count * HEAD_DIM).astype(jnp.bfloat16),
            (peak_score + jnp.log(exp_total))[..., 0],
        )

    mixture, log_sums = lax.map(per_block, jnp.arange(query_count // block_rows, dtype=jnp.int32))
    return (mixture.reshape(query_count, head_count * HEAD_DIM), log_sums)


def attend_backward(queries, key_vecs, value_vecs, grad_mixture, log_sums, key_limit, causal):
    query_count = queries.shape[0]
    key_count = key_vecs.shape[0]
    block_rows = min(512, query_count)
    head_count = queries.shape[1] // HEAD_DIM
    key_heads = key_vecs.reshape(key_count, head_count, HEAD_DIM)
    value_heads = value_vecs.reshape(key_count, head_count, HEAD_DIM)

    def per_block(sums_kv, scanned):
        block_id, block_sums = scanned
        grad_keys, grad_values = sums_kv
        row_start = block_id * block_rows
        query_heads = lax.dynamic_slice_in_dim(queries, row_start, block_rows, 0).reshape(
            block_rows, head_count, HEAD_DIM
        )
        grad_heads = lax.dynamic_slice_in_dim(grad_mixture, row_start, block_rows, 0).reshape(
            block_rows, head_count, HEAD_DIM
        )
        scores = jnp.einsum(
            "qhd,khd->hqk", query_heads, key_heads, preferred_element_type=jnp.float32
        )
        scores = jnp.where(
            seen_keys(row_start, block_rows, key_count, key_limit, causal)[None], scores, neg_big
        )
        softmaxed = jnp.exp(scores - block_sums[..., None])
        grad_values = grad_values + jnp.einsum(
            "hqk,qhd->khd",
            softmaxed.astype(jnp.bfloat16),
            grad_heads,
            preferred_element_type=jnp.float32,
        )
        grad_probs = jnp.einsum(
            "qhd,khd->hqk", grad_heads, value_heads, preferred_element_type=jnp.float32
        )
        inner_sum = jnp.sum(softmaxed * grad_probs, axis=-1, keepdims=True)
        grad_scores = (softmaxed * (grad_probs - inner_sum)).astype(jnp.bfloat16)
        grad_keys = grad_keys + jnp.einsum(
            "hqk,qhd->khd", grad_scores, query_heads, preferred_element_type=jnp.float32
        )
        grad_query = jnp.einsum(
            "hqk,khd->qhd", grad_scores, key_heads, preferred_element_type=jnp.float32
        )
        return ((grad_keys, grad_values), grad_query.reshape(block_rows, head_count * HEAD_DIM))

    empty_sums = jnp.zeros((key_count, head_count, HEAD_DIM), jnp.float32)
    block_ids = jnp.arange(query_count // block_rows, dtype=jnp.int32)
    sums_kv, grad_query = lax.scan(per_block, (empty_sums, empty_sums), (block_ids, log_sums))
    grad_query = (
        grad_query.reshape(query_count, head_count * HEAD_DIM).astype(jnp.bfloat16) * head_scale
    )
    grad_keys = sums_kv[0].reshape(key_count, head_count * HEAD_DIM).astype(jnp.bfloat16)
    grad_values = sums_kv[1].reshape(key_count, head_count * HEAD_DIM).astype(jnp.bfloat16)
    return (grad_query, grad_keys, grad_values)


def forward_one(inputs, encoder, seq_len, weights):
    self_in, self_out, cross_q, cross_kv, cross_out, fc_in, fc_out, norm_gain, norm_bias = weights
    gain_cols = norm_gain.astype(jnp.float32)
    bias_cols = norm_bias.astype(jnp.float32)
    stream = inputs.astype(jnp.float32)
    normed_one, pull_one = jax.vjp(layer_norm, stream, gain_cols[:, 0], bias_cols[:, 0])
    normed_one = normed_one.astype(jnp.bfloat16)
    projected = jnp.dot(normed_one, self_in, preferred_element_type=jnp.float32)
    queries = (projected[:, :D] * head_scale).astype(jnp.bfloat16)
    key_vecs = projected[:, D : 2 * D].astype(jnp.bfloat16)
    value_vecs = projected[:, 2 * D :].astype(jnp.bfloat16)
    mixture, log_sums = attend_forward(queries, key_vecs, value_vecs, seq_len, True)
    after_self = stream + jnp.dot(mixture, self_out, preferred_element_type=jnp.float32)
    normed_two, pull_two = jax.vjp(layer_norm, after_self, gain_cols[:, 1], bias_cols[:, 1])
    normed_two = normed_two.astype(jnp.bfloat16)
    queries_two = (
        jnp.dot(normed_two, cross_q, preferred_element_type=jnp.float32) * head_scale
    ).astype(jnp.bfloat16)
    frame_proj = jnp.dot(encoder, cross_kv, preferred_element_type=jnp.float32)
    frame_keys = frame_proj[:, :D].astype(jnp.bfloat16)
    frame_values = frame_proj[:, D:].astype(jnp.bfloat16)
    mixture_two, log_two = attend_forward(queries_two, frame_keys, frame_values, FRAMES, False)
    after_cross = after_self + jnp.dot(mixture_two, cross_out, preferred_element_type=jnp.float32)
    normed_three, pull_three = jax.vjp(layer_norm, after_cross, gain_cols[:, 2], bias_cols[:, 2])
    normed_three = normed_three.astype(jnp.bfloat16)
    pre_act = jnp.dot(normed_three, fc_in, preferred_element_type=jnp.float32)
    activated, pull_gelu = jax.vjp(exact_gelu, pre_act)
    hidden = activated.astype(jnp.bfloat16)
    after_mlp = after_cross + jnp.dot(hidden, fc_out, preferred_element_type=jnp.float32)
    final_norm, pull_four = jax.vjp(layer_norm, after_mlp, gain_cols[:, 3], bias_cols[:, 3])
    valid_rows = (lax.broadcasted_iota(jnp.int32, (inputs.shape[0], 1), 0) < seq_len).astype(
        jnp.float32
    )
    output = (final_norm * valid_rows).astype(jnp.bfloat16)
    saved_list = (
        valid_rows,
        normed_one,
        queries,
        key_vecs,
        value_vecs,
        mixture,
        log_sums,
        normed_two,
        queries_two,
        frame_keys,
        frame_values,
        mixture_two,
        log_two,
        normed_three,
        hidden,
        pull_one,
        pull_two,
        pull_three,
        pull_gelu,
        pull_four,
    )
    return (output, saved_list)


def backward_one(grad_out, encoder, seq_len, saved_list, weights):
    self_in, self_out, cross_q, cross_kv, cross_out, fc_in, fc_out, norm_gain, norm_bias = weights
    (
        valid_rows,
        normed_one,
        queries,
        key_vecs,
        value_vecs,
        mixture,
        log_sums,
        normed_two,
        queries_two,
        frame_keys,
        frame_values,
        mixture_two,
        log_two,
        normed_three,
        hidden,
        pull_one,
        pull_two,
        pull_three,
        pull_gelu,
        pull_four,
    ) = saved_list
    grad_mlp, gain_four, shift_four = pull_four(grad_out.astype(jnp.float32) * valid_rows)
    branch_three = grad_mlp.astype(jnp.bfloat16)
    grad_fc_out = jnp.einsum("rf,rd->fd", hidden, branch_three, preferred_element_type=jnp.float32)
    grad_hidden = jnp.einsum("rd,fd->rf", branch_three, fc_out, preferred_element_type=jnp.float32)
    grad_pre = pull_gelu(grad_hidden)[0].astype(jnp.bfloat16)
    grad_fc_in = jnp.einsum("rd,rf->df", normed_three, grad_pre, preferred_element_type=jnp.float32)
    grad_normed_three = jnp.einsum("rf,df->rd", grad_pre, fc_in, preferred_element_type=jnp.float32)
    norm_three_in, gain_three, shift_three = pull_three(grad_normed_three)
    grad_cross = grad_mlp + norm_three_in
    branch_two = grad_cross.astype(jnp.bfloat16)
    grad_cross_out = jnp.einsum(
        "rd,re->de", mixture_two, branch_two, preferred_element_type=jnp.float32
    )
    grad_mixture_two = jnp.einsum(
        "re,de->rd", branch_two, cross_out, preferred_element_type=jnp.float32
    ).astype(jnp.bfloat16)
    grad_queries_two, grad_frame_keys, grad_frame_values = attend_backward(
        queries_two, frame_keys, frame_values, grad_mixture_two, log_two, FRAMES, False
    )
    grad_cross_q = jnp.einsum(
        "rd,re->de", normed_two, grad_queries_two, preferred_element_type=jnp.float32
    )
    grad_normed_two = jnp.einsum(
        "re,de->rd", grad_queries_two, cross_q, preferred_element_type=jnp.float32
    )
    grad_frame_kv = jnp.concatenate([grad_frame_keys, grad_frame_values], axis=1)
    grad_cross_kv = jnp.einsum(
        "rd,re->de", encoder, grad_frame_kv, preferred_element_type=jnp.float32
    )
    grad_encoder = jnp.einsum(
        "re,de->rd", grad_frame_kv, cross_kv, preferred_element_type=jnp.float32
    ).astype(jnp.bfloat16)
    norm_two_in, gain_two, shift_two = pull_two(grad_normed_two)
    grad_attn = grad_cross + norm_two_in
    branch_one = grad_attn.astype(jnp.bfloat16)
    grad_self_out = jnp.einsum("rd,re->de", mixture, branch_one, preferred_element_type=jnp.float32)
    grad_mixture = jnp.einsum(
        "re,de->rd", branch_one, self_out, preferred_element_type=jnp.float32
    ).astype(jnp.bfloat16)
    grad_queries, grad_keys, grad_values = attend_backward(
        queries, key_vecs, value_vecs, grad_mixture, log_sums, seq_len, True
    )
    grad_projected = jnp.concatenate([grad_queries, grad_keys, grad_values], axis=1)
    grad_self_in = jnp.einsum(
        "rd,re->de", normed_one, grad_projected, preferred_element_type=jnp.float32
    )
    grad_normed_one = jnp.einsum(
        "re,de->rd", grad_projected, self_in, preferred_element_type=jnp.float32
    )
    norm_one_in, gain_one, shift_one = pull_one(grad_normed_one)
    grad_tokens = (grad_attn + norm_one_in).astype(jnp.bfloat16)
    grad_gain = jnp.stack([gain_one, gain_two, gain_three, gain_four], axis=1)
    grad_shift = jnp.stack([shift_one, shift_two, shift_three, shift_four], axis=1)
    weight_grads = (
        grad_self_in,
        grad_self_out,
        grad_cross_q,
        grad_cross_kv,
        grad_cross_out,
        grad_fc_in,
        grad_fc_out,
        grad_gain,
        grad_shift,
    )
    return (grad_tokens, grad_encoder, weight_grads)


def shards(
    tokens,
    frames,
    lengths,
    cotangent,
    self_in,
    self_out,
    cross_q,
    cross_kv,
    cross_out,
    fc_in,
    fc_out,
    norm_gain,
    norm_bias,
):
    fsdp_count = lax.axis_size("fsdp")
    group_seqs = lengths.shape[0]
    per_device = group_seqs // fsdp_count
    seq_ids = jnp.arange(group_seqs, dtype=jnp.int32)
    rank_order = jnp.argsort(-(lengths * group_seqs + (group_seqs - 1 - seq_ids)))
    rank_ids = np.arange(group_seqs)
    rounds = rank_ids // fsdp_count
    places = rank_ids % fsdp_count
    owners = np.where(rounds % 2 == 0, places, fsdp_count - 1 - places)
    rank_of_slot = np.argsort(owners * per_device + rounds)
    sender = rank_order[jnp.asarray(rank_of_slot, dtype=jnp.int32)]
    slot_of_seq = jnp.argsort(sender)
    arrived_tokens, arrived_frames, arrived_grads = (
        lax.all_to_all(tokens[sender], "fsdp", split_axis=0, concat_axis=1, tiled=True),
        lax.all_to_all(frames[sender], "fsdp", split_axis=0, concat_axis=1, tiled=True),
        lax.all_to_all(cotangent[sender], "fsdp", split_axis=0, concat_axis=1, tiled=True),
    )
    local_ids = lax.dynamic_slice_in_dim(sender, lax.axis_index("fsdp") * per_device, per_device)
    seq_lens = lengths[local_ids]
    weights = (
        lax.all_gather(self_in, ("grp", "fsdp"), axis=0, tiled=True),
        lax.all_gather(self_out, ("grp", "fsdp"), axis=0, tiled=True),
        lax.all_gather(cross_q, ("grp", "fsdp"), axis=0, tiled=True),
        lax.all_gather(cross_kv, ("grp", "fsdp"), axis=0, tiled=True),
        lax.all_gather(cross_out, ("grp", "fsdp"), axis=0, tiled=True),
        lax.all_gather(fc_in, ("grp", "fsdp"), axis=0, tiled=True),
        lax.all_gather(fc_out, ("grp", "fsdp"), axis=0, tiled=True),
        lax.all_gather(norm_gain, ("grp", "fsdp"), axis=0, tiled=True),
        lax.all_gather(norm_bias, ("grp", "fsdp"), axis=0, tiled=True),
    )
    outputs = []
    saved_all = []
    for seq_pos in range(per_device):
        output, saved_list = forward_one(
            arrived_tokens[seq_pos], arrived_frames[seq_pos], seq_lens[seq_pos], weights
        )
        outputs.append(output)
        saved_all.append(saved_list)
    returned = lax.all_to_all(
        jnp.stack(outputs, axis=0), "fsdp", split_axis=1, concat_axis=0, tiled=True
    )
    output_final = returned[slot_of_seq]
    weights_back = (
        lax.all_gather(self_in, ("grp", "fsdp"), axis=0, tiled=True),
        lax.all_gather(self_out, ("grp", "fsdp"), axis=0, tiled=True),
        lax.all_gather(cross_q, ("grp", "fsdp"), axis=0, tiled=True),
        lax.all_gather(cross_kv, ("grp", "fsdp"), axis=0, tiled=True),
        lax.all_gather(cross_out, ("grp", "fsdp"), axis=0, tiled=True),
        lax.all_gather(fc_in, ("grp", "fsdp"), axis=0, tiled=True),
        lax.all_gather(fc_out, ("grp", "fsdp"), axis=0, tiled=True),
        lax.all_gather(norm_gain, ("grp", "fsdp"), axis=0, tiled=True),
        lax.all_gather(norm_bias, ("grp", "fsdp"), axis=0, tiled=True),
    )
    grad_inputs = []
    grad_encoders = []
    grad_list = None
    for seq_pos in range(per_device):
        grad_tokens, grad_encoder, weight_grads = backward_one(
            arrived_grads[seq_pos],
            arrived_frames[seq_pos],
            seq_lens[seq_pos],
            saved_all[seq_pos],
            weights_back,
        )
        grad_inputs.append(grad_tokens)
        grad_encoders.append(grad_encoder)
        if grad_list is None:
            grad_list = list(weight_grads)
        else:
            grad_list = [summed + addend for summed, addend in zip(grad_list, weight_grads)]
    back_tokens, back_frames = (
        lax.all_to_all(
            jnp.stack(grad_inputs, axis=0), "fsdp", split_axis=1, concat_axis=0, tiled=True
        ),
        lax.all_to_all(
            jnp.stack(grad_encoders, axis=0), "fsdp", split_axis=1, concat_axis=0, tiled=True
        ),
    )
    grad_tokens_final = back_tokens[slot_of_seq]
    grad_frames_final = back_frames[slot_of_seq]
    reduced = (
        lax.psum_scatter(grad_list[0], ("grp", "fsdp"), scatter_dimension=0, tiled=True),
        lax.psum_scatter(grad_list[1], ("grp", "fsdp"), scatter_dimension=0, tiled=True),
        lax.psum_scatter(grad_list[2], ("grp", "fsdp"), scatter_dimension=0, tiled=True),
        lax.psum_scatter(grad_list[3], ("grp", "fsdp"), scatter_dimension=0, tiled=True),
        lax.psum_scatter(grad_list[4], ("grp", "fsdp"), scatter_dimension=0, tiled=True),
        lax.psum_scatter(grad_list[5], ("grp", "fsdp"), scatter_dimension=0, tiled=True),
        lax.psum_scatter(grad_list[6], ("grp", "fsdp"), scatter_dimension=0, tiled=True),
        lax.psum_scatter(grad_list[7], ("grp", "fsdp"), scatter_dimension=0, tiled=True),
        lax.psum_scatter(grad_list[8], ("grp", "fsdp"), scatter_dimension=0, tiled=True),
    )
    return (
        output_final,
        grad_tokens_final,
        grad_frames_final,
        reduced[0],
        reduced[1],
        reduced[2],
        reduced[3],
        reduced[4],
        reduced[5],
        reduced[6],
        reduced[7],
        reduced[8],
    )


def solution(mesh):
    return jax.shard_map(
        shards,
        mesh=mesh,
        in_specs=(
            P("grp", "fsdp", None),
            P("grp", "fsdp", None),
            P("grp"),
            P("grp", "fsdp", None),
            P(("grp", "fsdp"), None),
            P(("grp", "fsdp"), None),
            P(("grp", "fsdp"), None),
            P(("grp", "fsdp"), None),
            P(("grp", "fsdp"), None),
            P(("grp", "fsdp"), None),
            P(("grp", "fsdp"), None),
            P(("grp", "fsdp"), None),
            P(("grp", "fsdp"), None),
        ),
        out_specs=(
            P("grp", "fsdp", None),
            P("grp", "fsdp", None),
            P("grp", "fsdp", None),
            P(("grp", "fsdp"), None),
            P(("grp", "fsdp"), None),
            P(("grp", "fsdp"), None),
            P(("grp", "fsdp"), None),
            P(("grp", "fsdp"), None),
            P(("grp", "fsdp"), None),
            P(("grp", "fsdp"), None),
            P(("grp", "fsdp"), None),
            P(("grp", "fsdp"), None),
        ),
        check_vma=False,
    )
```

profile of v0, /device:TPU:0, one launch (start us, length us, event | category | flops | bytes accessed | tf_op | source)
XLA Modules:
  0.0 1650.8 jit_solution(6231108916929582636)
XLA Ops:
  16.2 7.4 all-to-all-start
  25.4 42.0 %all-to-all-done = bf16[16,64,768]{2,1,0:T(8,128)(2,1)S(1)} async-done(((bf16[16,64,768]{2,1,0:T(8,128)(2,1)}), bf16[16,64,768]{2,1,0:T(8,128)(2,1)S(1)}, u32[]{:S(2)}, u32[]{:S(2)}) %all-to-all-start) | async-done | bytes 1572896 | tf_op jit(solution)/shard_map/all_to_all | solution.py:305
  73.2 99.6 %all-gather = bf16[32,24,4]{1,2,0:T(4,128)(2,1)S(1)} all-gather(bf16[1,24,4]{1,2,0:T(4,128)(2,1)S(1)} %bitcast.378), channel_id=1, replica_groups=mesh['grp'=4,'fsdp'=8] {'grp','fsdp'}, dimensions={0}, use_global_device_ids=true | all-gather | bytes 6336 | tf_op jit(solution)/shard_map/all_gather | solution.py:319
  172.9 63.4 %all-gather.1 = bf16[32,24,4]{1,2,0:T(4,128)(2,1)S(1)} all-gather(bf16[1,24,4]{1,2,0:T(4,128)(2,1)S(1)} %bitcast.379), channel_id=1, replica_groups=mesh['grp'=4,'fsdp'=8] {'grp','fsdp'}, dimensions={0}, use_global_device_ids=true | all-gather | bytes 6336 | tf_op jit(solution)/shard_map/all_gather | solution.py:320
  261.3 6.8 fusion.165
  290.1 7.7 fusion.85
  323.3 44.5 %all-to-all-done.1 = bf16[16,192,768]{2,1,0:T(8,128)(2,1)} async-done(((bf16[16,192,768]{2,1,0:T(8,128)(2,1)}), bf16[16,192,768]{2,1,0:T(8,128)(2,1)}, u32[]{:S(2)}, u32[]{:S(2)}) %all-to-all-start.1) | async-done | bytes 4718624 | tf_op jit(solution)/shard_map/all_to_all | solution.py:306
  372.7 6.2 convolution_convert_fusion
  387.5 15.0 select_reduce_fusion.1
  402.5 26.3 %fusion = (f32[12,512]{1,0:T(8,128)S(1)}, f32[12,512]{1,0:T(8,128)S(1)}, f32[12,512,1536]{2,1,0:T(8,128)}) fusion(f32[12,512,1536]{2,1,0:T(8,128)} %get-tuple-element.314, f32[12,512]{1,0:T(8,128)S(1)} %get-tuple-element.313, pred[1536]{0:T(1024)(128)(4,1)S(1)} %iota_compare_fusion.1, bf16[512,12,64]{0,2,1:T(8,128)(2,1)S(1)} %bitcast.321, ...), kind=kOutput, calls=%fused_computation.18 | convolution fusion | flops 1255133184 | bytes 78718464 | tf_op jit(solution)/shard_map/while/body/eval_jaxpr/qhd,khd->hqk/dot_general | solution.py:50
  428.8 16.9 %fusion.1 = f32[12,512]{1,0:T(8,128)S(1)} fusion(f32[12,512,1536]{2,1,0:T(8,128)} %get-tuple-element.321, f32[12,512]{1,0:T(8,128)S(1)} %get-tuple-element.243, pred[1536]{0:T(1024)(128)(4,1)S(1)} %iota_compare_fusion.1), kind=kLoop, calls=%fused_computation.19 | loop fusion | flops 28305408 | bytes 37799424 | tf_op jit(solution)/shard_map/while/body/eval_jaxpr/reduce_sum | solution.py:58
  445.7 15.9 fusion.87
  461.6 15.9 fusion.88
  483.2 19.7 %multiply_convert_fusion.4 = (bf16[512,3072]{1,0:T(8,128)(2,1)}, f32[512,3072]{1,0:T(8,128)}, f32[512,3072]{1,0:T(8,128)}) fusion(bf16[768,3072]{1,0:T(8,128)(2,1)} %all-gather.20.cloned.1.call-done, f32[512,768]{1,0:T(8,128)S(1)} %get-tuple-element.328, f32[512]{0:T(512)S(1)} %fusion.120, f32[512]{0:T(512)S(1)} %broadcast_multiply_fusion.3, ...), kind=kOutput, calls=%fused_computation.62 | convolution fusion | flops 2520121344 | bytes 22030336 | tf_op jit(solution)/shard_map/dot_general | solution.py:152
  502.8 14.9 all-gather.22.cloned.1.call-done
  517.7 6.1 fusion.172
  524.2 18.4 %multiply_convert_fusion.5 = (bf16[512,3072]{1,0:T(8,128)(2,1)S(1)}, f32[512,3072]{1,0:T(8,128)}, f32[512,3072]{1,0:T(8,128)}) fusion(bf16[768,3072]{1,0:T(8,128)(2,1)S(1)} %copy-done.175, f32[512,768]{1,0:T(8,128)S(1)} %get-tuple-element.323, f32[768]{0:T(1024)S(1)} %copy-done.113, f32[768]{0:T(1024)S(1)} %copy-done.111, f32[512]{0:T(512)S(1)} %fusion.117, ...), kind=kOutput, calls=%fused_computation.75 | convolution fusion | flops 2520121344 | bytes 22030336 | tf_op jit(solution)/shard_map/dot_general | solution.py:152
  551.9 9.3 add_convert_fusion
  563.9 9.5 add_convert_fusion.1
  573.4 5.8 multiply_reduce_fusion.10
  591.9 16.4 fusion.174
  608.4 51.1 %multiply_reduce_fusion.1 = (f32[12,512]{1,0:T(8,128)S(1)}, f32[12,512]{1,0:T(8,128)S(1)}, f32[12,512,1536]{2,1,0:T(8,128)}) fusion(f32[12,512,1536]{2,1,0:T(8,128)} %get-tuple-element.314, f32[12,512]{1,0:T(8,128)S(1)} %copy-done.95, pred[1536]{0:T(1024)(128)(4,1)S(1)} %copy-done.108, f32[12,512,1536]{2,1,0:T(8,128)} %fusion.174, ...), kind=kOutput, calls=%fused_computation.12 | convolution fusion | flops 1283444736 | bytes 154240512 | tf_op jit(solution)/shard_map/while/body/eval_jaxpr/qhd,khd->hqk/dot_general | solution.py:103
  659.5 60.3 %multiply_convert_fusion.1 = (bf16[12,512,1536]{2,1,0:T(8,128)(2,1)}, bf16[12,512,1536]{2,1,0:T(8,128)(2,1)}) fusion(f32[12,512,1536]{2,1,0:T(8,128)} %get-tuple-element.333, f32[12,512,1536]{2,1,0:T(8,128)} %get-tuple-element.314, f32[12,512]{1,0:T(8,128)S(1)} %get-tuple-element.240, f32[12,512]{1,0:T(8,128)S(1)} %copy-done.95, ...), kind=kLoop, calls=%fused_computation.11 | loop fusion | flops 94371840 | bytes 188843520 | tf_op jit(solution)/shard_map/while/body/eval_jaxpr/convert_element_type | solution.py:107
  719.8 10.0 fusion.91
  729.8 11.2 convolution_convert_fusion.5
  743.3 10.4 fusion.92
  769.9 16.6 %fusion.47 = bf16[12,64,1536]{2,1,0:T(8,128)(2,1)} fusion(bf16[512,12,64]{0,2,1:T(8,128)(2,1)S(1)} %bitcast.310, f32[12,512,1536]{2,1,0:T(8,128)} %get-tuple-element.321, f32[12,512]{1,0:T(8,128)S(1)} %copy-done.96, pred[1536]{0:T(1024)(128)(4,1)S(1)} %copy-done.108), kind=kOutput, calls=%fused_computation.108 | convolution fusion | flops 1237450752 | bytes 40920576 | tf_op jit(solution)/shard_map/while/body/eval_jaxpr/hqk,qhd->khd/dot_general | solution.py:97
  799.9 16.6 %fusion.44 = bf16[12,64,1536]{2,1,0:T(8,128)(2,1)} fusion(bf16[512,12,64]{0,2,1:T(8,128)(2,1)S(1)} %bitcast.318, f32[12,512,1536]{2,1,0:T(8,128)} %get-tuple-element.314, f32[12,512]{1,0:T(8,128)S(1)} %copy-done.95, pred[1536]{0:T(1024)(128)(4,1)S(1)} %copy-done.108), kind=kOutput, calls=%fused_computation.107 | convolution fusion | flops 1237450752 | bytes 40920576 | tf_op jit(solution)/shard_map/while/body/eval_jaxpr/hqk,qhd->khd/dot_general | solution.py:97
  816.6 9.3 fusion.50
  825.9 11.0 multiply_reduce_fusion.3
  837.0 14.2 multiply_convert_fusion.3
  851.2 5.9 convolution_convert_fusion.13
  861.6 10.0 convolution_add_fusion.3
  876.8 7.8 fusion.79
  889.7 6.9 multiply_reduce_fusion.2
  896.6 7.1 multiply_convert_fusion.2
  922.4 6.3 convolution_add_fusion.2
  942.3 5.6 convolution_add_fusion.1
  962.8 12.9 all-to-all-done.2
  979.7 7.2 fusion.52
  991.5 33.7 %copy.179 = bf16[2,1536,768]{2,0,1:T(2,128)(2,1)} copy(bf16[2,1536,768]{2,1,0:T(8,128)(2,1)S(1)} %pad_maximum_fusion.2) | data formatting | bytes 9437184 | tf_op jit(solution)/shard_map/stack | solution.py:367
  1025.3 6.1 all-to-all-start.5
  1034.8 125.7 %all-reduce.2 = (f32[768,4]{0,1:T(4,128)S(1)}, f32[768,4]{0,1:T(4,128)S(1)}) all-reduce(f32[768,4]{0,1:T(4,128)S(1)} %maximum_add_fusion, f32[768,4]{0,1:T(4,128)S(1)} %maximum_add_fusion.1), channel_id=9, replica_groups=mesh['grp'=4,'fsdp'=8] {'grp','fsdp'}, use_global_device_ids=true, to_apply=%region_61.62.clone | all-reduce | flops 6144 | bytes 49152
  1176.0 5.5 gather_fusion.7
  1181.6 55.0 %reduce-scatter.16.cloned.1.call-done = f32[24,1536]{1,0:T(8,128)} async-done(((f32[768,1536]{1,0:T(8,128)}), f32[24,1536]{1,0:T(8,128)}) %reduce-scatter.16.cloned.1.call-update) | async-done | bytes 147472 | tf_op jit(solution)/shard_map/reduce_scatter | solution.py:376
  1236.5 124.3 %reduce-scatter.10.cloned.1.call-done = f32[24,2304]{1,0:T(8,128)} async-done(((f32[768,2304]{1,0:T(8,128)}), f32[24,2304]{1,0:T(8,128)}) %reduce-scatter.10.cloned.1.call-update) | async-done | bytes 221200 | tf_op jit(solution)/shard_map/reduce_scatter | solution.py:373
  1360.9 142.4 %reduce-scatter.20.cloned.1.call-done = f32[24,3072]{1,0:T(8,128)} async-done(((f32[768,3072]{1,0:T(8,128)}), f32[24,3072]{1,0:T(8,128)}) %reduce-scatter.20.cloned.1.call-update) | async-done | bytes 294928 | tf_op jit(solution)/shard_map/reduce_scatter | solution.py:378
  1503.2 140.7 %reduce-scatter.22.cloned.1.call-done = f32[96,768]{1,0:T(8,128)} async-done(((f32[3072,768]{1,0:T(8,128)}), f32[96,768]{1,0:T(8,128)}) %reduce-scatter.22.cloned.1.call-update) | async-done | bytes 294928 | tf_op jit(solution)/shard_map/reduce_scatter | solution.py:379
  (630 shorter events, 252.3 us)
Async XLA Ops:
  7.2 254.1 %all-gather.10.cloned.1.call-start = ((), (), s32[]{:S(2)}) async-start(), calls=%async_computation.13 | async-start | bytes 3649536 | tf_op jit(solution)/shard_map/all_gather | solution.py:312
  7.9 289.8 %all-gather.12.cloned.1.call-start = ((), (), s32[]{:S(2)}) async-start(), calls=%async_computation.14 | async-start | bytes 1216512 | tf_op jit(solution)/shard_map/all_gather | solution.py:313
  8.7 292.1 %all-gather.16.cloned.1.call-start = ((), (), s32[]{:S(2)}) async-start(), calls=%async_computation.16 | async-start | bytes 1216512 | tf_op jit(solution)/shard_map/all_gather | solution.py:314
  9.4 363.3 %all-gather.14.cloned.1.call-start = ((), (), s32[]{:S(2)}) async-start(), calls=%async_computation.15 | async-start | bytes 2433024 | tf_op jit(solution)/shard_map/all_gather | solution.py:315
  10.0 467.5 %all-gather.18.cloned.1.call-start = ((), (), s32[]{:S(2)}) async-start(), calls=%async_computation.17 | async-start | bytes 1216512 | tf_op jit(solution)/shard_map/all_gather | solution.py:316
  10.6 472.6 %all-gather.20.cloned.1.call-start = ((), (), s32[]{:S(2)}) async-start(), calls=%async_computation.18 | async-start | bytes 4866048 | tf_op jit(solution)/shard_map/all_gather | solution.py:317
  14.4 58.0 %copy-start.173 = (s32[16]{0:T(128)}, s32[16]{0:T(128)S(1)}, u32[]{:S(2)}) copy-start(s32[16]{0:T(128)S(1)} %gather_fusion) | copy-start | bytes 196
  16.2 51.2 %all-to-all-start = ((bf16[16,64,768]{2,1,0:T(8,128)(2,1)}), bf16[16,64,768]{2,1,0:T(8,128)(2,1)S(1)}, u32[]{:S(2)}, u32[]{:S(2)}) async-start(bf16[16,64,768]{2,1,0:T(8,128)(2,1)} %gather_fusion.1), calls=%async_computation | async-start | bytes 3145728 | tf_op jit(solution)/shard_map/all_to_all | solution.py:305
  25.4 47.1 %copy-start.2 = (s32[16]{0:T(128)S(1)}, s32[16]{0:T(128)}, u32[]{:S(2)}) copy-start(s32[16]{0:T(128)} %param.16) | copy-start | bytes 196
  25.4 47.8 %copy-start.171 = (bf16[24,4]{0,1:T(4,128)(2,1)S(1)}, bf16[24,4]{0,1:T(4,128)(2,1)}, u32[]{:S(2)}) copy-start(bf16[24,4]{0,1:T(4,128)(2,1)} %param.25) | copy-start | bytes 580
  25.4 147.5 %copy-start.172 = (bf16[24,4]{0,1:T(4,128)(2,1)S(1)}, bf16[24,4]{0,1:T(4,128)(2,1)}, u32[]{:S(2)}) copy-start(bf16[24,4]{0,1:T(4,128)(2,1)} %param.26) | copy-start | bytes 580
  67.4 174.8 %copy-start.66 = (bf16[16,64,768]{2,1,0:T(8,128)(2,1)}, bf16[16,64,768]{2,1,0:T(8,128)(2,1)S(1)}, u32[]{:S(2)}) copy-start(bf16[16,64,768]{2,1,0:T(8,128)(2,1)S(1)} %all-to-all-done) | copy-start | bytes 4718596
  67.4 184.0 %all-to-all-start.3 = ((bf16[16,64,768]{2,1,0:T(8,128)(2,1)}), bf16[16,64,768]{2,1,0:T(8,128)(2,1)}, u32[]{:S(2)}, u32[]{:S(2)}) async-start(bf16[16,64,768]{2,1,0:T(8,128)(2,1)} %gather_fusion.5), calls=%async_computation.3 | async-start | bytes 3145728 | tf_op jit(solution)/shard_map/all_to_all | solution.py:307
  71.7 446.1 %all-gather.22.cloned.1.call-start = ((), (), s32[]{:S(2)}) async-start(), calls=%async_computation.19 | async-start | bytes 4866048 | tf_op jit(solution)/shard_map/all_gather | solution.py:318
  244.1 217.5 %copy-start.107 = (pred[1536]{0:T(1024)(128)(4,1)}, pred[1536]{0:T(1024)(128)(4,1)S(1)}, u32[]{:S(2)}) copy-start(pred[1536]{0:T(1024)(128)(4,1)S(1)} %iota_compare_fusion.1) | copy-start | bytes 4612
  246.5 71.9 %copy-start.153 = (f32[768]{0:T(1024)}, f32[768]{0:T(1024)S(1)}, u32[]{:S(2)}) copy-start(f32[768]{0:T(1024)S(1)} %get-tuple-element.238) | copy-start | bytes 9220
  247.1 71.3 %copy-start.120 = (f32[768]{0:T(1024)}, f32[768]{0:T(1024)S(1)}, u32[]{:S(2)}) copy-start(f32[768]{0:T(1024)S(1)} %get-tuple-element.224) | copy-start | bytes 9220
  247.3 42.8 %copy-start.58 = (pred[512,512]{0,1:T(8,128)(4,1)}, pred[512,512]{0,1:T(8,128)(4,1)S(1)}, u32[]{:S(2)}) copy-start(pred[512,512]{0,1:T(8,128)(4,1)S(1)} %fusion.93) | copy-start | bytes 786436
  247.4 63.6 %copy-start.60 = (pred[512,512]{0,1:T(8,128)(4,1)}, pred[512,512]{0,1:T(8,128)(4,1)S(1)}, u32[]{:S(2)}) copy-start(pred[512,512]{0,1:T(8,128)(4,1)S(1)} %fusion.94) | copy-start | bytes 786436
  251.4 116.4 %all-to-all-start.1 = ((bf16[16,192,768]{2,1,0:T(8,128)(2,1)}), bf16[16,192,768]{2,1,0:T(8,128)(2,1)}, u32[]{:S(2)}, u32[]{:S(2)}) async-start(bf16[16,192,768]{2,1,0:T(8,128)(2,1)} %gather_fusion.3), calls=%async_computation.1 | async-start | bytes 9437184 | tf_op jit(solution)/shard_map/all_to_all | solution.py:306
  256.0 925.5 %reduce-scatter.18.cloned.1.call-start = ((), (), s32[]{:S(2)}) async-start(), calls=%async_computation.24 | async-start | bytes 2433024 | tf_op jit(solution)/shard_map/reduce_scatter | solution.py:377
  305.5 97.0 %copy-start.45 = (bf16[512,768]{0,1:T(8,128)(2,1)}, bf16[512,768]{0,1:T(8,128)(2,1)S(1)}, u32[]{:S(2)}) copy-start(bf16[512,768]{0,1:T(8,128)(2,1)S(1)} %copy.161) | copy-start | bytes 2359300
  322.0 65.6 %copy-start.43 = (bf16[512,768]{0,1:T(8,128)(2,1)}, bf16[512,768]{0,1:T(8,128)(2,1)S(1)}, u32[]{:S(2)}) copy-start(bf16[512,768]{0,1:T(8,128)(2,1)S(1)} %copy.156) | copy-start | bytes 2359300
  379.3 66.5 %copy-start.17 = (bf16[1536,768]{0,1:T(8,128)(2,1)}, bf16[1536,768]{0,1:T(8,128)(2,1)S(1)}, u32[]{:S(2)}) copy-start(bf16[1536,768]{0,1:T(8,128)(2,1)S(1)} %get-tuple-element.277) | copy-start | bytes 7077892
  387.5 74.1 %copy-start.49 = (bf16[1536,768]{0,1:T(8,128)(2,1)}, bf16[1536,768]{0,1:T(8,128)(2,1)S(1)}, u32[]{:S(2)}) copy-start(bf16[1536,768]{0,1:T(8,128)(2,1)S(1)} %get-tuple-element.272) | copy-start | bytes 7077892
  480.1 62.5 %copy-start.28 = (f32[512,768]{1,0:T(8,128)}, f32[512,768]{1,0:T(8,128)S(1)}, u32[]{:S(2)}) copy-start(f32[512,768]{1,0:T(8,128)S(1)} %get-tuple-element.323) | copy-start | bytes 4718596
  480.1 99.1 %copy-start.134 = (f32[512]{0:T(512)}, f32[512]{0:T(512)S(1)}, u32[]{:S(2)}) copy-start(f32[512]{0:T(512)S(1)} %broadcast_multiply_fusion.6) | copy-start | bytes 6148
  481.4 97.8 %copy-start.10 = (f32[512,768]{1,0:T(8,128)}, f32[512,768]{1,0:T(8,128)S(1)}, u32[]{:S(2)}) copy-start(f32[512,768]{1,0:T(8,128)S(1)} %get-tuple-element.328) | copy-start | bytes 4718596
  481.4 97.8 %copy-start.117 = (f32[512]{0:T(512)}, f32[512]{0:T(512)S(1)}, u32[]{:S(2)}) copy-start(f32[512]{0:T(512)S(1)} %broadcast_multiply_fusion.3) | copy-start | bytes 6148
  481.7 97.5 %copy-start.157 = (f32[512]{0:T(512)}, f32[512]{0:T(512)S(1)}, u32[]{:S(2)}) copy-start(f32[512]{0:T(512)S(1)} %fusion.117) | copy-start | bytes 6148
  481.7 97.5 %copy-start.130 = (f32[512]{0:T(512)}, f32[512]{0:T(512)S(1)}, u32[]{:S(2)}) copy-start(f32[512]{0:T(512)S(1)} %fusion.120) | copy-start | bytes 6148
  551.8 37.2 %copy-start.18 = (f32[512,768]{1,0:T(8,128)}, f32[512,768]{1,0:T(8,128)S(1)}, u32[]{:S(2)}) copy-start(f32[512,768]{1,0:T(8,128)S(1)} %get-tuple-element.267) | copy-start | bytes 4718596
  551.8 37.1 %copy-start.136 = (f32[512]{0:T(512)}, f32[512]{0:T(512)S(1)}, u32[]{:S(2)}) copy-start(f32[512]{0:T(512)S(1)} %negate_multiply_fusion.5) | copy-start | bytes 6148
  590.7 150.3 %copy-start.22 = (f32[512,768]{1,0:T(8,128)}, f32[512,768]{1,0:T(8,128)S(1)}, u32[]{:S(2)}) copy-start(f32[512,768]{1,0:T(8,128)S(1)} %add_add_fusion.9) | copy-start | bytes 4718596
  659.5 60.3 %copy-start.8 = (bf16[1536,768]{0,1:T(8,128)(2,1)S(1)}, bf16[1536,768]{0,1:T(8,128)(2,1)}, u32[]{:S(2)}) copy-start(bf16[1536,768]{0,1:T(8,128)(2,1)} %copy-done.7) | copy-start | bytes 7077892
  743.2 438.3 %reduce-scatter.14.cloned.1.call-start = ((), (), s32[]{:S(2)}) async-start(), calls=%async_computation.22 | async-start | bytes 2433024 | tf_op jit(solution)/shard_map/reduce_scatter | solution.py:375
  786.5 395.0 %reduce-scatter.12.cloned.1.call-start = ((), (), s32[]{:S(2)}) async-start(), calls=%async_computation.21 | async-start | bytes 2433024 | tf_op jit(solution)/shard_map/reduce_scatter | solution.py:374
  816.5 420.0 %reduce-scatter.16.cloned.1.call-start = ((), (), s32[]{:S(2)}) async-start(), calls=%async_computation.23 | async-start | bytes 4866048 | tf_op jit(solution)/shard_map/reduce_scatter | solution.py:376
  825.9 31.1 %slice-start = ((s8[18874368]{0:T(1024)(128)(4,1)}), s8[4194304]{0:T(1024)(128)(4,1)S(1)}, s32[]{:S(2)}) async-start(s8[18874368]{0:T(1024)(128)(4,1)} %bitcast.289), calls=%async_computation.27 | async-start | bytes 8388608
  825.9 31.1 %slice-start.1 = ((s8[18874368]{0:T(1024)(128)(4,1)}), s8[4194304]{0:T(1024)(128)(4,1)S(1)}, s32[]{:S(2)}) async-start(s8[18874368]{0:T(1024)(128)(4,1)} %bitcast.289), calls=%async_computation.28 | async-start | bytes 8388608
  825.9 31.1 %slice-start.2 = ((s8[18874368]{0:T(1024)(128)(4,1)}), s8[4194304]{0:T(1024)(128)(4,1)S(1)}, s32[]{:S(2)}) async-start(s8[18874368]{0:T(1024)(128)(4,1)} %bitcast.289), calls=%async_computation.29 | async-start | bytes 8388608
  871.7 489.2 %reduce-scatter.10.cloned.1.call-start = ((), (), s32[]{:S(2)}) async-start(), calls=%async_computation.20 | async-start | bytes 7299072 | tf_op jit(solution)/shard_map/reduce_scatter | solution.py:373
  916.0 587.2 %reduce-scatter.20.cloned.1.call-start = ((), (), s32[]{:S(2)}) async-start(), calls=%async_computation.25 | async-start | bytes 9732096 | tf_op jit(solution)/shard_map/reduce_scatter | solution.py:378
  932.9 42.7 %all-to-all-start.2 = ((bf16[2,512,768]{2,0,1:T(2,128)(2,1)}), bf16[2,512,768]{2,0,1:T(2,128)(2,1)}, u32[]{:S(2)}, u32[]{:S(2)}) async-start(bf16[2,512,768]{2,0,1:T(2,128)(2,1)} %copy.162), calls=%async_computation.2 | async-start | bytes 3145728 | tf_op jit(solution)/shard_map/all_to_all | solution.py:330
  937.4 706.6 %reduce-scatter.22.cloned.1.call-start = ((), (), s32[]{:S(2)}) async-start(), calls=%async_computation.26 | async-start | bytes 9732096 | tf_op jit(solution)/shard_map/reduce_scatter | solution.py:379
  975.7 49.6 %all-to-all-start.4 = ((bf16[2,512,768]{2,0,1:T(2,128)(2,1)}), bf16[2,512,768]{2,0,1:T(2,128)(2,1)S(1)}, u32[]{:S(2)}, u32[]{:S(2)}) async-start(bf16[2,512,768]{2,0,1:T(2,128)(2,1)} %copy.176), calls=%async_computation.4 | async-start | bytes 3145728 | tf_op jit(solution)/shard_map/all_to_all | solution.py:363
  1025.3 145.2 %all-to-all-start.5 = ((bf16[2,1536,768]{2,0,1:T(2,128)(2,1)}), bf16[2,1536,768]{2,0,1:T(2,128)(2,1)}, u32[]{:S(2)}, u32[]{:S(2)}) async-start(bf16[2,1536,768]{2,0,1:T(2,128)(2,1)} %copy.179), calls=%async_computation.5 | async-start | bytes 9437184 | tf_op jit(solution)/shard_map/all_to_all | solution.py:366
  1176.0 467.9 %copy-start.1 = (bf16[16,64,768]{2,1,0:T(8,128)(2,1)S(1)}, bf16[16,64,768]{2,1,0:T(8,128)(2,1)}, u32[]{:S(2)}) copy-start(bf16[16,64,768]{2,1,0:T(8,128)(2,1)} %param.14) | copy-start | bytes 4718596
  (169 other events, 1053.4 us)
Sparse Core Ops, SparseCore 0:
  11.0 87.5 all-gather.9
  101.6 60.4 all-gather.11
  165.1 53.0 all-gather.15
  221.1 74.0 all-gather.13
  298.0 88.6 all-gather.17
  389.6 62.6 all-gather.19
  455.2 62.4 all-gather.21
  743.4 97.8 reduce-scatter.17
  847.9 98.1 reduce-scatter.13
  951.9 172.3 reduce-scatter.11
  1131.3 105.2 reduce-scatter.15
  1242.6 118.1 reduce-scatter.9
  1368.3 134.8 reduce-scatter.19
  1509.6 134.3 reduce-scatter.21
where the time goes:
time: 1660 us; the launch traced here: 1650 us
  waiting for transfers between devices  581 us (35%)
  matrix products  469 us (28%)
  blocking collectives  289 us (17%)
  other arithmetic  142 us (9%)
  local copies, waits for them, and re-layouts  121 us (7%)
  starting transfers between devices  31.9 us (2%)
  between operations  16.9 us (1%)
    reduce_scatter x1, waiting for transfers between devices, shards(): lax.psum_scatter(grad_list[5], ('grp', 'fsdp'), scatter_dimension=0, tile...  142 us
    reduce_scatter x1, waiting for transfers between devices, shards(): lax.psum_scatter(grad_list[6], ('grp', 'fsdp'), scatter_dimension=0, tile...  141 us
    unnamed x1, blocking collectives  126 us
    reduce_scatter x1, waiting for transfers between devices, shards(): lax.psum_scatter(grad_list[0], ('grp', 'fsdp'), scatter_dimension=0, tile...  124 us
    all_gather x1, blocking collectives, shards(): lax.all_gather(norm_gain, ('grp', 'fsdp'), axis=0, tiled=True)  99.6 us
    dot_general x4, matrix products, per_block(): jnp.einsum('qhd,khd->hqk', grad_heads, value_heads, preferred_element_typ...  85.5 us
    convert_element_type x3, other arithmetic, per_block(): grad_scores = (softmaxed * (grad_probs - inner_sum)).astype(jnp.bfloat16)  81.6 us
    all_gather x1, blocking collectives, shards(): lax.all_gather(norm_bias, ('grp', 'fsdp'), axis=0, tiled=True)  63.4 us
  transfers between devices with their start and end apart: 20, of which 8 were waited for; matrix products, arithmetic and copies ran while one was open for 30% of the time, Pallas kernels for 0%

commit v1 on v0

v1 whole, which is shorter than its diff:
```python
import functools

import jax
import jax.numpy as jnp
import numpy as np
from jax import lax
from jax.experimental import pallas as pl
from jax.experimental.pallas import tpu as pltpu
from jax.sharding import PartitionSpec as P

D = 768
HEAD_DIM = 64
FRAMES = 1500
PAIR = 2 * HEAD_DIM
PAIRS = D // PAIR
TILE = 128
KEY_CHUNK = 256

eps_norm = 1e-05
neg_big = -1e30
head_scale = 0.125
bf16 = jnp.bfloat16
f32 = jnp.float32
VMEM_LIMIT = 56 * 1024 * 1024


def layer_norm(inputs, gain_vec, shift_vec):
    average = jnp.mean(inputs, axis=-1, keepdims=True)
    centered = inputs - average
    variance = jnp.mean(centered * centered, axis=-1, keepdims=True)
    return centered * lax.rsqrt(variance + eps_norm) * gain_vec + shift_vec


def exact_gelu(inputs):
    return jax.nn.gelu(inputs, approximate=False)


def nt(left, right):
    return lax.dot_general(left, right, (((1,), (1,)), ((), ())), preferred_element_type=f32)


def nn(left, right):
    return lax.dot_general(left, right, (((1,), (0,)), ((), ())), preferred_element_type=f32)


def split_heads(block):
    lanes = lax.broadcasted_iota(jnp.int32, block.shape, 1)
    zero = jnp.zeros_like(block)
    return jnp.concatenate(
        [jnp.where(lanes < HEAD_DIM, block, zero), jnp.where(lanes < HEAD_DIM, zero, block)], axis=0
    )


def join_heads(stacked):
    return jnp.concatenate([stacked[:HEAD_DIM, :TILE], stacked[HEAD_DIM:, TILE:]], axis=0).T


def row_dots(left, right):
    prod = (left.astype(f32) * right.astype(f32)).T
    return jnp.concatenate(
        [
            jnp.sum(prod[:HEAD_DIM], axis=0, keepdims=True),
            jnp.sum(prod[HEAD_DIM:], axis=0, keepdims=True),
        ],
        axis=1,
    )


def cross_forward_kernel(len_ref, q_ref, kv_ref, out_ref, lse_ref, vt_ref, s_ref):
    slots = kv_ref.shape[0]
    vt_ref[...] = kv_ref[:, PAIR:].T
    out_ref[...] = jnp.zeros_like(out_ref)
    lse_ref[...] = jnp.zeros_like(lse_ref)
    spans = [(k, min(KEY_CHUNK, slots - k)) for k in range(0, slots, KEY_CHUNK)]

    def per_tile(tile, carry):
        rows = pl.ds(pl.multiple_of(tile * TILE, TILE), TILE)
        queries = split_heads(q_ref[rows, :] * jnp.asarray(head_scale, bf16))
        peak = jnp.full((1, 2 * TILE), neg_big, f32)
        for start, size in spans:
            scores = nt(kv_ref[start : start + size, :PAIR], queries)
            if start + size > FRAMES:
                keys = start + lax.broadcasted_iota(jnp.int32, scores.shape, 0)
                scores = jnp.where(keys < FRAMES, scores, neg_big)
            s_ref[start : start + size, :] = scores
            peak = jnp.maximum(peak, jnp.max(scores, axis=0, keepdims=True))
        total = jnp.zeros((1, 2 * TILE), f32)
        mixed = jnp.zeros((PAIR, 2 * TILE), f32)
        for start, size in spans:
            probs = jnp.exp(s_ref[start : start + size, :] - peak)
            total = total + jnp.sum(probs, axis=0, keepdims=True)
            mixed = mixed + nn(vt_ref[:, start : start + size], probs.astype(bf16))
        out_ref[rows, :] = join_heads(mixed / total).astype(bf16)
        lse_ref[0, pl.ds(tile, 1), :] = peak + jnp.log(total)
        return carry

    lax.fori_loop(0, pl.cdiv(len_ref[0], TILE), per_tile, 0)


def cross_forward(queries, kv, seq_len):
    rows, slots = queries.shape[0], kv.shape[0]
    tiles = rows // TILE
    return pl.pallas_call(
        cross_forward_kernel,
        name="cross_forward",
        out_shape=(
            jax.ShapeDtypeStruct((rows, D), bf16),
            jax.ShapeDtypeStruct((PAIRS, tiles, 2 * TILE), f32),
        ),
        grid_spec=pltpu.PrefetchScalarGridSpec(
            num_scalar_prefetch=1,
            grid=(PAIRS,),
            in_specs=[
                pl.BlockSpec((rows, PAIR), lambda h, n: (0, h)),
                pl.BlockSpec((slots, 2 * PAIR), lambda h, n: (0, h)),
            ],
            out_specs=[
                pl.BlockSpec((rows, PAIR), lambda h, n: (0, h)),
                pl.BlockSpec((1, tiles, 2 * TILE), lambda h, n: (h, 0, 0)),
            ],
            scratch_shapes=[
                pltpu.VMEM((PAIR, slots), bf16),
                pltpu.VMEM((slots, 2 * TILE), f32),
            ],
        ),
        compiler_params=pltpu.CompilerParams(vmem_limit_bytes=VMEM_LIMIT),
        cost_estimate=pl.CostEstimate(
            flops=8 * rows * slots * D, bytes_accessed=2 * (2 * rows + 2 * slots) * D, transcendentals=rows * slots * 12
        ),
    )(seq_len, queries, kv)


def cross_backward_kernel(len_ref, q_ref, kv_ref, mix_ref, grad_ref, lse_ref, dq_ref, dkv_ref, kt_ref, dk_ref, dv_ref):
    slots = kv_ref.shape[0]
    kt_ref[...] = kv_ref[:, :PAIR].T
    dq_ref[...] = jnp.zeros_like(dq_ref)
    dk_ref[...] = jnp.zeros_like(dk_ref)
    dv_ref[...] = jnp.zeros_like(dv_ref)
    spans = [(k, min(KEY_CHUNK, slots - k)) for k in range(0, slots, KEY_CHUNK)]

    def per_tile(tile, carry):
        rows = pl.ds(pl.multiple_of(tile * TILE, TILE), TILE)
        queries = split_heads(q_ref[rows, :] * jnp.asarray(head_scale, bf16))
        grads = split_heads(grad_ref[rows, :])
        inner = row_dots(mix_ref[rows, :], grad_ref[rows, :])
        lse = lse_ref[0, pl.ds(tile, 1), :]
        dq = jnp.zeros((PAIR, 2 * TILE), f32)
        for start, size in spans:
            span = slice(start, start + size)
            probs = jnp.exp(nt(kv_ref[span, :PAIR], queries) - lse)
            if start + size > FRAMES:
                keys = start + lax.broadcasted_iota(jnp.int32, probs.shape, 0)
                probs = jnp.where(keys < FRAMES, probs, 0.0)
            dscores = (probs * (nt(kv_ref[span, PAIR:], grads) - inner)).astype(bf16)
            dv_ref[span, :] += nn(probs.astype(bf16), grads)
            dk_ref[span, :] += nn(dscores, queries)
            dq = dq + nn(kt_ref[:, span], dscores)
        dq_ref[rows, :] = join_heads(dq).astype(bf16) * jnp.asarray(head_scale, bf16)
        return carry

    lax.fori_loop(0, pl.cdiv(len_ref[0], TILE), per_tile, 0)
    dkv_ref[:, :PAIR] = dk_ref[...].astype(bf16)
    dkv_ref[:, PAIR:] = dv_ref[...].astype(bf16)


def cross_backward(queries, kv, mixture, grad_mixture, lse, seq_len):
    rows, slots = queries.shape[0], kv.shape[0]
    tiles = rows // TILE
    row_spec = pl.BlockSpec((rows, PAIR), lambda h, n: (0, h))
    kv_spec = pl.BlockSpec((slots, 2 * PAIR), lambda h, n: (0, h))
    return pl.pallas_call(
        cross_backward_kernel,
        name="cross_backward",
        out_shape=(
            jax.ShapeDtypeStruct((rows, D), bf16),
            jax.ShapeDtypeStruct((slots, 2 * D), bf16),
        ),
        grid_spec=pltpu.PrefetchScalarGridSpec(
            num_scalar_prefetch=1,
            grid=(PAIRS,),
            in_specs=[
                row_spec,
                kv_spec,
                row_spec,
                row_spec,
                pl.BlockSpec((1, tiles, 2 * TILE), lambda h, n: (h, 0, 0)),
            ],
            out_specs=[row_spec, kv_spec],
            scratch_shapes=[
                pltpu.VMEM((PAIR, slots), bf16),
                pltpu.VMEM((slots, PAIR), f32),
                pltpu.VMEM((slots, PAIR), f32),
            ],
        ),
        compiler_params=pltpu.CompilerParams(vmem_limit_bytes=VMEM_LIMIT),
        cost_estimate=pl.CostEstimate(
            flops=20 * rows * slots * D, bytes_accessed=2 * (4 * rows + 4 * slots) * D, transcendentals=rows * slots * 12
        ),
    )(seq_len, queries, kv, mixture, grad_mixture, lse)


def seen(shape, row_start, seq_len):
    keys = lax.broadcasted_iota(jnp.int32, shape, 0)
    rows = row_start + lax.rem(lax.broadcasted_iota(jnp.int32, shape, 1), TILE)
    return (keys <= rows) & (keys < seq_len)


def self_forward_kernel(len_ref, qkv_ref, out_ref, lse_ref, vt_ref):
    seq_len = len_ref[0]
    vt_ref[...] = qkv_ref[:, 2 * PAIR :].T
    out_ref[...] = jnp.zeros_like(out_ref)
    lse_ref[...] = jnp.zeros_like(lse_ref)
    for tile in range(qkv_ref.shape[0] // TILE):

        @pl.when(tile * TILE < seq_len)
        def _():
            rows = slice(tile * TILE, (tile + 1) * TILE)
            size = (tile + 1) * TILE
            queries = split_heads(qkv_ref[rows, :PAIR] * jnp.asarray(head_scale, bf16))
            scores = nt(qkv_ref[:size, PAIR : 2 * PAIR], queries)
            scores = jnp.where(seen(scores.shape, tile * TILE, seq_len), scores, neg_big)
            peak = jnp.max(scores, axis=0, keepdims=True)
            probs = jnp.exp(scores - peak)
            total = jnp.sum(probs, axis=0, keepdims=True)
            mixed = nn(vt_ref[:, :size], probs.astype(bf16))
            out_ref[rows, :] = join_heads(mixed / total).astype(bf16)
            lse_ref[0, tile : tile + 1, :] = peak + jnp.log(total)


def self_forward(qkv, seq_len):
    rows = qkv.shape[0]
    tiles = rows // TILE
    return pl.pallas_call(
        self_forward_kernel,
        name="self_forward",
        out_shape=(
            jax.ShapeDtypeStruct((rows, D), bf16),
            jax.ShapeDtypeStruct((PAIRS, tiles, 2 * TILE), f32),
        ),
        grid_spec=pltpu.PrefetchScalarGridSpec(
            num_scalar_prefetch=1,
            grid=(PAIRS,),
            in_specs=[pl.BlockSpec((rows, 3 * PAIR), lambda h, n: (0, h))],
            out_specs=[
                pl.BlockSpec((rows, PAIR), lambda h, n: (0, h)),
                pl.BlockSpec((1, tiles, 2 * TILE), lambda h, n: (h, 0, 0)),
            ],
            scratch_shapes=[pltpu.VMEM((PAIR, rows), bf16)],
        ),
        compiler_params=pltpu.CompilerParams(vmem_limit_bytes=VMEM_LIMIT),
        cost_estimate=pl.CostEstimate(
            flops=5 * rows * rows * D, bytes_accessed=8 * rows * D, transcendentals=rows * rows * 8
        ),
    )(seq_len, qkv)


def self_backward_kernel(len_ref, qkv_ref, mix_ref, grad_ref, lse_ref, dqkv_ref, kt_ref, dk_ref, dv_ref):
    seq_len = len_ref[0]
    kt_ref[...] = qkv_ref[:, PAIR : 2 * PAIR].T
    dqkv_ref[...] = jnp.zeros_like(dqkv_ref)
    dk_ref[...] = jnp.zeros_like(dk_ref)
    dv_ref[...] = jnp.zeros_like(dv_ref)
    for tile in range(qkv_ref.shape[0] // TILE):

        @pl.when(tile * TILE < seq_len)
        def _():
            rows = slice(tile * TILE, (tile + 1) * TILE)
            size = (tile + 1) * TILE
            queries = split_heads(qkv_ref[rows, :PAIR] * jnp.asarray(head_scale, bf16))
            grads = split_heads(grad_ref[rows, :])
            inner = row_dots(mix_ref[rows, :], grad_ref[rows, :])
            lse = lse_ref[0, tile : tile + 1, :]
            scores = nt(qkv_ref[:size, PAIR : 2 * PAIR], queries)
            scores = jnp.where(seen(scores.shape, tile * TILE, seq_len), scores, neg_big)
            probs = jnp.exp(scores - lse)
            dscores = (probs * (nt(qkv_ref[:size, 2 * PAIR :], grads) - inner)).astype(bf16)
            dv_ref[:size, :] += nn(probs.astype(bf16), grads)
            dk_ref[:size, :] += nn(dscores, queries)
            dq = nn(kt_ref[:, :size], dscores)
            dqkv_ref[rows, :PAIR] = join_heads(dq).astype(bf16) * jnp.asarray(head_scale, bf16)

    dqkv_ref[:, PAIR : 2 * PAIR] = dk_ref[...].astype(bf16)
    dqkv_ref[:, 2 * PAIR :] = dv_ref[...].astype(bf16)


def self_backward(qkv, mixture, grad_mixture, lse, seq_len):
    rows = qkv.shape[0]
    tiles = rows // TILE
    row_spec = pl.BlockSpec((rows, PAIR), lambda h, n: (0, h))
    qkv_spec = pl.BlockSpec((rows, 3 * PAIR), lambda h, n: (0, h))
    return pl.pallas_call(
        self_backward_kernel,
        name="self_backward",
        out_shape=jax.ShapeDtypeStruct((rows, 3 * D), bf16),
        grid_spec=pltpu.PrefetchScalarGridSpec(
            num_scalar_prefetch=1,
            grid=(PAIRS,),
            in_specs=[
                qkv_spec,
                row_spec,
                row_spec,
                pl.BlockSpec((1, tiles, 2 * TILE), lambda h, n: (h, 0, 0)),
            ],
            out_specs=qkv_spec,
            scratch_shapes=[
                pltpu.VMEM((PAIR, rows), bf16),
                pltpu.VMEM((rows, PAIR), f32),
                pltpu.VMEM((rows, PAIR), f32),
            ],
        ),
        compiler_params=pltpu.CompilerParams(vmem_limit_bytes=VMEM_LIMIT),
        cost_estimate=pl.CostEstimate(
            flops=12 * rows * rows * D, bytes_accessed=16 * rows * D, transcendentals=rows * rows * 8
        ),
    )(seq_len, qkv, mixture, grad_mixture, lse)


def dot(left, right):
    return jnp.dot(left, right, preferred_element_type=f32)


def dot_t(left, right):
    return jnp.einsum("re,de->rd", left, right, preferred_element_type=f32)


def by_pair(weight, parts):
    rows = weight.shape[0]
    return weight.reshape(rows, parts, PAIRS, PAIR).swapaxes(1, 2).reshape(rows, parts * D)


def by_part(weight, parts):
    rows = weight.shape[0]
    return weight.reshape(rows, PAIRS, parts, PAIR).swapaxes(1, 2).reshape(rows, parts * D)


def gather_rows(shard):
    half = lax.all_gather(shard, "fsdp", axis=0, tiled=True)
    half = lax.optimization_barrier(half)
    return lax.all_gather(half, "grp", axis=0, tiled=True)


def scatter_sum(grad):
    n_grp, n_fsdp = lax.axis_size("grp"), lax.axis_size("fsdp")
    bits = [("grp", b) for b in range(n_grp.bit_length() - 1)]
    bits += [("fsdp", b) for b in range(n_fsdp.bit_length() - 1)]
    rows = grad.shape[0] // (n_grp * n_fsdp)
    total = len(bits)
    current = grad.reshape((2,) * total + (rows,) + grad.shape[1:])
    dims = [("grp", b) for b in reversed(range(n_grp.bit_length() - 1))]
    dims += [("fsdp", b) for b in reversed(range(n_fsdp.bit_length() - 1))]
    for step, (axis, b) in enumerate(bits):
        dim = dims.index((axis, b))
        dims.pop(dim)
        mine = (lax.axis_index(axis) >> b) & 1
        sent = lax.dynamic_index_in_dim(current, 1 - mine, dim, keepdims=False)
        kept = lax.dynamic_index_in_dim(current, mine, dim, keepdims=False)
        count = lax.axis_size(axis)
        got = lax.ppermute(sent, axis, [(i, i ^ (1 << b)) for i in range(count)])
        current = kept.astype(f32) + got.astype(f32)
        if step + 1 < total:
            current = current.astype(grad.dtype)
    return current


def shards(
    tokens,
    frames,
    lengths,
    cotangent,
    self_in,
    self_out,
    cross_q,
    cross_kv,
    cross_out,
    fc_in,
    fc_out,
    norm_gain,
    norm_bias,
):
    fsdp_count = lax.axis_size("fsdp")
    group_seqs = lengths.shape[0]
    per_device = group_seqs // fsdp_count
    seq_ids = jnp.arange(group_seqs, dtype=jnp.int32)
    rank_order = jnp.argsort(-(lengths * group_seqs + (group_seqs - 1 - seq_ids)))
    rank_ids = np.arange(group_seqs)
    rounds = rank_ids // fsdp_count
    places = rank_ids % fsdp_count
    rank_of = np.where(rounds % 2 == 0, rank_ids, rounds * fsdp_count + fsdp_count - 1 - places)
    sender = rank_order[jnp.asarray(rank_of, dtype=jnp.int32)]
    slot_of_seq = jnp.argsort(sender)
    device = lax.axis_index("fsdp")

    def bring(array, slot):
        picked = array[sender[slot * fsdp_count : (slot + 1) * fsdp_count]]
        moved = lax.all_to_all(picked, "fsdp", split_axis=0, concat_axis=0, tiled=True)
        return moved.reshape(-1, array.shape[-1])

    def send_back(array):
        parts = array.reshape(fsdp_count, -1, array.shape[-1])
        return lax.all_to_all(parts, "fsdp", split_axis=0, concat_axis=0, tiled=True)

    norms = jnp.concatenate(
        [norm_gain, norm_bias, jnp.zeros((norm_gain.shape[0], 120), bf16)], axis=1
    )
    group_one = gather_rows(jnp.concatenate([by_pair(self_in, 3), self_out, norms], axis=1))
    group_two = gather_rows(jnp.concatenate([by_pair(cross_kv, 2), cross_q, cross_out], axis=1))
    w_fc_in = gather_rows(fc_in)
    n_all = lax.axis_size("grp") * fsdp_count
    w_fc_out = gather_rows(fc_out)
    w_self_in = group_one[:, : 3 * D]
    w_self_out = group_one[:, 3 * D : 4 * D]
    gains = group_one[:, 4 * D : 4 * D + 4].astype(f32)
    biases = group_one[:, 4 * D + 4 : 4 * D + 8].astype(f32)
    w_cross_kv = group_two[:, : 2 * D]
    w_cross_q = group_two[:, 2 * D : 3 * D]
    w_cross_out = group_two[:, 3 * D :]

    tok = [bring(tokens, s) for s in range(per_device)]
    frm = [bring(frames, s) for s in range(per_device)]
    cot = [bring(cotangent, s) for s in range(per_device)]
    lens = [
        lax.dynamic_slice_in_dim(lengths[sender], s * fsdp_count + device, 1)
        for s in range(per_device)
    ]

    results = []
    for slot in range(per_device):
        seq_len = lens[slot]
        stream = tok[slot].astype(f32)
        valid = (lax.broadcasted_iota(jnp.int32, (stream.shape[0], 1), 0) < seq_len[0]).astype(f32)
        normed_one, pull_one = jax.vjp(layer_norm, stream, gains[:, 0], biases[:, 0])
        normed_one = normed_one.astype(bf16)
        qkv = dot(normed_one, w_self_in).astype(bf16)
        mixture, lse = self_forward(qkv, seq_len)
        after_self = stream + dot(mixture, w_self_out)
        normed_two, pull_two = jax.vjp(layer_norm, after_self, gains[:, 1], biases[:, 1])
        normed_two = normed_two.astype(bf16)
        queries_two = dot(normed_two, w_cross_q).astype(bf16)
        kv = dot(frm[slot], w_cross_kv).astype(bf16)
        mixture_two, lse_two = cross_forward(queries_two, kv, seq_len)
        after_cross = after_self + dot(mixture_two, w_cross_out)
        normed_three, pull_three = jax.vjp(layer_norm, after_cross, gains[:, 2], biases[:, 2])
        normed_three = normed_three.astype(bf16)
        pre_act = dot(normed_three, w_fc_in)
        activated, pull_gelu = jax.vjp(exact_gelu, pre_act)
        hidden = activated.astype(bf16)
        after_mlp = after_cross + dot(hidden, w_fc_out)
        final_norm, pull_four = jax.vjp(layer_norm, after_mlp, gains[:, 3], biases[:, 3])
        output = (final_norm * valid).astype(bf16)

        grad_mlp, gain_four, shift_four = pull_four(cot[slot].astype(f32) * valid)
        branch_three = grad_mlp.astype(bf16)
        grad_pre = pull_gelu(dot_t(branch_three, w_fc_out))[0].astype(bf16)
        norm_three_in, gain_three, shift_three = pull_three(dot_t(grad_pre, w_fc_in))
        grad_cross = grad_mlp + norm_three_in
        branch_two = grad_cross.astype(bf16)
        grad_mixture_two = dot_t(branch_two, w_cross_out).astype(bf16)
        grad_q_two, grad_kv = cross_backward(
            queries_two, kv, mixture_two, grad_mixture_two, lse_two, seq_len
        )
        grad_frames = dot_t(grad_kv, w_cross_kv).astype(bf16)
        norm_two_in, gain_two, shift_two = pull_two(dot_t(grad_q_two, w_cross_q))
        grad_attn = grad_cross + norm_two_in
        branch_one = grad_attn.astype(bf16)
        grad_mixture = dot_t(branch_one, w_self_out).astype(bf16)
        grad_qkv = self_backward(qkv, mixture, grad_mixture, lse, seq_len)
        norm_one_in, gain_one, shift_one = pull_one(dot_t(grad_qkv, w_self_in))
        grad_tokens = (grad_attn + norm_one_in).astype(bf16)
        norm_grads = jnp.stack(
            [gain_one, gain_two, gain_three, gain_four, shift_one, shift_two, shift_three, shift_four],
            axis=1,
        )
        results.append(
            dict(
                output=output,
                grad_tokens=grad_tokens,
                grad_frames=grad_frames,
                norm=norm_grads,
                fc_out=(hidden, branch_three),
                fc_in=(normed_three, grad_pre),
                cross_out=(mixture_two, branch_two),
                cross_q=(normed_two, grad_q_two),
                cross_kv=(frm[slot], grad_kv),
                self_out=(mixture, branch_one),
                self_in=(normed_one, grad_qkv),
            )
        )

    def weight_grad(name):
        total = None
        for res in results:
            left, right = res[name]
            part = jnp.einsum("rd,re->de", left, right, preferred_element_type=f32)
            total = part if total is None else total + part
        return total.astype(bf16)

    def finish(name):
        back = jnp.concatenate([send_back(res[name]) for res in results], axis=0)
        return back[slot_of_seq]

    g_fc_out = scatter_sum(weight_grad("fc_out"))
    g_fc_in = scatter_sum(weight_grad("fc_in"))
    g_two = scatter_sum(
        jnp.concatenate([weight_grad(n) for n in ("cross_kv", "cross_q", "cross_out")], axis=1)
    )
    g_one = scatter_sum(jnp.concatenate([weight_grad(n) for n in ("self_in", "self_out")], axis=1))
    norm_sum = results[0]["norm"]
    for res in results[1:]:
        norm_sum = norm_sum + res["norm"]
    g_norm = scatter_sum(norm_sum.reshape(n_all, 1, -1)).reshape(-1, 8)
    grad_frames_final = finish("grad_frames")
    output_final = finish("output")
    grad_tokens_final = finish("grad_tokens")
    return (
        output_final,
        grad_tokens_final,
        grad_frames_final,
        by_part(g_one[:, : 3 * D], 3),
        g_one[:, 3 * D :],
        g_two[:, 2 * D : 3 * D],
        by_part(g_two[:, : 2 * D], 2),
        g_two[:, 3 * D :],
        g_fc_in,
        g_fc_out,
        g_norm[:, :4],
        g_norm[:, 4:],
    )


def solution(mesh):
    rows = P(("grp", "fsdp"), None)
    seqs = P("grp", "fsdp", None)
    return jax.shard_map(
        shards,
        mesh=mesh,
        in_specs=(seqs, seqs, P("grp"), seqs) + (rows,) * 9,
        out_specs=(seqs,) * 3 + (rows,) * 9,
        check_vma=False,
    )
```

time: 1660 us -> 1040 us (0.63)
  blocking collectives: 289 us -> 0 us
  matrix products: 469 us -> 220 us
  waiting for transfers between devices: 581 us -> 402 us
  Pallas kernels: 0 us -> 146 us
  other arithmetic: 142 us -> 60.8 us
  starting transfers between devices: 31.9 us -> 104 us
  local copies, waits for them, and re-layouts: 121 us -> 71.5 us
    reduce_scatter x7 -> x0, waiting for transfers between devices: 462 us -> none  [the longest x1 142 us: shards(): lax.psum_scatter(grad_list[5], ('grp', 'fsdp'), scatter_dimension=0, tile...]
    dot_general x66 -> x42, matrix products: 469 us -> 220 us  [the longest x14 88.6 us: dot(): return jnp.dot(left, right, preferred_element_type=f32)]
    all_gather x2 -> x0, blocking collectives: 163 us -> none  [the longest x1 99.6 us: shards(): lax.all_gather(norm_gain, ('grp', 'fsdp'), axis=0, tiled=True)]
    pallas_call x0 -> x8, Pallas kernels: none -> 146 us  [the longest x2 59.6 us: cross_backward(): pl.pallas_call(cross_backward_kernel, name='cross_backward', out_shape=(j...]
    unnamed x1 -> x0, blocking collectives: 126 us -> none
    all_to_all x6 -> x12, waiting for transfers between devices: 99.4 us -> 210 us  [the longest x6 173 us: bring(): lax.all_to_all(picked, 'fsdp', split_axis=0, concat_axis=0, tiled=True)]
    ppermute x0 -> x25, waiting for transfers between devices: none -> 106 us  [scatter_sum(): got = lax.ppermute(sent, axis, [(i, i ^ 1 << b) for i in range(count)])]
    all_gather x7 -> x8, waiting for transfers between devices: 14.9 us -> 84 us  [the longest x4 84 us: gather_rows(): half = lax.all_gather(shard, 'fsdp', axis=0, tiled=True)]
  transfers between devices with their start and end apart: 20 -> 45, of which waited for: 8 -> 22; matrix products, arithmetic and copies ran while one was open for 30% -> 20% of each run, Pallas kernels for 0% -> 2%
where the time goes in v1:
time: 1040 us; the launch traced here: 1020 us
  waiting for transfers between devices  402 us (39%)
  matrix products  220 us (21%)
  Pallas kernels  146 us (14%)
  starting transfers between devices  104 us (10%)
  local copies, waits for them, and re-layouts  71.5 us (7%)
  other arithmetic  60.8 us (6%)
  between operations  16.6 us (2%)
    all_to_all x6, waiting for transfers between devices, bring(): lax.all_to_all(picked, 'fsdp', split_axis=0, concat_axis=0, tiled=True)  173 us
    ppermute x25, waiting for transfers between devices, scatter_sum(): got = lax.ppermute(sent, axis, [(i, i ^ 1 << b) for i in range(count)])  106 us
    dot_general x14, matrix products, dot(): return jnp.dot(left, right, preferred_element_type=f32)  88.6 us
    all_gather x4, waiting for transfers between devices, gather_rows(): half = lax.all_gather(shard, 'fsdp', axis=0, tiled=True)  84 us
    dot_general x14, matrix products, dot_t(): return jnp.einsum('re,de->rd', left, right, preferred_element_type=f32)  70.3 us
    dot_general x14, matrix products, weight_grad(): part = jnp.einsum('rd,re->de', left, right, preferred_element_type=f32)  61.4 us
    pallas_call x2, Pallas kernels, cross_backward(): pl.pallas_call(cross_backward_kernel, name='cross_backward', out_shape=(j...  59.6 us
    all_to_all x6, starting transfers between devices, send_back(): lax.all_to_all(parts, 'fsdp', split_axis=0, concat_axis=0, tiled=True)  44.2 us
  transfers between devices with their start and end apart: 45, of which 22 were waited for; matrix products, arithmetic and copies ran while one was open for 20% of the time, Pallas kernels for 2%

profile of v1, /device:TPU:0, one launch (start us, length us, event | category | flops | bytes accessed | tf_op | source)
XLA Modules:
  0.0 1021.0 jit_solution(8310403216067818674)
XLA Ops:
  13.6 41.0 %all-gather.13.cloned.1.call-done = bf16[192,3072]{1,0:T(8,128)(2,1)} async-done(((bf16[24,3072]{1,0:T(8,128)(2,1)}), bf16[192,3072]{1,0:T(8,128)(2,1)}) %all-gather.13.cloned.1.call-update) | async-done | bytes 1179664 | tf_op jit(solution)/shard_map/all_gather | solution.py:337
  54.7 42.9 %all-gather.9.cloned.1.call-done = bf16[192,3200]{1,0:T(8,128)(2,1)} async-done(((bf16[24,3200]{1,0:T(8,128)(2,1)}), bf16[192,3200]{1,0:T(8,128)(2,1)}) %all-gather.9.cloned.1.call-update) | async-done | bytes 1228816 | tf_op jit(solution)/shard_map/all_gather | solution.py:337
  106.2 22.5 %all-to-all-done = bf16[8,64,768]{2,1,0:T(8,128)(2,1)S(1)} async-done(((bf16[8,64,768]{2,1,0:T(8,128)(2,1)}), bf16[8,64,768]{2,1,0:T(8,128)(2,1)S(1)}, u32[]{:S(2)}, u32[]{:S(2)}) %all-to-all-start) | async-done | bytes 786464 | tf_op jit(solution)/shard_map/all_to_all | solution.py:395
  135.1 24.0 %all-to-all-done.3 = bf16[8,64,768]{2,1,0:T(8,128)(2,1)S(1)} async-done(((bf16[8,64,768]{2,1,0:T(8,128)(2,1)}), bf16[8,64,768]{2,1,0:T(8,128)(2,1)S(1)}, u32[]{:S(2)}, u32[]{:S(2)}) %all-to-all-start.3) | async-done | bytes 786464 | tf_op jit(solution)/shard_map/all_to_all | solution.py:395
  165.6 22.0 %all-to-all-done.6 = bf16[8,64,768]{2,1,0:T(8,128)(2,1)S(1)} async-done(((bf16[8,64,768]{2,1,0:T(8,128)(2,1)}), bf16[8,64,768]{2,1,0:T(8,128)(2,1)S(1)}, u32[]{:S(2)}, u32[]{:S(2)}) %all-to-all-start.6) | async-done | bytes 786464 | tf_op jit(solution)/shard_map/all_to_all | solution.py:395
  195.6 21.8 %all-to-all-done.8 = bf16[8,64,768]{2,1,0:T(8,128)(2,1)S(1)} async-done(((bf16[8,64,768]{2,1,0:T(8,128)(2,1)}), bf16[8,64,768]{2,1,0:T(8,128)(2,1)S(1)}, u32[]{:S(2)}, u32[]{:S(2)}) %all-to-all-start.8) | async-done | bytes 786464 | tf_op jit(solution)/shard_map/all_to_all | solution.py:395
  222.6 4.9 gather_fusion.3
  227.5 48.4 %all-to-all-done.4 = bf16[8,192,768]{2,1,0:T(8,128)(2,1)} async-done(((bf16[8,192,768]{2,1,0:T(8,128)(2,1)}), bf16[8,192,768]{2,1,0:T(8,128)(2,1)}, u32[]{:S(2)}, u32[]{:S(2)}) %all-to-all-start.4) | async-done | bytes 2359328 | tf_op jit(solution)/shard_map/all_to_all | solution.py:395
  290.5 8.4 convolution_convert_fusion.kv_ref
  298.8 34.8 %all-to-all-done.1 = bf16[8,192,768]{2,1,0:T(8,128)(2,1)} async-done(((bf16[8,192,768]{2,1,0:T(8,128)(2,1)}), bf16[8,192,768]{2,1,0:T(8,128)(2,1)}, u32[]{:S(2)}, u32[]{:S(2)}) %all-to-all-start.1) | async-done | bytes 2359328 | tf_op jit(solution)/shard_map/all_to_all | solution.py:395
  333.6 8.6 convolution_convert_fusion.1.kv_ref
  350.0 6.9 self_forward.3
  362.9 10.2 cross_forward.3
  375.8 19.8 %multiply_convert_fusion = (bf16[512,3072]{1,0:T(8,128)(2,1)}, f32[512,3072]{1,0:T(8,128)}, f32[512,3072]{1,0:T(8,128)}) fusion(bf16[768,3072]{1,0:T(8,128)(2,1)} %all-gather.19.cloned.1.call-done, f32[512,768]{1,0:T(8,128)S(1)} %get-tuple-element.153, f32[512]{0:T(512)S(1)} %fusion.105, f32[512]{0:T(512)S(1)} %broadcast_multiply_fusion.3, ...), kind=kOutput, calls=%fused_computation.22 | convolution fusion | flops 2520121344 | bytes 22030336 | tf_op jit(solution)/shard_map/dot_general | solution.py:319
  395.7 6.6 fusion.139
  406.7 15.7 %self_forward.2 = (bf16[512,768]{1,0:T(8,128)(2,1)}, f32[6,4,256]{2,1,0:T(4,128)}) custom-call(s32[1]{0:T(128)} %get-tuple-element.139.len_ref, bf16[512,2304]{1,0:T(8,128)(2,1)} %convolution_convert_fusion.3.qkv_ref), custom_call_target="tpu_custom_call" | custom-call | flops 1006632960 | bytes 3145728 | tf_op jit(solution)/shard_map/self_forward/pallas_call | solution.py:233
  428.3 30.0 %cross_forward.2 = (bf16[512,768]{1,0:T(8,128)(2,1)}, f32[6,4,256]{2,1,0:T(4,128)}) custom-call(s32[1]{0:T(128)} %get-tuple-element.139.len_ref, bf16[512,768]{1,0:T(8,128)(2,1)} %convolution_convert_fusion.11.q_ref, bf16[1536,1536]{1,0:T(8,128)(2,1)} %convolution_convert_fusion.1.kv_ref), custom_call_target="tpu_custom_call" | custom-call | flops 4831838208 | bytes 6291456 | tf_op jit(solution)/shard_map/cross_forward/pallas_call | solution.py:103
  461.1 19.7 %multiply_convert_fusion.1 = (bf16[512,3072]{1,0:T(8,128)(2,1)S(1)}, f32[512,3072]{1,0:T(8,128)}, f32[512,3072]{1,0:T(8,128)}) fusion(bf16[768,3072]{1,0:T(8,128)(2,1)} %all-gather.19.cloned.1.call-done, f32[512,768]{1,0:T(8,128)S(1)} %get-tuple-element.146, f32[768]{0:T(1024)S(1)} %get-tuple-element.81, f32[768]{0:T(1024)S(1)} %get-tuple-element.162, ...), kind=kOutput, calls=%fused_computation.35 | convolution fusion | flops 2520121344 | bytes 22030336 | tf_op jit(solution)/shard_map/dot_general | solution.py:319
  488.9 5.2 fusion.112
  494.1 8.2 add_convert_fusion.4
  502.3 7.5 fusion.118
  509.8 9.3 add_convert_fusion.3
  524.0 5.6 multiply_reduce_fusion.6
  538.2 44.9 %cross_backward.2 = (bf16[512,768]{1,0:T(8,128)(2,1)}, bf16[1536,1536]{1,0:T(8,128)(2,1)}) custom-call(s32[1]{0:T(128)} %get-tuple-element.139.len_ref, bf16[512,768]{1,0:T(8,128)(2,1)} %convolution_convert_fusion.11.q_ref, bf16[1536,1536]{1,0:T(8,128)(2,1)} %convolution_convert_fusion.1.kv_ref, bf16[512,768]{1,0:T(8,128)(2,1)} %get-tuple-element.28.mix_ref, ...), custom_call_target="tpu_custom_call" | custom-call | flops 12079595520 | bytes 12582912 | tf_op jit(solution)/shard_map/cross_backward/pallas_call | solution.py:171
  590.0 14.7 %cross_backward.3 = (bf16[512,768]{1,0:T(8,128)(2,1)}, bf16[1536,1536]{1,0:T(8,128)(2,1)}) custom-call(s32[1]{0:T(128)} %get-tuple-element.140.len_ref, bf16[512,768]{1,0:T(8,128)(2,1)} %convolution_convert_fusion.10.q_ref, bf16[1536,1536]{1,0:T(8,128)(2,1)} %convolution_convert_fusion.kv_ref, bf16[512,768]{1,0:T(8,128)(2,1)} %get-tuple-element.30.mix_ref, ...), custom_call_target="tpu_custom_call" | custom-call | flops 12079595520 | bytes 12582912 | tf_op jit(solution)/shard_map/cross_backward/pallas_call | solution.py:171
  615.3 16.1 %self_backward.2 = bf16[512,2304]{1,0:T(8,128)(2,1)} custom-call(s32[1]{0:T(128)} %get-tuple-element.139.len_ref, bf16[512,2304]{1,0:T(8,128)(2,1)} %convolution_convert_fusion.3.qkv_ref, bf16[512,768]{1,0:T(8,128)(2,1)} %get-tuple-element.27.mix_ref, bf16[512,768]{1,0:T(8,128)(2,1)} %convolution_convert_fusion.8.grad_ref, ...), custom_call_target="tpu_custom_call" | custom-call | flops 2415919104 | bytes 6291456 | tf_op jit(solution)/shard_map/self_backward/pallas_call | solution.py:291
  631.4 6.7 fusion.141
  641.8 7.9 self_backward.3
  663.7 7.8 add_convert_fusion
  675.8 6.1 add_convert_fusion.1
  685.9 5.7 fusion.142
  694.5 5.9 add_convert_fusion.5
  708.3 23.6 %all-to-all-start.7 = ((bf16[8,64,768]{2,1,0:T(8,128)(2,1)}), bf16[8,64,768]{2,1,0:T(8,128)(2,1)S(1)}, u32[]{:S(2)}, u32[]{:S(2)}) async-start(bf16[8,64,768]{2,1,0:T(8,128)(2,1)} %bitcast.292), calls=%async_computation.7 | async-start | bytes 1572864 | tf_op jit(solution)/shard_map/all_to_all | solution.py:400
  733.8 7.0 add_convert_fusion.2
  741.7 10.5 %all-to-all-done.7 = bf16[8,64,768]{2,1,0:T(8,128)(2,1)S(1)} async-done(((bf16[8,64,768]{2,1,0:T(8,128)(2,1)}), bf16[8,64,768]{2,1,0:T(8,128)(2,1)S(1)}, u32[]{:S(2)}, u32[]{:S(2)}) %all-to-all-start.7) | async-done | bytes 786464 | tf_op jit(solution)/shard_map/all_to_all | solution.py:400
  766.2 9.9 all-to-all-done.9
  781.8 8.4 convolution_convert_fusion.5
  804.3 8.4 convolution_convert_fusion.4
  816.4 7.8 all-to-all-done.5
  850.6 13.7 %collective-permute-done.16 = bf16[2,2,2,96,768]{4,3,0,1,2:T(8,128)(2,1)S(1)} collective-permute-done((bf16[2,2,2,96,768]{4,3,0,1,2:T(8,128)(2,1)S(1)}, bf16[2,2,2,96,768]{4,3,0,1,2:T(8,128)(2,1)S(1)}, u32[]{:S(2)}, u32[]{:S(2)}) %collective-permute-start.16) | collective-permute-done | bytes 1179680 | tf_op jit(solution)/shard_map/ppermute | solution.py:358
  866.6 22.9 %collective-permute-done.11 = bf16[2,2,2,24,3072]{4,3,0,1,2:T(8,128)(2,1)S(1)} collective-permute-done((bf16[2,2,2,24,3072]{4,3,0,1,2:T(8,128)(2,1)S(1)}, bf16[2,2,2,24,3072]{4,3,0,1,2:T(8,128)(2,1)S(1)}, u32[]{:S(2)}, u32[]{:S(2)}) %collective-permute-start.11) | collective-permute-done | bytes 1179680 | tf_op jit(solution)/shard_map/ppermute | solution.py:358
  892.8 22.0 %collective-permute-done.6 = bf16[2,2,2,24,3072]{4,3,0,1,2:T(8,128)(2,1)S(1)} collective-permute-done((bf16[2,2,2,24,3072]{4,3,0,1,2:T(8,128)(2,1)S(1)}, bf16[2,2,2,24,3072]{4,3,0,1,2:T(8,128)(2,1)S(1)}, u32[]{:S(2)}, u32[]{:S(2)}) %collective-permute-start.6) | collective-permute-done | bytes 1179680 | tf_op jit(solution)/shard_map/ppermute | solution.py:358
  923.7 14.4 %collective-permute-done.1 = bf16[2,2,2,24,3072]{4,3,0,1,2:T(8,128)(2,1)} collective-permute-done((bf16[2,2,2,24,3072]{4,3,0,1,2:T(8,128)(2,1)}, bf16[2,2,2,24,3072]{4,3,0,1,2:T(8,128)(2,1)}, u32[]{:S(2)}, u32[]{:S(2)}) %collective-permute-start.1) | collective-permute-done | bytes 1179680 | tf_op jit(solution)/shard_map/ppermute | solution.py:358
  952.4 13.9 %collective-permute-done.2 = bf16[2,2,24,3072]{3,2,0,1:T(8,128)(2,1)S(1)} collective-permute-done((bf16[2,2,24,3072]{3,2,0,1:T(8,128)(2,1)S(1)}, bf16[2,2,24,3072]{3,2,0,1:T(8,128)(2,1)S(1)}, u32[]{:S(2)}, u32[]{:S(2)}) %collective-permute-start.2) | collective-permute-done | bytes 589856 | tf_op jit(solution)/shard_map/ppermute | solution.py:358
  967.8 5.5 all-to-all-done.11
  973.2 4.9 pad_maximum_fusion
  978.2 5.6 gather_fusion.10
  993.2 13.6 %collective-permute-done.9 = bf16[24,3072]{1,0:T(8,128)(2,1)S(1)} collective-permute-done((bf16[24,3072]{1,0:T(8,128)(2,1)S(1)}, bf16[24,3072]{1,0:T(8,128)(2,1)S(1)}, u32[]{:S(2)}, u32[]{:S(2)}) %collective-permute-start.9) | collective-permute-done | bytes 147488 | tf_op jit(solution)/shard_map/ppermute | solution.py:358
  (538 shorter events, 272.6 us)
Async XLA Ops:
  7.2 47.4 %all-gather.13.cloned.1.call-start = ((), (), s32[]{:S(2)}) async-start(), calls=%async_computation.14 | async-start | bytes 1327104 | tf_op jit(solution)/shard_map/all_gather | solution.py:337
  10.0 87.7 %all-gather.9.cloned.1.call-start = ((), (), s32[]{:S(2)}) async-start(), calls=%async_computation.12 | async-start | bytes 1382400 | tf_op jit(solution)/shard_map/all_gather | solution.py:337
  12.2 209.6 %all-gather.17.cloned.1.call-start = ((), (), s32[]{:S(2)}) async-start(), calls=%async_computation.16 | async-start | bytes 1327104 | tf_op jit(solution)/shard_map/all_gather | solution.py:337
  13.0 277.4 %all-gather.21.cloned.1.call-start = ((), (), s32[]{:S(2)}) async-start(), calls=%async_computation.18 | async-start | bytes 1327104 | tf_op jit(solution)/shard_map/all_gather | solution.py:337
  13.6 276.9 %all-gather.15.cloned.1.call-start = ((), (), s32[]{:S(2)}) async-start(), calls=%async_computation.15 | async-start | bytes 5898240 | tf_op jit(solution)/shard_map/all_gather | solution.py:339
  54.6 287.6 %all-gather.11.cloned.1.call-start = ((), (), s32[]{:S(2)}) async-start(), calls=%async_computation.13 | async-start | bytes 6144000 | tf_op jit(solution)/shard_map/all_gather | solution.py:339
  101.2 27.5 %all-to-all-start = ((bf16[8,64,768]{2,1,0:T(8,128)(2,1)}), bf16[8,64,768]{2,1,0:T(8,128)(2,1)S(1)}, u32[]{:S(2)}, u32[]{:S(2)}) async-start(bf16[8,64,768]{2,1,0:T(8,128)(2,1)} %gather_fusion.1), calls=%async_computation | async-start | bytes 1572864 | tf_op jit(solution)/shard_map/all_to_all | solution.py:395
  128.7 293.8 %copy-start.3 = (bf16[8,64,768]{2,1,0:T(8,128)(2,1)}, bf16[8,64,768]{2,1,0:T(8,128)(2,1)S(1)}, u32[]{:S(2)}) copy-start(bf16[8,64,768]{2,1,0:T(8,128)(2,1)S(1)} %all-to-all-done) | copy-start | bytes 2359300
  128.7 30.5 %all-to-all-start.3 = ((bf16[8,64,768]{2,1,0:T(8,128)(2,1)}), bf16[8,64,768]{2,1,0:T(8,128)(2,1)S(1)}, u32[]{:S(2)}, u32[]{:S(2)}) async-start(bf16[8,64,768]{2,1,0:T(8,128)(2,1)} %gather_fusion.4), calls=%async_computation.3 | async-start | bytes 1572864 | tf_op jit(solution)/shard_map/all_to_all | solution.py:395
  159.1 28.4 %all-to-all-start.6 = ((bf16[8,64,768]{2,1,0:T(8,128)(2,1)}), bf16[8,64,768]{2,1,0:T(8,128)(2,1)S(1)}, u32[]{:S(2)}, u32[]{:S(2)}) async-start(bf16[8,64,768]{2,1,0:T(8,128)(2,1)} %gather_fusion.7), calls=%async_computation.6 | async-start | bytes 1572864 | tf_op jit(solution)/shard_map/all_to_all | solution.py:395
  187.6 29.8 %all-to-all-start.8 = ((bf16[8,64,768]{2,1,0:T(8,128)(2,1)}), bf16[8,64,768]{2,1,0:T(8,128)(2,1)S(1)}, u32[]{:S(2)}, u32[]{:S(2)}) async-start(bf16[8,64,768]{2,1,0:T(8,128)(2,1)} %gather_fusion.8), calls=%async_computation.8 | async-start | bytes 1572864 | tf_op jit(solution)/shard_map/all_to_all | solution.py:395
  217.4 58.5 %all-to-all-start.4 = ((bf16[8,192,768]{2,1,0:T(8,128)(2,1)}), bf16[8,192,768]{2,1,0:T(8,128)(2,1)}, u32[]{:S(2)}, u32[]{:S(2)}) async-start(bf16[8,192,768]{2,1,0:T(8,128)(2,1)} %gather_fusion.5), calls=%async_computation.4 | async-start | bytes 4718592 | tf_op jit(solution)/shard_map/all_to_all | solution.py:395
  221.8 154.0 %all-gather.19.cloned.1.call-start = ((), (), s32[]{:S(2)}) async-start(), calls=%async_computation.17 | async-start | bytes 5898240 | tf_op jit(solution)/shard_map/all_gather | solution.py:339
  275.9 57.8 %all-to-all-start.1 = ((bf16[8,192,768]{2,1,0:T(8,128)(2,1)}), bf16[8,192,768]{2,1,0:T(8,128)(2,1)}, u32[]{:S(2)}, u32[]{:S(2)}) async-start(bf16[8,192,768]{2,1,0:T(8,128)(2,1)} %gather_fusion.3), calls=%async_computation.1 | async-start | bytes 4718592 | tf_op jit(solution)/shard_map/all_to_all | solution.py:395
  280.2 115.4 %all-gather.23.cloned.1.call-start = ((), (), s32[]{:S(2)}) async-start(), calls=%async_computation.19 | async-start | bytes 5898240 | tf_op jit(solution)/shard_map/all_gather | solution.py:339
  344.9 238.1 %copy-start.93 = (f32[768]{0:T(1024)}, f32[768]{0:T(1024)S(1)}, u32[]{:S(2)}) copy-start(f32[768]{0:T(1024)S(1)} %get-tuple-element.82) | copy-start | bytes 9220
  345.0 265.1 %copy-start.79 = (f32[768]{0:T(1024)}, f32[768]{0:T(1024)S(1)}, u32[]{:S(2)}) copy-start(f32[768]{0:T(1024)S(1)} %get-tuple-element.161) | copy-start | bytes 9220
  663.7 92.1 %collective-permute-start.20 = (f32[2,2,2,2,1,1,192]{6,3,2,1,0,5,4:T(2,128)}, f32[2,2,2,2,1,1,192]{6,3,2,1,0,5,4:T(2,128)}, u32[]{:S(2)}, u32[]{:S(2)}) collective-permute-start(f32[2,2,2,2,1,1,192]{6,3,2,1,0,5,4:T(2,128)} %dynamic-slice_bitcast_fusion.16), channel_id=1, source_target_pairs={{0,8},{8,0},{16,24},{24,16},{1,9},{9,1},{17,25},{25,17},{2,10},{10... | collective-permute-start | bytes 36872 | tf_op jit(solution)/shard_map/ppermute | solution.py:358
  674.9 157.2 %collective-permute-start.15 = (bf16[2,2,2,2,96,768]{5,4,1,2,3,0:T(8,128)(2,1)}, bf16[2,2,2,2,96,768]{5,4,1,2,3,0:T(8,128)(2,1)}, u32[]{:S(2)}, u32[]{:S(2)}) collective-permute-start(bf16[2,2,2,2,96,768]{5,4,1,2,3,0:T(8,128)(2,1)} %bitcast.281), channel_id=1, source_target_pairs={{0,8},{8,0},{16,24},{24,16},{1,9},{9,1},{17,25},{25,17},{2,10},{10... | collective-permute-start | bytes 7077896 | tf_op jit(solution)/shard_map/ppermute | solution.py:358
  685.3 151.5 %collective-permute-start.10 = (bf16[2,2,2,2,24,3072]{5,4,1,2,3,0:T(8,128)(2,1)}, bf16[2,2,2,2,24,3072]{5,4,1,2,3,0:T(8,128)(2,1)}, u32[]{:S(2)}, u32[]{:S(2)}) collective-permute-start(bf16[2,2,2,2,24,3072]{5,4,1,2,3,0:T(8,128)(2,1)} %bitcast.282), channel_id=1, source_target_pairs={{0,8},{8,0},{16,24},{24,16},{1,9},{9,1},{17,25},{25,17},{2,10},{10... | collective-permute-start | bytes 7077896 | tf_op jit(solution)/shard_map/ppermute | solution.py:358
  704.5 136.6 %collective-permute-start.5 = (bf16[2,2,2,2,24,3072]{5,4,1,2,3,0:T(8,128)(2,1)}, bf16[2,2,2,2,24,3072]{5,4,1,2,3,0:T(8,128)(2,1)}, u32[]{:S(2)}, u32[]{:S(2)}) collective-permute-start(bf16[2,2,2,2,24,3072]{5,4,1,2,3,0:T(8,128)(2,1)} %bitcast.283), channel_id=1, source_target_pairs={{0,8},{8,0},{16,24},{24,16},{1,9},{9,1},{17,25},{25,17},{2,10},{10... | collective-permute-start | bytes 7077896 | tf_op jit(solution)/shard_map/ppermute | solution.py:358
  708.3 43.9 %all-to-all-start.7 = ((bf16[8,64,768]{2,1,0:T(8,128)(2,1)}), bf16[8,64,768]{2,1,0:T(8,128)(2,1)S(1)}, u32[]{:S(2)}, u32[]{:S(2)}) async-start(bf16[8,64,768]{2,1,0:T(8,128)(2,1)} %bitcast.292), calls=%async_computation.7 | async-start | bytes 1572864 | tf_op jit(solution)/shard_map/all_to_all | solution.py:400
  752.2 23.9 %all-to-all-start.9 = ((bf16[8,64,768]{2,1,0:T(8,128)(2,1)}), bf16[8,64,768]{2,1,0:T(8,128)(2,1)S(1)}, u32[]{:S(2)}, u32[]{:S(2)}) async-start(bf16[8,64,768]{2,1,0:T(8,128)(2,1)} %bitcast.15), calls=%async_computation.9 | async-start | bytes 1572864 | tf_op jit(solution)/shard_map/all_to_all | solution.py:400
  756.5 4.1 collective-permute-start.21
  760.7 19.0 %collective-permute-start.22 = (f32[2,2,1,1,192]{4,2,3,1,0:T(1,128)S(1)}, f32[2,2,1,1,192]{4,2,3,1,0:T(1,128)S(1)}, u32[]{:S(2)}, u32[]{:S(2)}) collective-permute-start(f32[2,2,1,1,192]{4,2,3,1,0:T(1,128)S(1)} %fusion.91), channel_id=1, source_target_pairs={{0,1},{1,0},{2,3},{3,2},{4,5},{5,4},{6,7},{7,6},{8,9},{9,8},{10,11... | collective-permute-start | bytes 9224 | tf_op jit(solution)/shard_map/ppermute | solution.py:358
  766.2 79.1 %collective-permute-start = (bf16[2,2,2,2,24,3072]{5,4,1,2,3,0:T(8,128)(2,1)}, bf16[2,2,2,2,24,3072]{5,4,1,2,3,0:T(8,128)(2,1)}, u32[]{:S(2)}, u32[]{:S(2)}) collective-permute-start(bf16[2,2,2,2,24,3072]{5,4,1,2,3,0:T(8,128)(2,1)} %bitcast.284), channel_id=1, source_target_pairs={{0,8},{8,0},{16,24},{24,16},{1,9},{9,1},{17,25},{25,17},{2,10},{10... | collective-permute-start | bytes 7077896 | tf_op jit(solution)/shard_map/ppermute | solution.py:358
  776.2 24.0 %all-to-all-start.2 = ((bf16[8,64,768]{2,1,0:T(8,128)(2,1)}), bf16[8,64,768]{2,1,0:T(8,128)(2,1)S(1)}, u32[]{:S(2)}, u32[]{:S(2)}) async-start(bf16[8,64,768]{2,1,0:T(8,128)(2,1)} %bitcast.7), calls=%async_computation.2 | async-start | bytes 1572864 | tf_op jit(solution)/shard_map/all_to_all | solution.py:400
  779.8 13.0 %collective-permute-start.23 = (f32[2,1,1,192]{3,2,1,0:T(1,128)S(1)}, f32[2,1,1,192]{3,2,1,0:T(1,128)S(1)}, u32[]{:S(2)}, u32[]{:S(2)}) collective-permute-start(f32[2,1,1,192]{3,2,1,0:T(1,128)S(1)} %fusion.98), channel_id=1, source_target_pairs={{0,2},{1,3},{2,0},{3,1},{4,6},{5,7},{6,4},{7,5},{8,10},{9,11},{10,... | collective-permute-start | bytes 4616 | tf_op jit(solution)/shard_map/ppermute | solution.py:358
  792.8 20.0 %collective-permute-start.24 = (f32[1,1,192]{2,1,0:T(1,128)S(1)}, f32[1,1,192]{2,1,0:T(1,128)S(1)}, u32[]{:S(2)}, u32[]{:S(2)}) collective-permute-start(f32[1,1,192]{2,1,0:T(1,128)S(1)} %fusion.110), channel_id=1, source_target_pairs={{0,4},{1,5},{2,6},{3,7},{4,0},{5,1},{6,2},{7,3},{8,12},{9,13},{10,... | collective-permute-start | bytes 2312 | tf_op jit(solution)/shard_map/ppermute | solution.py:358
  800.1 24.1 %all-to-all-start.5 = ((bf16[8,64,768]{2,1,0:T(8,128)(2,1)}), bf16[8,64,768]{2,1,0:T(8,128)(2,1)}, u32[]{:S(2)}, u32[]{:S(2)}) async-start(bf16[8,64,768]{2,1,0:T(8,128)(2,1)} %bitcast.11), calls=%async_computation.5 | async-start | bytes 1572864 | tf_op jit(solution)/shard_map/all_to_all | solution.py:400
  824.2 94.9 %all-to-all-start.10 = ((bf16[8,192,768]{2,1,0:T(8,128)(2,1)}), bf16[8,192,768]{2,1,0:T(8,128)(2,1)}, u32[]{:S(2)}, u32[]{:S(2)}) async-start(bf16[8,192,768]{2,1,0:T(8,128)(2,1)} %bitcast.294), calls=%async_computation.10 | async-start | bytes 4718592 | tf_op jit(solution)/shard_map/all_to_all | solution.py:400
  835.3 29.0 %collective-permute-start.16 = (bf16[2,2,2,96,768]{4,3,0,1,2:T(8,128)(2,1)S(1)}, bf16[2,2,2,96,768]{4,3,0,1,2:T(8,128)(2,1)S(1)}, u32[]{:S(2)}, u32[]{:S(2)}) collective-permute-start(bf16[2,2,2,96,768]{4,3,0,1,2:T(8,128)(2,1)S(1)} %dynamic-slice_bitcast_fusion), channel_id=1, source_target_pairs={{0,16},{8,24},{16,0},{24,8},{1,17},{9,25},{17,1},{25,9},{2,18},{10... | collective-permute-start | bytes 3538952 | tf_op jit(solution)/shard_map/ppermute | solution.py:358
  839.5 50.0 %collective-permute-start.11 = (bf16[2,2,2,24,3072]{4,3,0,1,2:T(8,128)(2,1)S(1)}, bf16[2,2,2,24,3072]{4,3,0,1,2:T(8,128)(2,1)S(1)}, u32[]{:S(2)}, u32[]{:S(2)}) collective-permute-start(bf16[2,2,2,24,3072]{4,3,0,1,2:T(8,128)(2,1)S(1)} %dynamic-slice_bitcast_fusion.1), channel_id=1, source_target_pairs={{0,16},{8,24},{16,0},{24,8},{1,17},{9,25},{17,1},{25,9},{2,18},{10... | collective-permute-start | bytes 3538952 | tf_op jit(solution)/shard_map/ppermute | solution.py:358
  843.8 71.1 %collective-permute-start.6 = (bf16[2,2,2,24,3072]{4,3,0,1,2:T(8,128)(2,1)S(1)}, bf16[2,2,2,24,3072]{4,3,0,1,2:T(8,128)(2,1)S(1)}, u32[]{:S(2)}, u32[]{:S(2)}) collective-permute-start(bf16[2,2,2,24,3072]{4,3,0,1,2:T(8,128)(2,1)S(1)} %dynamic-slice_bitcast_fusion.2), channel_id=1, source_target_pairs={{0,16},{8,24},{16,0},{24,8},{1,17},{9,25},{17,1},{25,9},{2,18},{10... | collective-permute-start | bytes 3538952 | tf_op jit(solution)/shard_map/ppermute | solution.py:358
  849.1 89.0 %collective-permute-start.1 = (bf16[2,2,2,24,3072]{4,3,0,1,2:T(8,128)(2,1)}, bf16[2,2,2,24,3072]{4,3,0,1,2:T(8,128)(2,1)}, u32[]{:S(2)}, u32[]{:S(2)}) collective-permute-start(bf16[2,2,2,24,3072]{4,3,0,1,2:T(8,128)(2,1)} %dynamic-slice_bitcast_fusion.3), channel_id=1, source_target_pairs={{0,16},{8,24},{16,0},{24,8},{1,17},{9,25},{17,1},{25,9},{2,18},{10... | collective-permute-start | bytes 3538952 | tf_op jit(solution)/shard_map/ppermute | solution.py:358
  864.6 77.4 %collective-permute-start.17 = (bf16[2,2,96,768]{3,2,0,1:T(8,128)(2,1)S(1)}, bf16[2,2,96,768]{3,2,0,1:T(8,128)(2,1)}, u32[]{:S(2)}, u32[]{:S(2)}) collective-permute-start(bf16[2,2,96,768]{3,2,0,1:T(8,128)(2,1)S(1)} %dynamic-slice_bitcast_fusion.4), channel_id=1, source_target_pairs={{0,1},{1,0},{2,3},{3,2},{4,5},{5,4},{6,7},{7,6},{8,9},{9,8},{10,11... | collective-permute-start | bytes 1769480 | tf_op jit(solution)/shard_map/ppermute | solution.py:358
  890.9 54.5 %collective-permute-start.12 = (bf16[2,2,24,3072]{3,2,0,1:T(8,128)(2,1)}, bf16[2,2,24,3072]{3,2,0,1:T(8,128)(2,1)}, u32[]{:S(2)}, u32[]{:S(2)}) collective-permute-start(bf16[2,2,24,3072]{3,2,0,1:T(8,128)(2,1)} %dynamic-slice_bitcast_fusion.5), channel_id=1, source_target_pairs={{0,1},{1,0},{2,3},{3,2},{4,5},{5,4},{6,7},{7,6},{8,9},{9,8},{10,11... | collective-permute-start | bytes 1769480 | tf_op jit(solution)/shard_map/ppermute | solution.py:358
  917.2 31.3 %collective-permute-start.7 = (bf16[2,2,24,3072]{3,2,0,1:T(8,128)(2,1)}, bf16[2,2,24,3072]{3,2,0,1:T(8,128)(2,1)}, u32[]{:S(2)}, u32[]{:S(2)}) collective-permute-start(bf16[2,2,24,3072]{3,2,0,1:T(8,128)(2,1)} %dynamic-slice_bitcast_fusion.6), channel_id=1, source_target_pairs={{0,1},{1,0},{2,3},{3,2},{4,5},{5,4},{6,7},{7,6},{8,9},{9,8},{10,11... | collective-permute-start | bytes 1769480 | tf_op jit(solution)/shard_map/ppermute | solution.py:358
  919.1 54.1 %all-to-all-start.11 = ((bf16[8,192,768]{2,1,0:T(8,128)(2,1)}), bf16[8,192,768]{2,1,0:T(8,128)(2,1)}, u32[]{:S(2)}, u32[]{:S(2)}) async-start(bf16[8,192,768]{2,1,0:T(8,128)(2,1)} %bitcast.293), calls=%async_computation.11 | async-start | bytes 4718592 | tf_op jit(solution)/shard_map/all_to_all | solution.py:400
  940.2 26.2 %collective-permute-start.2 = (bf16[2,2,24,3072]{3,2,0,1:T(8,128)(2,1)S(1)}, bf16[2,2,24,3072]{3,2,0,1:T(8,128)(2,1)S(1)}, u32[]{:S(2)}, u32[]{:S(2)}) collective-permute-start(bf16[2,2,24,3072]{3,2,0,1:T(8,128)(2,1)S(1)} %dynamic-slice_bitcast_fusion.7), channel_id=1, source_target_pairs={{0,1},{1,0},{2,3},{3,2},{4,5},{5,4},{6,7},{7,6},{8,9},{9,8},{10,11... | collective-permute-start | bytes 1769480 | tf_op jit(solution)/shard_map/ppermute | solution.py:358
  944.0 39.8 %collective-permute-start.18 = (bf16[2,96,768]{2,1,0:T(8,128)(2,1)}, bf16[2,96,768]{2,1,0:T(8,128)(2,1)S(1)}, u32[]{:S(2)}, u32[]{:S(2)}) collective-permute-start(bf16[2,96,768]{2,1,0:T(8,128)(2,1)} %dynamic-slice_bitcast_fusion.8), channel_id=1, source_target_pairs={{0,2},{1,3},{2,0},{3,1},{4,6},{5,7},{6,4},{7,5},{8,10},{9,11},{10,... | collective-permute-start | bytes 884744 | tf_op jit(solution)/shard_map/ppermute | solution.py:358
  946.7 37.2 %collective-permute-start.13 = (bf16[2,24,3072]{2,1,0:T(8,128)(2,1)S(1)}, bf16[2,24,3072]{2,1,0:T(8,128)(2,1)}, u32[]{:S(2)}, u32[]{:S(2)}) collective-permute-start(bf16[2,24,3072]{2,1,0:T(8,128)(2,1)S(1)} %dynamic-slice_bitcast_fusion.9), channel_id=1, source_target_pairs={{0,2},{1,3},{2,0},{3,1},{4,6},{5,7},{6,4},{7,5},{8,10},{9,11},{10,... | collective-permute-start | bytes 884744 | tf_op jit(solution)/shard_map/ppermute | solution.py:358
  950.4 37.6 %collective-permute-start.8 = (bf16[2,24,3072]{2,1,0:T(8,128)(2,1)}, bf16[2,24,3072]{2,1,0:T(8,128)(2,1)}, u32[]{:S(2)}, u32[]{:S(2)}) collective-permute-start(bf16[2,24,3072]{2,1,0:T(8,128)(2,1)} %dynamic-slice_bitcast_fusion.10), channel_id=1, source_target_pairs={{0,2},{1,3},{2,0},{3,1},{4,6},{5,7},{6,4},{7,5},{8,10},{9,11},{10,... | collective-permute-start | bytes 884744 | tf_op jit(solution)/shard_map/ppermute | solution.py:358
  967.3 21.9 %collective-permute-start.3 = (bf16[2,24,3072]{2,1,0:T(8,128)(2,1)}, bf16[2,24,3072]{2,1,0:T(8,128)(2,1)}, u32[]{:S(2)}, u32[]{:S(2)}) collective-permute-start(bf16[2,24,3072]{2,1,0:T(8,128)(2,1)} %dynamic-slice_bitcast_fusion.11), channel_id=1, source_target_pairs={{0,2},{1,3},{2,0},{3,1},{4,6},{5,7},{6,4},{7,5},{8,10},{9,11},{10,... | collective-permute-start | bytes 884744 | tf_op jit(solution)/shard_map/ppermute | solution.py:358
  983.8 26.9 %collective-permute-start.19 = (bf16[96,768]{1,0:T(8,128)(2,1)S(1)}, bf16[96,768]{1,0:T(8,128)(2,1)S(1)}, u32[]{:S(2)}, u32[]{:S(2)}) collective-permute-start(bf16[96,768]{1,0:T(8,128)(2,1)S(1)} %dynamic-slice_bitcast_fusion.12), channel_id=1, source_target_pairs={{0,4},{1,5},{2,6},{3,7},{4,0},{5,1},{6,2},{7,3},{8,12},{9,13},{10,... | collective-permute-start | bytes 442376 | tf_op jit(solution)/shard_map/ppermute | solution.py:358
  985.0 27.2 %collective-permute-start.14 = (bf16[24,3072]{1,0:T(8,128)(2,1)S(1)}, bf16[24,3072]{1,0:T(8,128)(2,1)}, u32[]{:S(2)}, u32[]{:S(2)}) collective-permute-start(bf16[24,3072]{1,0:T(8,128)(2,1)S(1)} %dynamic-slice_bitcast_fusion.13), channel_id=1, source_target_pairs={{0,4},{1,5},{2,6},{3,7},{4,0},{5,1},{6,2},{7,3},{8,12},{9,13},{10,... | collective-permute-start | bytes 442376 | tf_op jit(solution)/shard_map/ppermute | solution.py:358
  989.0 17.7 %collective-permute-start.9 = (bf16[24,3072]{1,0:T(8,128)(2,1)S(1)}, bf16[24,3072]{1,0:T(8,128)(2,1)S(1)}, u32[]{:S(2)}, u32[]{:S(2)}) collective-permute-start(bf16[24,3072]{1,0:T(8,128)(2,1)S(1)} %dynamic-slice_bitcast_fusion.14), channel_id=1, source_target_pairs={{0,4},{1,5},{2,6},{3,7},{4,0},{5,1},{6,2},{7,3},{8,12},{9,13},{10,... | collective-permute-start | bytes 442376 | tf_op jit(solution)/shard_map/ppermute | solution.py:358
  990.2 18.1 %collective-permute-start.4 = (bf16[24,3072]{1,0:T(8,128)(2,1)S(1)}, bf16[24,3072]{1,0:T(8,128)(2,1)S(1)}, u32[]{:S(2)}, u32[]{:S(2)}) collective-permute-start(bf16[24,3072]{1,0:T(8,128)(2,1)S(1)} %dynamic-slice_bitcast_fusion.15), channel_id=1, source_target_pairs={{0,4},{1,5},{2,6},{3,7},{4,0},{5,1},{6,2},{7,3},{8,12},{9,13},{10,... | collective-permute-start | bytes 442376 | tf_op jit(solution)/shard_map/ppermute | solution.py:358
  (115 other events, 2227.1 us)
Sparse Core Ops, SparseCore 0:
  10.8 43.7 all-gather.12
  57.4 40.2 all-gather.8
  99.8 57.4 all-gather.16
  159.3 55.6 all-gather.20
  216.4 34.9 all-gather.14
  252.8 38.5 all-gather.10
  293.0 37.4 all-gather.18
  332.0 37.4 all-gather.22

commit v2 on v1

v2 whole, which is shorter than its diff:
```python
import functools

import jax
import jax.numpy as jnp
import numpy as np
from jax import lax
from jax.experimental import pallas as pl
from jax.experimental.pallas import tpu as pltpu
from jax.sharding import PartitionSpec as P

D = 768
FF = 3072
HEAD_DIM = 64
FRAMES = 1500
PAIR = 2 * HEAD_DIM
PAIRS = D // PAIR
TILE = 128
ROWS = 256
KEY_CHUNK = 256
FF_PARTS = FF // D

eps_norm = 1e-05
neg_big = -1e30
head_scale = 0.125
bf16 = jnp.bfloat16
f32 = jnp.float32
MIB = 1024 * 1024
COST = pl.CostEstimate(flops=1000000, bytes_accessed=1000000, transcendentals=0)

ONE_OUT = 3 * D
ONE_Q = 4 * D
ONE_NORM = 5 * D
ONE_COLS = 5 * D + 128
TWO_OUT = 2 * D


def nt(left, right):
    return lax.dot_general(left, right, (((1,), (1,)), ((), ())), preferred_element_type=f32)


def nn(left, right):
    return lax.dot_general(left, right, (((1,), (0,)), ((), ())), preferred_element_type=f32)


def normalize(stream):
    centered = stream - jnp.mean(stream, axis=-1, keepdims=True)
    scale = lax.rsqrt(jnp.mean(centered * centered, axis=-1, keepdims=True) + eps_norm)
    return centered * scale, scale


def norm_backward(normed, scale, gain, grad):
    scaled = grad * gain
    mean_scaled = jnp.mean(scaled, axis=-1, keepdims=True)
    mean_along = jnp.mean(scaled * normed, axis=-1, keepdims=True)
    return scale * (scaled - mean_scaled - normed * mean_along)


def col_sum(values):
    return jnp.sum(values, axis=0, keepdims=True)


def split_heads(block):
    lanes = lax.broadcasted_iota(jnp.int32, block.shape, 1)
    zero = jnp.zeros_like(block)
    return jnp.concatenate(
        [jnp.where(lanes < HEAD_DIM, block, zero), jnp.where(lanes < HEAD_DIM, zero, block)], axis=0
    )


def join_heads(stacked):
    return jnp.concatenate([stacked[:HEAD_DIM, :TILE], stacked[HEAD_DIM:, TILE:]], axis=0).T


def row_dots(left, right):
    prod = (left.astype(f32) * right.astype(f32)).T
    return jnp.concatenate([col_sum(prod[:HEAD_DIM]), col_sum(prod[HEAD_DIM:])], axis=1)


def seen(shape, row_start, seq_len):
    keys = lax.broadcasted_iota(jnp.int32, shape, 0)
    rows = row_start + lax.rem(lax.broadcasted_iota(jnp.int32, shape, 1), TILE)
    return (keys <= rows) & (keys < seq_len)


def each_tile(count, size, body):
    def step(i, carry):
        body(pl.ds(pl.multiple_of(i * size, size), size), i)
        return carry

    lax.fori_loop(0, count, step, 0)


def lane_block(index):
    return pl.ds(pl.multiple_of(index * PAIR, PAIR), PAIR)


def token_rows(ref, tile):
    count = ROWS // ref.shape[1]
    return ref[pl.ds(tile * count, count)].reshape(ROWS, D).astype(f32)


def clear(*refs):
    for ref in refs:
        ref[...] = jnp.zeros_like(ref)


scale_of_heads = functools.partial(jnp.asarray, head_scale, bf16)


def self_part_forward(
    len_ref, tok_ref, one_ref, norm_ref,
    qkv_ref, normed_one_ref, mix_ref, lse_ref, after_ref, normed_two_ref, q_two_ref,
    vt_ref,
):
    seq_len = len_ref[0]
    row_tiles = pl.cdiv(seq_len, ROWS)
    clear(normed_one_ref, mix_ref, lse_ref, normed_two_ref)

    def project(rows, i):
        normed, _ = normalize(token_rows(tok_ref, i))
        normed = (normed * norm_ref[0:1, :] + norm_ref[4:5, :]).astype(bf16)
        normed_one_ref[rows, :] = normed
        qkv_ref[rows, :] = nn(normed, one_ref[:, :ONE_OUT]).astype(bf16)

    each_tile(row_tiles, ROWS, project)

    def per_pair(pair, carry):
        q_lanes, k_lanes, v_lanes = (lane_block(3 * pair + i) for i in range(3))
        for tile in range(qkv_ref.shape[0] // TILE):

            @pl.when(tile * TILE < seq_len)
            def _():
                rows = slice(tile * TILE, (tile + 1) * TILE)
                size = (tile + 1) * TILE
                vt_ref[:, rows] = qkv_ref[rows, v_lanes].T
                queries = split_heads(qkv_ref[rows, q_lanes] * scale_of_heads())
                scores = nt(qkv_ref[:size, k_lanes], queries)
                scores = jnp.where(seen(scores.shape, tile * TILE, seq_len), scores, neg_big)
                peak = jnp.max(scores, axis=0, keepdims=True)
                probs = jnp.exp(scores - peak)
                total = col_sum(probs)
                mixed = nn(vt_ref[:, :size], probs.astype(bf16))
                mix_ref[rows, lane_block(pair)] = join_heads(mixed / total).astype(bf16)
                lse_ref[pair, tile : tile + 1, :] = peak + jnp.log(total)

        return carry

    lax.fori_loop(0, PAIRS, per_pair, 0)

    def finish(rows, i):
        after = token_rows(tok_ref, i) + nn(mix_ref[rows, :], one_ref[:, ONE_OUT:ONE_Q])
        after_ref[rows, :] = after
        normed, _ = normalize(after)
        normed = (normed * norm_ref[1:2, :] + norm_ref[5:6, :]).astype(bf16)
        normed_two_ref[rows, :] = normed
        q_two_ref[rows, :] = nn(normed, one_ref[:, ONE_Q:ONE_NORM]).astype(bf16)

    each_tile(row_tiles, ROWS, finish)


PARTS = {"frames": 4, "tokens": 4, "first": 2, "second": 2}


def part_at(part):
    return {"frames": 0, "tokens": 3, "first": 0, "second": 1}[part]


def whole():
    return pl.BlockSpec(memory_space=pltpu.VMEM)


def in_smem():
    return pl.BlockSpec(memory_space=pltpu.SMEM)


def shape_of(*dims, dtype=bf16):
    return jax.ShapeDtypeStruct(dims, dtype)


def in_hbm(*dims, dtype=bf16):
    return pltpu.HBM(dims, dtype)


def run_self_forward(seq_len, arrived, part, one, norm_rows):
    blocks, size = arrived.shape[0], arrived.shape[1] // PARTS[part]
    at = part_at(part)
    rows = blocks * size
    fixed = lambda *dims: pl.BlockSpec(dims, lambda i: (0,) * len(dims), pipeline_mode=pl.Buffered(1))
    shapes = [
        in_hbm(rows, 3 * D),
        in_hbm(rows, D),
        in_hbm(rows, D),
        in_hbm(PAIRS, rows // TILE, 2 * TILE, dtype=f32),
        in_hbm(rows, D, dtype=f32),
        in_hbm(rows, D),
        in_hbm(rows, D),
    ]
    return pl.pallas_call(
        self_part_forward,
        name="self_part_forward",
        grid=(1,),
        in_specs=[
            in_smem(),
            pl.BlockSpec((blocks, size, D), lambda i: (0, at, 0), pipeline_mode=pl.Buffered(1)),
            fixed(*one.shape),
            fixed(8, D),
        ],
        out_specs=[fixed(*s.shape) for s in shapes],
        out_shape=shapes,
        scratch_shapes=[pltpu.VMEM((PAIR, rows), bf16)],
        compiler_params=pltpu.CompilerParams(vmem_limit_bytes=36 * MIB),
        cost_estimate=COST,
    )(seq_len, arrived, one, norm_rows)


def cross_forward_kernel(len_ref, frm_ref, w_ref, q_ref, out_ref, lse_ref, kv_ref, vt_ref, s_ref):
    slots = kv_ref.shape[0]
    clear(out_ref, lse_ref)
    kv_ref[...] = nn(frm_ref[...].reshape(slots, D), w_ref[...]).astype(bf16)
    vt_ref[...] = kv_ref[:, PAIR:].T
    spans = [(k, min(KEY_CHUNK, slots - k)) for k in range(0, slots, KEY_CHUNK)]

    def per_tile(rows, tile):
        queries = split_heads(q_ref[rows, :] * scale_of_heads())
        peak = jnp.full((1, 2 * TILE), neg_big, f32)
        for start, size in spans:
            scores = nt(kv_ref[start : start + size, :PAIR], queries)
            if start + size > FRAMES:
                keys = start + lax.broadcasted_iota(jnp.int32, scores.shape, 0)
                scores = jnp.where(keys < FRAMES, scores, neg_big)
            s_ref[start : start + size, :] = scores
            peak = jnp.maximum(peak, jnp.max(scores, axis=0, keepdims=True))
        total = jnp.zeros((1, 2 * TILE), f32)
        mixed = jnp.zeros((PAIR, 2 * TILE), f32)
        for start, size in spans:
            probs = jnp.exp(s_ref[start : start + size, :] - peak)
            total = total + col_sum(probs)
            mixed = mixed + nn(vt_ref[:, start : start + size], probs.astype(bf16))
        out_ref[rows, :] = join_heads(mixed / total).astype(bf16)
        lse_ref[0, pl.ds(tile, 1), :] = peak + jnp.log(total)

    each_tile(pl.cdiv(len_ref[0], TILE), TILE, per_tile)


def run_cross_forward(seq_len, arrived, two, q_two):
    blocks, size = arrived.shape[0], 3 * arrived.shape[1] // 4
    rows, slots = q_two.shape[0], blocks * size
    tiles = rows // TILE
    return pl.pallas_call(
        cross_forward_kernel,
        name="cross_forward",
        grid=(PAIRS,),
        in_specs=[
            in_smem(),
            pl.BlockSpec((blocks, size, D), lambda h: (0, 0, 0), pipeline_mode=pl.Buffered(1)),
            pl.BlockSpec((D, 2 * PAIR), lambda h: (0, h)),
            pl.BlockSpec((rows, PAIR), lambda h: (0, h)),
        ],
        out_specs=[
            pl.BlockSpec((rows, PAIR), lambda h: (0, h)),
            pl.BlockSpec((1, tiles, 2 * TILE), lambda h: (h, 0, 0)),
            pl.BlockSpec((slots, 2 * PAIR), lambda h: (0, h)),
        ],
        out_shape=[
            in_hbm(rows, D),
            in_hbm(PAIRS, tiles, 2 * TILE, dtype=f32),
            in_hbm(slots, 2 * D),
        ],
        scratch_shapes=[pltpu.VMEM((PAIR, slots), bf16), pltpu.VMEM((slots, 2 * TILE), f32)],
        compiler_params=pltpu.CompilerParams(vmem_limit_bytes=24 * MIB),
        cost_estimate=COST,
    )(seq_len, arrived, two, q_two)


def cross_backward_kernel(
    len_ref, q_ref, kv_ref, mix_ref, grad_ref, lse_ref, w_ref, _,
    dq_ref, dkv_ref, dfrm_ref,
    kt_ref, dk_ref, dv_ref, acc_ref,
):
    slots = kv_ref.shape[0]
    pair = pl.program_id(0)
    kt_ref[...] = kv_ref[:, :PAIR].T
    clear(dq_ref, dk_ref, dv_ref)
    spans = [(k, min(KEY_CHUNK, slots - k)) for k in range(0, slots, KEY_CHUNK)]

    def per_tile(rows, tile):
        queries = split_heads(q_ref[rows, :] * scale_of_heads())
        grads = split_heads(grad_ref[rows, :])
        inner = row_dots(mix_ref[rows, :], grad_ref[rows, :])
        lse = lse_ref[0, pl.ds(tile, 1), :]
        dq = jnp.zeros((PAIR, 2 * TILE), f32)
        for start, size in spans:
            span = slice(start, start + size)
            probs = jnp.exp(nt(kv_ref[span, :PAIR], queries) - lse)
            if start + size > FRAMES:
                keys = start + lax.broadcasted_iota(jnp.int32, probs.shape, 0)
                probs = jnp.where(keys < FRAMES, probs, 0.0)
            dscores = (probs * (nt(kv_ref[span, PAIR:], grads) - inner)).astype(bf16)
            dv_ref[span, :] += nn(probs.astype(bf16), grads)
            dk_ref[span, :] += nn(dscores, queries)
            dq = dq + nn(kt_ref[:, span], dscores)
        dq_ref[rows, :] = join_heads(dq).astype(bf16) * scale_of_heads()

    each_tile(pl.cdiv(len_ref[0], TILE), TILE, per_tile)
    dkv_ref[:, :PAIR] = dk_ref[...].astype(bf16)
    dkv_ref[:, PAIR:] = dv_ref[...].astype(bf16)
    part = nt(dkv_ref[...], w_ref[...])

    @pl.when(pair == 0)
    def _():
        acc_ref[...] = part

    @pl.when((pair > 0) & (pair < PAIRS - 1))
    def _():
        acc_ref[...] += part

    @pl.when(pair == PAIRS - 1)
    def _():
        dfrm_ref[...] = (acc_ref[...] + part).astype(bf16).reshape(dfrm_ref.shape)


def run_cross_backward(seq_len, q_two, kv, mix, grad_mix, lse, two, leaving):
    rows, slots, blocks = q_two.shape[0], kv.shape[0], leaving.shape[0]
    tiles = rows // TILE
    row_spec = pl.BlockSpec((rows, PAIR), lambda h: (0, h))
    kv_spec = pl.BlockSpec((slots, 2 * PAIR), lambda h: (0, h))
    return pl.pallas_call(
        cross_backward_kernel,
        name="cross_backward",
        grid=(PAIRS,),
        in_specs=[
            in_smem(),
            row_spec,
            kv_spec,
            row_spec,
            row_spec,
            pl.BlockSpec((1, tiles, 2 * TILE), lambda h: (h, 0, 0)),
            pl.BlockSpec((D, 2 * PAIR), lambda h: (0, h)),
            pl.BlockSpec(memory_space=pl.ANY),
        ],
        out_specs=[
            row_spec,
            kv_spec,
            pl.BlockSpec((blocks, slots // blocks, D), lambda h: (0, 0, 0), pipeline_mode=pl.Buffered(1)),
        ],
        out_shape=[in_hbm(rows, D), in_hbm(slots, 2 * D), in_hbm(*leaving.shape)],
        input_output_aliases={7: 2},
        scratch_shapes=[
            pltpu.VMEM((PAIR, slots), bf16),
            pltpu.VMEM((slots, PAIR), f32),
            pltpu.VMEM((slots, PAIR), f32),
            pltpu.VMEM((slots, D), f32),
        ],
        compiler_params=pltpu.CompilerParams(vmem_limit_bytes=36 * MIB),
        cost_estimate=COST,
    )(seq_len, q_two, kv, mix, grad_mix, lse, two, leaving)


def middle_kernel(
    len_ref, mix_ref, after_ref, cot_ref, two_ref, fc_ref, norm_ref,
    out_ref, normed_ref, hidden_ref, grad_pre_ref, branch_three_ref, branch_two_ref,
    grad_cross_ref, grad_mix_ref, norm_grad_ref,
    slope_ref,
):
    seq_len = len_ref[0]
    step = pl.program_id(0)
    parts = [(slice(k, k + D), slice(FF + k, FF + k + D)) for k in range(0, FF, D)]

    @pl.when(step == 0)
    def _():
        clear(norm_grad_ref)

    @pl.when(step * ROWS >= seq_len)
    def _():
        clear(out_ref, normed_ref, hidden_ref, grad_pre_ref, branch_three_ref, branch_two_ref)
        clear(grad_cross_ref, grad_mix_ref)

    @pl.when(step * ROWS < seq_len)
    def _():
        w_out = two_ref[:, TWO_OUT:]
        after_cross = after_ref[...] + nn(mix_ref[...], w_out)
        n_three, scale_three = normalize(after_cross)
        normed = (n_three * norm_ref[2:3, :] + norm_ref[6:7, :]).astype(bf16)
        normed_ref[...] = normed
        mlp = jnp.zeros((ROWS, D), f32)
        for span, rows_out in parts:
            pre = nn(normed, fc_ref[:, span])
            below = 0.5 * (1.0 + lax.erf(pre * np.float32(np.sqrt(0.5))))
            density = jnp.exp(-0.5 * pre * pre) * np.float32(1.0 / np.sqrt(2.0 * np.pi))
            slope_ref[:, span] = below + pre * density
            hidden = (pre * below).astype(bf16)
            hidden_ref[:, span] = hidden
            mlp = mlp + nn(hidden, fc_ref[:, rows_out])
        n_four, scale_four = normalize(after_cross + mlp)
        row_ids = step * ROWS + lax.broadcasted_iota(jnp.int32, (ROWS, 1), 0)
        valid = (row_ids < seq_len).astype(f32)
        output = ((n_four * norm_ref[3:4, :] + norm_ref[7:8, :]) * valid).astype(bf16)
        out_ref[...] = output.reshape(out_ref.shape)

        grad = cot_ref[...].reshape(ROWS, D).astype(f32) * valid
        norm_grad_ref[1:2, :] += col_sum(grad * n_four)
        norm_grad_ref[3:4, :] += col_sum(grad)
        grad_mlp = norm_backward(n_four, scale_four, norm_ref[3:4, :], grad)
        branch_three = grad_mlp.astype(bf16)
        branch_three_ref[...] = branch_three
        back = jnp.zeros((ROWS, D), f32)
        for span, rows_out in parts:
            grad_pre = (nt(branch_three, fc_ref[:, rows_out]) * slope_ref[:, span]).astype(bf16)
            grad_pre_ref[:, span] = grad_pre
            back = back + nt(grad_pre, fc_ref[:, span])
        norm_grad_ref[0:1, :] += col_sum(back * n_three)
        norm_grad_ref[2:3, :] += col_sum(back)
        grad_cross = grad_mlp + norm_backward(n_three, scale_three, norm_ref[2:3, :], back)
        grad_cross_ref[...] = grad_cross
        branch_two = grad_cross.astype(bf16)
        branch_two_ref[...] = branch_two
        grad_mix_ref[...] = nt(branch_two, w_out).astype(bf16)


def run_middle(seq_len, mix, after, arrived, part, two, fc, norm_rows):
    rows, blocks = mix.shape[0], arrived.shape[0]
    size = rows // blocks
    at = part_at(part)
    count = ROWS // size
    row_spec = pl.BlockSpec((ROWS, D), lambda i: (i, 0))
    wide_spec = pl.BlockSpec((ROWS, FF), lambda i: (i, 0))

    def fixed(*dims):
        return pl.BlockSpec(dims, lambda i: (0, 0), pipeline_mode=pl.Buffered(1))

    return pl.pallas_call(
        middle_kernel,
        name="mlp_and_back",
        grid=(rows // ROWS,),
        in_specs=[
            in_smem(), row_spec, row_spec, pl.BlockSpec((count, size, D), lambda i: (i, at, 0)),
            fixed(D, 3 * D), fixed(D, 2 * FF), fixed(8, D),
        ],
        out_specs=[pl.BlockSpec((count, size, D), lambda i: (i, 3, 0)), row_spec, wide_spec, wide_spec, row_spec, row_spec, row_spec, row_spec,
                   pl.BlockSpec((8, D), lambda i: (0, 0))],
        out_shape=[
            in_hbm(blocks, 4 * size, D), in_hbm(rows, D), in_hbm(rows, FF), in_hbm(rows, FF),
            in_hbm(rows, D), in_hbm(rows, D), in_hbm(rows, D, dtype=f32), in_hbm(rows, D),
            in_hbm(8, D, dtype=f32),
        ],
        scratch_shapes=[pltpu.VMEM((ROWS, FF), f32)],
        compiler_params=pltpu.CompilerParams(vmem_limit_bytes=48 * MIB),
        cost_estimate=COST,
    )(seq_len, mix, after, arrived, two, fc, norm_rows)


def self_part_backward(
    len_ref, dq_ref, grad_cross_ref, after_ref, qkv_ref, mix_ref, lse_ref, tok_ref, one_ref, norm_ref, _,
    branch_ref, dqkv_ref, grad_tok_ref, norm_grad_ref,
    attn_ref, grad_mix_ref, kt_ref, dk_ref, dv_ref,
):
    seq_len = len_ref[0]
    row_tiles = pl.cdiv(seq_len, ROWS)
    clear(branch_ref, dqkv_ref, grad_tok_ref, norm_grad_ref)

    def enter(rows, _):
        normed, scale = normalize(after_ref[rows, :])
        grad = nt(dq_ref[rows, :], one_ref[:, ONE_Q:ONE_NORM])
        norm_grad_ref[1:2, :] += col_sum(grad * normed)
        norm_grad_ref[3:4, :] += col_sum(grad)
        attn = grad_cross_ref[rows, :] + norm_backward(normed, scale, norm_ref[1:2, :], grad)
        attn_ref[rows, :] = attn
        branch = attn.astype(bf16)
        branch_ref[rows, :] = branch
        grad_mix_ref[rows, :] = nt(branch, one_ref[:, ONE_OUT:ONE_Q]).astype(bf16)

    each_tile(row_tiles, ROWS, enter)

    def per_pair(pair, carry):
        q_lanes, k_lanes, v_lanes = (lane_block(3 * pair + i) for i in range(3))
        clear(dk_ref, dv_ref)
        for tile in range(qkv_ref.shape[0] // TILE):

            @pl.when(tile * TILE < seq_len)
            def _():
                rows = slice(tile * TILE, (tile + 1) * TILE)
                size = (tile + 1) * TILE
                kt_ref[:, rows] = qkv_ref[rows, k_lanes].T
                queries = split_heads(qkv_ref[rows, q_lanes] * scale_of_heads())
                grad_mix = grad_mix_ref[rows, lane_block(pair)]
                grads = split_heads(grad_mix)
                inner = row_dots(mix_ref[rows, lane_block(pair)], grad_mix)
                scores = nt(qkv_ref[:size, k_lanes], queries)
                scores = jnp.where(seen(scores.shape, tile * TILE, seq_len), scores, neg_big)
                probs = jnp.exp(scores - lse_ref[pair, tile : tile + 1, :])
                dscores = (probs * (nt(qkv_ref[:size, v_lanes], grads) - inner)).astype(bf16)
                dv_ref[:size, :] += nn(probs.astype(bf16), grads)
                dk_ref[:size, :] += nn(dscores, queries)
                dq = nn(kt_ref[:, :size], dscores)
                dqkv_ref[rows, q_lanes] = join_heads(dq).astype(bf16) * scale_of_heads()

        dqkv_ref[:, k_lanes] = dk_ref[...].astype(bf16)
        dqkv_ref[:, v_lanes] = dv_ref[...].astype(bf16)
        return carry

    lax.fori_loop(0, PAIRS, per_pair, 0)

    def leave(rows, i):
        normed, scale = normalize(token_rows(tok_ref, i))
        grad = nt(dqkv_ref[rows, :], one_ref[:, :ONE_OUT])
        norm_grad_ref[0:1, :] += col_sum(grad * normed)
        norm_grad_ref[2:3, :] += col_sum(grad)
        total = attn_ref[rows, :] + norm_backward(normed, scale, norm_ref[0:1, :], grad)
        count = ROWS // grad_tok_ref.shape[1]
        grad_tok_ref[pl.ds(i * count, count)] = total.astype(bf16).reshape(count, -1, D)

    each_tile(row_tiles, ROWS, leave)


def run_self_backward(seq_len, dq, grad_cross, after, qkv, mix, lse, arrived, part, one, norm_rows, leaving, slot):
    blocks, size = arrived.shape[0], arrived.shape[1] // PARTS[part]
    at = part_at(part)
    rows = blocks * size
    fixed = lambda *dims: pl.BlockSpec(dims, lambda i: (0,) * len(dims), pipeline_mode=pl.Buffered(1))
    spec = lambda block: pl.BlockSpec(
        (blocks, size, D), lambda i: (0, block, 0), pipeline_mode=pl.Buffered(1)
    )
    before = [] if leaving is None else [leaving]
    body = self_part_backward
    if leaving is None:
        body = lambda *refs: self_part_backward(*refs[:10], None, *refs[10:])
    return pl.pallas_call(
        body,
        name="self_part_backward",
        grid=(1,),
        in_specs=[in_smem()]
        + [fixed(*a.shape) for a in (dq, grad_cross, after, qkv, mix, lse)]
        + [spec(at), fixed(*one.shape), fixed(8, D)]
        + [anywhere()] * len(before),
        out_specs=[fixed(rows, D), fixed(rows, 3 * D), spec(slot), fixed(8, D)],
        out_shape=[
            in_hbm(rows, D),
            in_hbm(rows, 3 * D),
            in_hbm(blocks, 2 * size, D),
            in_hbm(8, D, dtype=f32),
        ],
        input_output_aliases={10: 2} if before else {},
        scratch_shapes=[
            pltpu.VMEM((rows, D), f32),
            pltpu.VMEM((rows, D), bf16),
            pltpu.VMEM((PAIR, rows), bf16),
            pltpu.VMEM((rows, PAIR), f32),
            pltpu.VMEM((rows, PAIR), f32),
        ],
        compiler_params=pltpu.CompilerParams(vmem_limit_bytes=40 * MIB),
        cost_estimate=COST,
    )(seq_len, dq, grad_cross, after, qkv, mix, lse, arrived, one, norm_rows, *before)


def anywhere():
    return pl.BlockSpec(memory_space=pl.ANY)


def copy_kernel(plan, n_in, n_out, scalar_ref, *refs):
    ins, outs, sem = refs[:n_in], refs[n_in : n_in + n_out], refs[-1]
    for which, src, dst in plan(scalar_ref, ins, outs):
        pltpu.make_async_copy(src, dst, sem.at[which]).start()
    for which, out in enumerate(outs):
        pltpu.make_async_copy(out, out, sem.at[which]).wait()


def run_copies(name, plan, scalars, ins, out_shapes, stage="in"):
    vmem = pl.BlockSpec(memory_space=pltpu.VMEM)
    return pl.pallas_call(
        functools.partial(copy_kernel, plan, len(ins), len(out_shapes)),
        name=name,
        in_specs=[in_smem()] + [vmem if stage == "in" else anywhere()] * len(ins),
        out_specs=[vmem if stage == "out" else anywhere()] * len(out_shapes),
        out_shape=out_shapes,
        scratch_shapes=[pltpu.SemaphoreType.DMA((len(out_shapes),))],
        compiler_params=pltpu.CompilerParams(vmem_limit_bytes=16 * MIB),
        cost_estimate=pl.CostEstimate(flops=0, bytes_accessed=1000, transcendentals=0),
    )(scalars, *ins)


def device_bits():
    return [
        (axis, b)
        for axis in ("grp", "fsdp")
        for b in reversed(range(lax.axis_size(axis).bit_length() - 1))
    ]


def swap(array, axis, b):
    return lax.ppermute(array, axis, [(i, i ^ (1 << b)) for i in range(lax.axis_size(axis))])


def bit_mask(axis, b):
    return (1 << b) if axis == "fsdp" else lax.axis_size("fsdp") << b


def my_bit(axis, b):
    return (lax.axis_index(axis) >> b) & 1


class Gather:
    def __init__(self, name, shard, me, outs, pieces):
        self.name = name
        bits = device_bits()
        self.left = [p for p in bits if p[0] == "fsdp"] + [p for p in bits if p[0] == "grp"]
        self.masks = [0]
        self.value = shard[None]
        self.me = me
        self.outs = outs
        self.pieces = pieces
        self.got = None

    def send(self):
        self.got = swap(self.value, *self.left[0])

    def take(self):
        mask = bit_mask(*self.left.pop(0))
        masks = self.masks
        self.masks = masks + [mask ^ m for m in masks]
        k = len(masks)
        if self.left:

            def plan(_, ins, outs):
                return [(0, ins[0], outs[0].at[:k]), (0, ins[1], outs[0].at[k:])]

            shape = (2 * k,) + self.value.shape[1:]
            (self.value,) = run_copies(
                self.name + "_join", plan, self.me, [self.value, self.got], [in_hbm(*shape)]
            )
            return self.value

        def plan(me_ref, ins, outs):
            me = me_ref[0]
            return [
                (which, src, dst)
                for i in range(k)
                for half, src_ref in ((0, ins[0]), (k, ins[1]))
                for which, src, dst in self.pieces(src_ref.at[i], outs, me ^ self.masks[half + i])
            ]

        self.value = run_copies(
            self.name + "_order", plan, self.me, [self.value, self.got], self.outs
        )
        return self.value

    def step(self):
        self.send()
        return self.take()


def pack_shards(me, self_in, self_out, cross_q, norms, cross_kv, cross_out):
    rows = self_in.shape[0]

    def plan(_, ins, outs):
        w_in, w_out, w_q, w_norm, w_kv, w_cross = ins
        one, two = outs
        copies = []
        for pair in range(PAIRS):
            for o, w, parts in ((0, w_in, 3), (1, w_kv, 2)):
                for part in range(parts):
                    src = w.at[:, part * D + pair * PAIR : part * D + (pair + 1) * PAIR]
                    at = (parts * pair + part) * PAIR
                    copies.append((o, src, outs[o].at[:, at : at + PAIR]))
        copies.append((0, w_out, one.at[:, ONE_OUT:ONE_Q]))
        copies.append((0, w_q, one.at[:, ONE_Q:ONE_NORM]))
        copies.append((0, w_norm, one.at[:, ONE_NORM:]))
        copies.append((1, w_cross, two.at[:, TWO_OUT:]))
        return copies

    ins = [self_in, self_out, cross_q, norms, cross_kv, cross_out]
    shapes = [in_hbm(rows, ONE_COLS), in_hbm(rows, 3 * D)]
    return run_copies("pack_shards", plan, me, ins, shapes, "out")


def gather_rows(shard):
    return lax.all_gather(shard, ("grp", "fsdp"), axis=0, tiled=True)


def grad_kernel(
    full, len0_ref, len1_ref, bit_ref, left0_ref, right0_ref, left1_ref, right1_ref, *refs
):
    keep_ref, send_ref, flip_ref, acc_ref = refs[-4:]
    chunk, half, count = acc_ref.shape[0], acc_ref.shape[0] // 2, right0_ref.shape[0]
    sides = (
        (len0_ref[0], left0_ref, right0_ref, 0),
        (len1_ref[0], left1_ref, right1_ref, count),
    )
    tiles = [slice(k, k + ROWS) for k in range(0, count, ROWS)]

    @pl.when((pl.program_id(0) == 0) & (pl.program_id(1) == 0))
    def _():
        for seq_len, left_ref, _, at in sides:
            for tile in tiles:

                @pl.when(jnp.logical_or(full or tile.start == 0, tile.start < seq_len))
                def _():
                    if len(left_ref.shape) == 3:
                        size = left_ref.shape[1]
                        left = left_ref[tile.start // size : (tile.stop + size - 1) // size]
                        skip = tile.start % size
                        left = left.reshape(-1, D)[skip : skip + ROWS]
                    else:
                        left = left_ref[tile, :]
                    flip_ref[:, at + tile.start : at + tile.stop] = left.T

    mine = pl.ds(pl.multiple_of(pl.program_id(0) * chunk, chunk), chunk)
    if full:
        acc_ref[...] = nn(flip_ref[mine, :count], right0_ref[...]) + nn(
            flip_ref[mine, count:], right1_ref[...]
        )
    else:
        acc_ref[...] = nn(flip_ref[mine, :ROWS], right0_ref[:ROWS, :]) + nn(
            flip_ref[mine, count : count + ROWS], right1_ref[:ROWS, :]
        )
        for seq_len, _, right_ref, at in sides:
            for tile in tiles[1:]:

                @pl.when(tile.start < seq_len)
                def _():
                    acc_ref[...] += nn(flip_ref[mine, at + tile.start : at + tile.stop], right_ref[tile, :])

    bit = bit_ref[0]
    keep_ref[0] = acc_ref[pl.ds(pl.multiple_of(bit * half, half), half), :].astype(bf16)
    send_ref[0] = acc_ref[pl.ds(pl.multiple_of((1 - bit) * half, half), half), :].astype(bf16)


def run_grad(name, lens, pairs, cols, at, before=(), full=False, left_at=0):
    (left0, right0), (left1, right1) = pairs
    count, wide = right0.shape
    tall = D
    n_grp = lax.axis_size("grp")
    chunk = 2 * tall // n_grp
    if left0.ndim == 3:
        left_spec = pl.BlockSpec(
            (left0.shape[0], 3 * left0.shape[1] // 4, D), lambda m, n: (0, 0, 0), pipeline_mode=pl.Buffered(1)
        )
    else:
        left_spec = pl.BlockSpec((count, tall), lambda m, n: (0, left_at), pipeline_mode=pl.Buffered(1))
    right_spec = pl.BlockSpec((count, D), lambda m, n: (0, n))
    out_spec = pl.BlockSpec((1, chunk // 2, D), lambda m, n: (m, 0, n + at))
    shape = in_hbm(n_grp // 2, chunk // 2, cols)
    bit = my_bit("grp", 0).reshape(1)
    return pl.pallas_call(
        functools.partial(grad_kernel, full),
        name=name,
        grid=(n_grp // 2, wide // D),
        in_specs=[in_smem()] * 3
        + [left_spec, right_spec, left_spec, right_spec]
        + [anywhere()] * len(before),
        out_specs=[out_spec, out_spec],
        out_shape=[shape, shape],
        input_output_aliases={7: 0, 8: 1} if before else {},
        scratch_shapes=[pltpu.VMEM((tall, 2 * count), bf16), pltpu.VMEM((chunk, D), f32)],
        compiler_params=pltpu.CompilerParams(vmem_limit_bytes=48 * MIB),
        cost_estimate=COST,
    )(*lens, bit, left0, right0, left1, right1, *before)


def add_split_kernel(me_ref, kept_ref, got_ref, keep_ref, send_ref):
    for out_ref, half in ((keep_ref, me_ref[0]), (send_ref, 1 - me_ref[0])):
        total = kept_ref[0, half].astype(f32) + got_ref[0, half].astype(f32)
        out_ref[0] = total.astype(out_ref.dtype)


def add_kernel(kept_ref, got_ref, out_ref):
    out_ref[...] = kept_ref[...].astype(f32) + got_ref[...].astype(f32)


class Scatter:
    def __init__(self, name, keep, send):
        self.name = name
        self.held = device_bits()
        self.order = [p for p in reversed(self.held) if p[0] == "grp"]
        self.order += [p for p in reversed(self.held) if p[0] == "fsdp"]
        self.split()
        blocks = 1 << len(self.held)
        self.keep, self.send = (a.reshape(blocks, -1, a.shape[-1]) for a in (keep, send))
        self.block = self.keep.shape[1:]

    def split(self):
        self.bit = self.order.pop(0)
        dim = self.held.index(self.bit)
        self.held.remove(self.bit)
        return 1 << dim, 1 << (len(self.held) - dim)

    def step(self):
        got = swap(self.send, *self.bit)
        if not self.order:
            spec = pl.BlockSpec((1,) + self.block, lambda i: (0, 0, 0))
            return pl.pallas_call(
                add_kernel,
                name=self.name + "_sum",
                grid=(1,),
                in_specs=[spec, spec],
                out_specs=spec,
                out_shape=shape_of(1, *self.block, dtype=f32),
                compiler_params=pltpu.CompilerParams(vmem_limit_bytes=8 * MIB),
                cost_estimate=COST,
            )(self.keep, got).reshape(self.block)
        before, after = self.split()
        half = self.keep.shape[0] // 2
        view = (before, 2, after) + self.block
        some = min(after, 4)
        in_spec = pl.BlockSpec((1, 2, some) + self.block, lambda i, j, _: (i, 0, j, 0, 0))
        out_spec = pl.BlockSpec((1, some) + self.block, lambda i, j, _: (i, j, 0, 0))
        shape = shape_of(before, after, *self.block, dtype=self.keep.dtype)
        keep, send = pl.pallas_call(
            add_split_kernel,
            name=self.name + "_add",
            grid_spec=pltpu.PrefetchScalarGridSpec(
                num_scalar_prefetch=1,
                grid=(before, after // some),
                in_specs=[in_spec, in_spec],
                out_specs=[out_spec, out_spec],
            ),
            out_shape=[shape, shape],
            compiler_params=pltpu.CompilerParams(vmem_limit_bytes=16 * MIB),
            cost_estimate=COST,
        )(my_bit(*self.bit).reshape(1), self.keep.reshape(view), got.reshape(view))
        self.keep, self.send = (a.reshape((half,) + self.block) for a in (keep, send))

    def finish(self):
        while True:
            done = self.step()
            if done is not None:
                return done


def fence(*values):
    return lax.optimization_barrier(values)


def by_part(weight, parts):
    rows = weight.shape[0]
    return weight.reshape(rows, PAIRS, parts, PAIR).swapaxes(1, 2).reshape(rows, parts * D)


def rows_of(array):
    return array.reshape(-1, array.shape[-1])


def exchange(array):
    return lax.all_to_all(array, "fsdp", split_axis=0, concat_axis=0, tiled=True)


def shards(
    tokens,
    frames,
    lengths,
    cotangent,
    self_in,
    self_out,
    cross_q,
    cross_kv,
    cross_out,
    fc_in,
    fc_out,
    norm_gain,
    norm_bias,
):
    fsdp_count = lax.axis_size("fsdp")
    n_all = lax.axis_size("grp") * fsdp_count
    group_seqs, size = tokens.shape[:2]
    seq_ids = jnp.arange(group_seqs, dtype=jnp.int32)
    rank_order = jnp.argsort(-(lengths * group_seqs + (group_seqs - 1 - seq_ids)))
    sender = jnp.concatenate([rank_order[:fsdp_count], rank_order[fsdp_count:][::-1]])
    device = lax.axis_index("fsdp")
    len0, len1 = (
        lax.dynamic_slice_in_dim(lengths[sender], s * fsdp_count + device, 1) for s in range(2)
    )
    rows = self_in.shape[0]
    me = (lax.axis_index("grp") * fsdp_count + device).reshape(1)

    def pick(name, *parts):
        total = sum(array.shape[1] for array, _ in parts)

        def plan(seq_ref, ins, outs):
            copies, at = [], 0
            for src, (array, slot) in zip(ins, parts):
                span = slice(at, at + array.shape[1])
                at += array.shape[1]
                for j in range(fsdp_count):
                    seq = seq_ref[slot * fsdp_count + j]
                    copies.append((0, src.at[seq], outs[0].at[j, span]))
            return copies

        shape = in_hbm(fsdp_count, total, D)
        return run_copies(name, plan, sender, [array for array, _ in parts], [shape], "out")[0]

    def put_back(name, *parts):
        ins = []
        for first, _, second, _ in parts:
            ins += [a for a in (first, second) if not any(a is b for b in ins)]
        where = [[next(i for i, a in enumerate(ins) if a is p[k]) for k in (0, 2)] for p in parts]

        def plan(seq_ref, in_refs, outs):
            return [
                (o, in_refs[where[o][slot]].at[j, part[2 * slot + 1]], outs[o].at[seq_ref[slot * fsdp_count + j]])
                for o, part in enumerate(parts)
                for slot in range(2)
                for j in range(fsdp_count)
            ]

        shapes = [in_hbm(group_seqs, p[1].stop - p[1].start, D) for p in parts]
        return run_copies(name, plan, sender, ins, shapes)

    norms = jnp.pad(jnp.concatenate([norm_gain, norm_bias], axis=1), ((0, 0), (0, 120)))
    shard_one, shard_two = pack_shards(me, self_in, self_out, cross_q, norms, cross_kv, cross_out)
    w_two = gather_rows(shard_two)
    fc_up = fc_in.reshape(rows, n_all, FF_PARTS, rows).swapaxes(1, 2).reshape(rows, FF)
    fc_down = fc_out.reshape(FF_PARTS, rows, D).swapaxes(0, 1).reshape(rows, FF)
    w_fc = gather_rows(jnp.concatenate([fc_up, fc_down], axis=1))
    one = Gather(
        "one", shard_one, me, [in_hbm(n_all, rows, ONE_COLS)],
        lambda src, outs, b: [(0, src, outs[0].at[b])],
    )

    pick_a = pick("pick_first", (frames, 0), (tokens, 0))
    for _ in range(sum(1 for axis, _ in device_bits() if axis == "fsdp") - 1):
        one.step()
    (one.value, pick_a) = fence(one.value, pick_a)
    in_a = exchange(pick_a)
    pick_b = pick("pick_second", (tokens, 1), (cotangent, 0))
    pick_c = pick("pick_third", (frames, 1), (cotangent, 1))
    while len(one.left) > 1:
        one.step()
    (w_one,) = one.step()
    (in_a, w_one, pick_b, pick_c) = fence(in_a, w_one, pick_b, pick_c)
    w_one = rows_of(w_one)
    norm_rows = w_one[:, ONE_NORM : ONE_NORM + 8].T.astype(f32)

    in_b = exchange(pick_b)
    fwd0 = run_self_forward(len0, in_a, "tokens", w_one, norm_rows)
    crs0 = run_cross_forward(len0, in_a, w_two, fwd0[6])
    (in_b, fwd0, crs0, pick_c) = fence(in_b, fwd0, crs0, pick_c)

    in_c = exchange(pick_c)
    fwd1 = run_self_forward(len1, in_b, "first", w_one, norm_rows)
    mid0 = run_middle(len0, crs0[0], fwd0[4], in_b, "second", w_two, w_fc, norm_rows)
    cb0 = run_cross_backward(len0, fwd0[6], crs0[2], crs0[0], mid0[7], crs0[1], w_two, mid0[0])
    (in_c, crs0, cb0, fwd1, mid0) = fence(in_c, crs0, cb0, fwd1, mid0)

    lens = (len0, len1)

    back_a = exchange(cb0[2])
    crs1 = run_cross_forward(len1, in_c, w_two, fwd1[6])
    mid1 = run_middle(len1, crs1[0], fwd1[4], in_c, "tokens", w_two, w_fc, norm_rows)
    (crs1, mid1, mid0) = fence(crs1, mid1, mid0)
    g_up = Scatter(
        "up", *run_grad("grad_fc_in", lens, ((mid0[1], mid0[3]), (mid1[1], mid1[3])), FF, 0)
    )
    halves = ()
    for j in range(FF_PARTS):
        halves = run_grad("grad_fc_out", lens, ((mid0[2], mid0[4]), (mid1[2], mid1[4])), FF, j, halves, left_at=j)
    g_down = Scatter("down", *halves)
    g_up.step()
    g_down.step()
    (crs1, mid1, g_down.keep, g_down.send, g_up.keep, g_up.send) = fence(
        crs1, mid1, g_down.keep, g_down.send, g_up.keep, g_up.send
    )
    cb1 = run_cross_backward(len1, fwd1[6], crs1[2], crs1[0], mid1[7], crs1[1], w_two, mid1[0])
    g_down.step()
    g_up.step()
    (back_a, cb0, cb1, mid0, mid1, g_down.keep, g_down.send, g_up.keep, g_up.send) = fence(
        back_a, cb0, cb1, mid0, mid1, g_down.keep, g_down.send, g_up.keep, g_up.send
    )

    back_b = exchange(cb1[2])
    halves = run_grad("grad_cross_kv", lens, ((in_a, cb0[1]), (in_c, cb1[1])), 3 * D, 0, full=True)
    halves = run_grad(
        "grad_cross_out", lens, ((crs0[0], mid0[5]), (crs1[0], mid1[5])), 3 * D, 2, halves
    )
    g_two = Scatter("two", *halves)
    g_two.step()
    sb0 = run_self_backward(
        len0, cb0[0], mid0[6], fwd0[4], fwd0[0], fwd0[2], fwd0[3], in_a, "tokens", w_one, norm_rows, None, 0
    )
    sb1 = run_self_backward(
        len1, cb1[0], mid1[6], fwd1[4], fwd1[0], fwd1[2], fwd1[3], in_b, "first", w_one, norm_rows, sb0[2], 1
    )
    halves = run_grad("grad_self_in", lens, ((fwd0[1], sb0[1]), (fwd1[1], sb1[1])), 5 * D, 0)
    halves = run_grad("grad_self_out", lens, ((fwd0[2], sb0[0]), (fwd1[2], sb1[0])), 5 * D, 3, halves)
    halves = run_grad("grad_cross_q", lens, ((fwd0[5], cb0[0]), (fwd1[5], cb1[0])), 5 * D, 4, halves)
    g_one = Scatter("one", *halves)
    g_one.step()
    g_down.step()
    g_up.step()
    every = (back_b, sb0, sb1, g_one.keep, g_one.send, g_two.keep, g_two.send)
    every += (g_down.keep, g_down.send, g_up.keep, g_up.send)
    (back_b, sb0, sb1, g_one.keep, g_one.send, g_two.keep, g_two.send, *rest) = fence(*every)
    (g_down.keep, g_down.send, g_up.keep, g_up.send) = rest

    back_c = exchange(sb1[2])
    ng_self = sb0[3] + sb1[3]
    ng_mid = mid0[8] + mid1[8]
    norm_sum = jnp.concatenate([ng_self[:2], ng_mid[:2], ng_self[2:4], ng_mid[2:4]], axis=0)
    by_device = norm_sum.reshape(8, n_all, rows).swapaxes(0, 1).reshape(-1, 2, fsdp_count, 8 * rows)
    core = my_bit("grp", 0)
    g_norm = Scatter(
        "norms",
        *(
            lax.dynamic_index_in_dim(by_device, c, 1, keepdims=False).reshape(-1, 1, 8 * rows)
            for c in (core, 1 - core)
        ),
    )
    grad_frames, output = put_back(
        "put_frames",
        (back_a, slice(0, 3 * size), back_b, slice(0, 3 * size)),
        (back_a, slice(3 * size, 4 * size), back_b, slice(3 * size, 4 * size)),
    )
    g_one = g_one.finish()
    g_two = g_two.finish()
    g_down = g_down.finish()
    g_up = g_up.finish()
    g_norm = g_norm.finish().reshape(8, rows).T
    (grad_tokens,) = put_back("put_tokens", (back_c, slice(0, size), back_c, slice(size, 2 * size)))
    return (
        output,
        grad_tokens,
        grad_frames,
        by_part(g_one[:, :ONE_OUT], 3),
        g_one[:, ONE_OUT:ONE_Q],
        g_one[:, ONE_Q:],
        by_part(g_two[:, :TWO_OUT], 2),
        g_two[:, TWO_OUT:],
        g_up.reshape(rows, FF_PARTS, n_all, rows).swapaxes(1, 2).reshape(rows, FF),
        g_down.reshape(rows, FF_PARTS, D).swapaxes(0, 1).reshape(FF_PARTS * rows, D),
        g_norm[:, :4],
        g_norm[:, 4:],
    )


def solution(mesh):
    rows = P(("grp", "fsdp"), None)
    seqs = P("grp", "fsdp", None)
    return jax.shard_map(
        shards,
        mesh=mesh,
        in_specs=(seqs, seqs, P("grp"), seqs) + (rows,) * 9,
        out_specs=(seqs,) * 3 + (rows,) * 9,
        check_vma=False,
    )
```

time: 1040 us -> 790 us (0.76)
  matrix products: 220 us -> 0 us
  Pallas kernels: 146 us -> 365 us
  waiting for transfers between devices: 402 us -> 192 us
  other arithmetic: 60.8 us -> 4.31 us
  starting transfers between devices: 104 us -> 119 us
    dot_general x42 -> x0, matrix products: 220 us -> none  [the longest x14 88.6 us: dot(): return jnp.dot(left, right, preferred_element_type=f32)]
    pallas_call x8 -> x56, Pallas kernels: 146 us -> 365 us  [the longest x10 74.9 us: run_grad(): pl.pallas_call(functools.partial(grad_kernel, full), name=name, grid=(n_g...]
    all_to_all x12 -> x6, waiting for transfers between devices: 210 us -> 0.02 us  [exchange(): lax.all_to_all(array, 'fsdp', split_axis=0, concat_axis=0, tiled=True)]
    ppermute x25 -> x30, waiting for transfers between devices: 106 us -> 192 us  [swap(): lax.ppermute(array, axis, [(i, i ^ 1 << b) for i in range(lax.axis_size(a...]
    all_gather x8 -> x2, waiting for transfers between devices: 84 us -> 0.01 us  [gather_rows(): return lax.all_gather(shard, ('grp', 'fsdp'), axis=0, tiled=True)]
    unnamed x240 -> x201, local copies, waits for them, and re-layouts: 10.2 us -> 56.1 us
    convert_element_type x22 -> x1, other arithmetic: 28.2 us -> 0.01 us  [shards(): norm_rows = w_one[:, ONE_NORM:ONE_NORM + 8].T.astype(f32)]
    gather x10 -> x0, local copies, waits for them, and re-layouts: 28.2 us -> none  [the longest x6 18.1 us: bring(): picked = array[sender[slot * fsdp_count:(slot + 1) * fsdp_count]]]
  transfers between devices with their start and end apart: 45 -> 38, of which waited for: 22 -> 16; matrix products, arithmetic and copies ran while one was open for 20% -> 5% of each run, Pallas kernels for 2% -> 47%
where the time goes in v2:
time: 790 us; the launch traced here: 777 us
  Pallas kernels  365 us (46%)
  waiting for transfers between devices  192 us (24%)
  starting transfers between devices  119 us (15%)
  local copies, waits for them, and re-layouts  81.6 us (10%)
  between operations  15.3 us (2%)
    ppermute x30, waiting for transfers between devices, swap(): lax.ppermute(array, axis, [(i, i ^ 1 << b) for i in range(lax.axis_size(a...  192 us
    pallas_call x10, Pallas kernels, run_grad(): pl.pallas_call(functools.partial(grad_kernel, full), name=name, grid=(n_g...  74.9 us
    pallas_call x2, Pallas kernels, run_cross_backward(): pl.pallas_call(cross_backward_kernel, name='cross_backward', grid=(PAIRS,...  74 us
    all_to_all x6, starting transfers between devices, exchange(): lax.all_to_all(array, 'fsdp', split_axis=0, concat_axis=0, tiled=True)  70.1 us
    unnamed x201, local copies, waits for them, and re-layouts  56.1 us
    pallas_call x2, Pallas kernels, run_cross_forward(): pl.pallas_call(cross_forward_kernel, name='cross_forward', grid=(PAIRS,),...  51 us
    ppermute x30, starting transfers between devices, swap(): lax.ppermute(array, axis, [(i, i ^ 1 << b) for i in range(lax.axis_size(a...  49.2 us
    pallas_call x2, Pallas kernels, run_middle(): pl.pallas_call(middle_kernel, name='mlp_and_back', grid=(rows // ROWS,),...  42.2 us
  transfers between devices with their start and end apart: 38, of which 16 were waited for; matrix products, arithmetic and copies ran while one was open for 5% of the time, Pallas kernels for 47%

profile of v2, /device:TPU:0, one launch (start us, length us, event | category | flops | bytes accessed | tf_op | source)
XLA Modules:
  0.0 777.1 jit_solution(7797546810915231945)
XLA Ops:
  19.6 4.1 collective-permute-start
  23.7 10.3 %collective-permute-done.refs_1_ = bf16[1,24,3968]{2,1,0:T(8,128)(2,1)S(1)} collective-permute-done((bf16[1,24,3968]{2,1,0:T(8,128)(2,1)S(1)}, bf16[1,24,3968]{2,1,0:T(8,128)(2,1)S(1)}, u32[]{:S(2)}, u32[]{:S(2)}) %collective-permute-start) | collective-permute-done | bytes 190496 | tf_op jit(solution)/shard_map/ppermute | solution.py:590
  39.7 3.7 pick_first.1
  46.6 7.7 all-to-all-start
  56.4 54.8 %collective-permute-done.2.refs_1_ = bf16[4,24,3968]{2,1,0:T(8,128)(2,1)S(1)} collective-permute-done((bf16[4,24,3968]{2,1,0:T(8,128)(2,1)}, bf16[4,24,3968]{2,1,0:T(8,128)(2,1)S(1)}, u32[]{:S(2)}, u32[]{:S(2)}) %collective-permute-start.2) | collective-permute-done | bytes 761888 | tf_op jit(solution)/shard_map/ppermute | solution.py:590
  115.1 30.5 %collective-permute-done.3.refs_1_ = bf16[8,24,3968]{2,1,0:T(8,128)(2,1)S(1)} collective-permute-done((bf16[8,24,3968]{2,1,0:T(8,128)(2,1)}, bf16[8,24,3968]{2,1,0:T(8,128)(2,1)S(1)}, u32[]{:S(2)}, u32[]{:S(2)}) %collective-permute-start.3) | collective-permute-done | bytes 1523744 | tf_op jit(solution)/shard_map/ppermute | solution.py:590
  151.3 3.8 pick_third.1
  155.1 3.7 pick_second.1
  161.5 8.7 %all-to-all-start.1 = ((bf16[8,128,768]{2,1,0:T(8,128)(2,1)}), bf16[8,128,768]{2,1,0:T(8,128)(2,1)}, u32[]{:S(2)}, u32[]{:S(2)}) async-start(bf16[8,128,768]{2,1,0:T(8,128)(2,1)} %pick_second.1), calls=%async_computation.1 | async-start | bytes 3145728 | tf_op jit(solution)/shard_map/all_to_all | solution.py:843
  175.4 21.9 %self_part_forward.2 = (bf16[512,2304]{1,0:T(8,128)(2,1)}, bf16[512,768]{1,0:T(8,128)(2,1)}, bf16[512,768]{1,0:T(8,128)(2,1)}, f32[6,4,256]{2,1,0:T(4,128)}, f32...) custom-call(s32[1]{0:T(128)} %get-tuple-element.449.len_ref.len0_ref.refs_0_, ...), custom_call_target="tpu_custom_call" | custom-call | flops 1000000 | bytes 1000000 | tf_op jit(solution)/shard_map/self_part_forward/pallas_call | solution.py:198
  200.5 34.5 %cross_forward.2 = (bf16[512,768]{1,0:T(8,128)(2,1)}, f32[6,4,256]{2,1,0:T(4,128)}, bf16[1536,1536]{1,0:T(8,128)(2,1)}) custom-call(s32[1]{0:T(128)} %get-tuple-element.449.len_ref.len0_ref.refs_0_, bf16[8,256,768]{2,1,0:T(8,128)(2,1)S(1)} %all-to-all-done.tok_ref.frm_ref.refs_7_.left0_ref, bf16[768,2304]{1,0:T(8,128)(2,1)S(1)} %copy-done.2, ...), custom_call_target="tpu_custom_call" | custom-call | flops 1000000 | bytes 1000000 | tf_op jit(solution)/shard_map/cross_forward/pallas_call | solution.py:249
  235.0 4.5 all-to-all-start.2
  242.2 10.5 %self_part_forward.3 = (bf16[512,2304]{1,0:T(8,128)(2,1)}, bf16[512,768]{1,0:T(8,128)(2,1)}, bf16[512,768]{1,0:T(8,128)(2,1)}, f32[6,4,256]{2,1,0:T(4,128)}, f32...) custom-call(s32[1]{0:T(128)} %get-tuple-element.448.len_ref.len1_ref, ...), custom_call_target="tpu_custom_call" | custom-call | flops 1000000 | bytes 1000000 | tf_op jit(solution)/shard_map/self_part_forward/pallas_call | solution.py:198
  252.8 23.9 %mlp_and_back.2 = (bf16[8,256,768]{2,1,0:T(8,128)(2,1)}, bf16[512,768]{1,0:T(8,128)(2,1)}, bf16[512,3072]{1,0:T(8,128)(2,1)}, bf16[512,3072]{1,0:T(8,128)(2,1)},...) custom-call(s32[1]{0:T(128)} %get-tuple-element.449.len_ref.len0_ref, ...), custom_call_target="tpu_custom_call" | custom-call | flops 1000000 | bytes 1000000 | tf_op jit(solution)/shard_map/mlp_and_back/pallas_call | solution.py:431
  276.7 3.9 copy.76._
  283.6 51.9 %cross_backward.2 = (bf16[512,768]{1,0:T(8,128)(2,1)}, bf16[1536,1536]{1,0:T(8,128)(2,1)}, bf16[8,256,768]{2,1,0:T(8,128)(2,1)}) custom-call(s32[1]{0:T(128)} %get-tuple-element.449.len_ref.len0_ref.refs_0_, bf16[512,768]{1,0:T(8,128)(2,1)S(1)} %copy-done.42, bf16[1536,1536]{1,0:T(8,128)(2,1)S(1)} %copy-done.31, ...), custom_call_target="tpu_custom_call", output_to_operand_aliasing={{2}: (7, {})} | custom-call | flops 1000000 | bytes 1000000 | tf_op jit(solution)/shard_map/cross_backward/pallas_call | solution.py:327
  335.6 4.7 all-to-all-start.3
  341.4 16.5 %cross_forward.3 = (bf16[512,768]{1,0:T(8,128)(2,1)}, f32[6,4,256]{2,1,0:T(4,128)}, bf16[1536,1536]{1,0:T(8,128)(2,1)}) custom-call(s32[1]{0:T(128)} %get-tuple-element.448.len_ref.len1_ref, bf16[8,256,768]{2,1,0:T(8,128)(2,1)} %all-to-all-done.2.frm_ref.cot_ref.left1_ref, bf16[768,2304]{1,0:T(8,128)(2,1)S(1)} %copy-done.3, bf16[512,768]{1,0:T(8,128)(2,1)S(1)} %copy-done.39), custom_call_target="tpu_custom_call" | custom-call | flops 1000000 | bytes 1000000 | tf_op jit(solution)/shard_map/cross_forward/pallas_call | solution.py:249
  359.0 18.3 %mlp_and_back.3 = (bf16[8,256,768]{2,1,0:T(8,128)(2,1)}, bf16[512,768]{1,0:T(8,128)(2,1)}, bf16[512,3072]{1,0:T(8,128)(2,1)}, bf16[512,3072]{1,0:T(8,128)(2,1)},...) custom-call(s32[1]{0:T(128)} %get-tuple-element.448.len_ref.len1_ref, ...), custom_call_target="tpu_custom_call" | custom-call | flops 1000000 | bytes 1000000 | tf_op jit(solution)/shard_map/mlp_and_back/pallas_call | solution.py:431
  378.5 12.9 %grad_fc_in.1 = (bf16[2,192,3072]{2,1,0:T(8,128)(2,1)}, bf16[2,192,3072]{2,1,0:T(8,128)(2,1)}) custom-call(s32[1]{0:T(128)} %get-tuple-element.449.len_ref.len0_ref.refs_0_, s32[1]{0:T(128)} %get-tuple-element.448.len_ref.len1_ref, s32[1]{0:T(128)} %bitcast.11.bit_ref, bf16[512,768]{1,0:T(8,128)(2,1)S(1)} %copy-done.59, bf16[512,3072]{1,0:T(8,128)(2,1)S(1)} %copy-done.38, ...), custom_call_target="tpu_custom_call" | custom-call | flops 1000000 | bytes 1000000 | tf_op jit(solution)/shard_map/grad_fc_in/pallas_call | solution.py:743
  391.7 5.6 grad_fc_out.4
  397.3 6.0 grad_fc_out.5
  403.3 5.5 grad_fc_out.6
  408.8 5.7 grad_fc_out.7
  422.2 3.7 collective-permute-start.8
  425.9 3.9 copy.83._
  432.9 22.1 %cross_backward.3 = (bf16[512,768]{1,0:T(8,128)(2,1)}, bf16[1536,1536]{1,0:T(8,128)(2,1)}, bf16[8,256,768]{2,1,0:T(8,128)(2,1)}) custom-call(s32[1]{0:T(128)} %get-tuple-element.448.len_ref.len1_ref, bf16[512,768]{1,0:T(8,128)(2,1)S(1)} %copy-done.40, bf16[1536,1536]{1,0:T(8,128)(2,1)S(1)} %copy-done.30, ...), custom_call_target="tpu_custom_call", output_to_operand_aliasing={{2}: (7, {})} | custom-call | flops 1000000 | bytes 1000000 | tf_op jit(solution)/shard_map/cross_backward/pallas_call | solution.py:327
  459.2 18.4 %collective-permute-done.7 = bf16[8,24,3072]{2,1,0:T(8,128)(2,1)S(1)} collective-permute-done((bf16[8,24,3072]{2,1,0:T(8,128)(2,1)}, bf16[8,24,3072]{2,1,0:T(8,128)(2,1)S(1)}, u32[]{:S(2)}, u32[]{:S(2)}) %collective-permute-start.7) | collective-permute-done | bytes 1179680 | tf_op jit(solution)/shard_map/ppermute | solution.py:590
  479.9 29.8 %all-to-all-start.4 = ((bf16[8,256,768]{2,1,0:T(8,128)(2,1)}), bf16[8,256,768]{2,1,0:T(8,128)(2,1)}, u32[]{:S(2)}, u32[]{:S(2)}) async-start(bf16[8,256,768]{2,1,0:T(8,128)(2,1)} %get-tuple-element.348), calls=%async_computation.4 | async-start | bytes 6291456 | tf_op jit(solution)/shard_map/all_to_all | solution.py:843
  516.6 24.4 %self_part_backward.2 = (bf16[512,768]{1,0:T(8,128)(2,1)}, bf16[512,2304]{1,0:T(8,128)(2,1)}, bf16[8,128,768]{2,1,0:T(8,128)(2,1)}, f32[8,768]{1,0:T(8,128)}) custom-call(s32[1]{0:T(128)} %get-tuple-element.449.len_ref.len0_ref.refs_0_, bf16[512,768]{1,0:T(8,128)(2,1)S(1)} %copy-done.35, f32[512,768]{1,0:T(8,128)S(1)} %copy-done.48, ...), custom_call_target="tpu_custom_call" | custom-call | flops 1000000 | bytes 1000000 | tf_op jit(solution)/shard_map/self_part_backward/pallas_call | solution.py:527
  543.9 12.0 %self_part_backward.3 = (bf16[512,768]{1,0:T(8,128)(2,1)}, bf16[512,2304]{1,0:T(8,128)(2,1)}, bf16[8,128,768]{2,1,0:T(8,128)(2,1)}, f32[8,768]{1,0:T(8,128)}) custom-call(s32[1]{0:T(128)} %get-tuple-element.448.len_ref.len1_ref, bf16[512,768]{1,0:T(8,128)(2,1)S(1)} %copy-done.37, f32[512,768]{1,0:T(8,128)S(1)} %copy-done.49, ...), custom_call_target="tpu_custom_call", output_to_operand_aliasing={{2}: (10, {})} | custom-call | flops 1000000 | bytes 1000000 | tf_op jit(solution)/shard_map/self_part_backward/pallas_call | solution.py:527
  556.0 10.5 %grad_self_in.1 = (bf16[2,192,3840]{2,1,0:T(8,128)(2,1)}, bf16[2,192,3840]{2,1,0:T(8,128)(2,1)}) custom-call(s32[1]{0:T(128)} %get-tuple-element.449.len_ref.len0_ref.refs_0_, s32[1]{0:T(128)} %get-tuple-element.448.len_ref.len1_ref, s32[1]{0:T(128)} %bitcast.11.bit_ref, bf16[512,768]{1,0:T(8,128)(2,1)S(1)} %copy-done.64, bf16[512,2304]{1,0:T(8,128)(2,1)S(1)} %copy-done.45, ...), custom_call_target="tpu_custom_call" | custom-call | flops 1000000 | bytes 1000000 | tf_op jit(solution)/shard_map/grad_self_in/pallas_call | solution.py:743
  566.5 4.5 grad_self_out.1
  571.1 4.4 grad_cross_q.1
  576.6 15.6 %grad_cross_kv.1 = (bf16[2,192,2304]{2,1,0:T(8,128)(2,1)}, bf16[2,192,2304]{2,1,0:T(8,128)(2,1)}) custom-call(s32[1]{0:T(128)} %get-tuple-element.449.len_ref.len0_ref.refs_0_, s32[1]{0:T(128)} %get-tuple-element.448.len_ref.len1_ref, s32[1]{0:T(128)} %bitcast.11.bit_ref, bf16[8,256,768]{2,1,0:T(8,128)(2,1)S(1)} %copy-done.6, ...), custom_call_target="tpu_custom_call" | custom-call | flops 1000000 | bytes 1000000 | tf_op jit(solution)/shard_map/grad_cross_kv/pallas_call | solution.py:743
  592.2 4.3 grad_cross_out.1
  598.8 14.4 %collective-permute-done.12 = bf16[4,24,3072]{2,1,0:T(8,128)(2,1)} collective-permute-done((bf16[4,24,3072]{2,1,0:T(8,128)(2,1)}, bf16[4,24,3072]{2,1,0:T(8,128)(2,1)}, u32[]{:S(2)}, u32[]{:S(2)}) %collective-permute-start.12) | collective-permute-done | bytes 589856 | tf_op jit(solution)/shard_map/ppermute | solution.py:590
  616.9 8.4 %collective-permute-done.11 = bf16[4,24,3072]{2,1,0:T(8,128)(2,1)} collective-permute-done((bf16[4,24,3072]{2,1,0:T(8,128)(2,1)}, bf16[4,24,3072]{2,1,0:T(8,128)(2,1)}, u32[]{:S(2)}, u32[]{:S(2)}) %collective-permute-start.11) | collective-permute-done | bytes 589856 | tf_op jit(solution)/shard_map/ppermute | solution.py:590
  635.6 14.7 %all-to-all-start.5 = ((bf16[8,128,768]{2,1,0:T(8,128)(2,1)}), bf16[8,128,768]{2,1,0:T(8,128)(2,1)S(1)}, u32[]{:S(2)}, u32[]{:S(2)}) async-start(bf16[8,128,768]{2,1,0:T(8,128)(2,1)} %get-tuple-element.400), calls=%async_computation.5 | async-start | bytes 3145728 | tf_op jit(solution)/shard_map/all_to_all | solution.py:843
  650.7 18.8 %collective-permute-done.13 = bf16[8,24,3840]{2,1,0:T(8,128)(2,1)} collective-permute-done((bf16[8,24,3840]{2,1,0:T(8,128)(2,1)}, bf16[8,24,3840]{2,1,0:T(8,128)(2,1)}, u32[]{:S(2)}, u32[]{:S(2)}) %collective-permute-start.13) | collective-permute-done | bytes 1474592 | tf_op jit(solution)/shard_map/ppermute | solution.py:590
  674.7 12.2 %collective-permute-done.17 = bf16[8,24,2304]{2,1,0:T(8,128)(2,1)S(1)} collective-permute-done((bf16[8,24,2304]{2,1,0:T(8,128)(2,1)}, bf16[8,24,2304]{2,1,0:T(8,128)(2,1)S(1)}, u32[]{:S(2)}, u32[]{:S(2)}) %collective-permute-start.17) | collective-permute-done | bytes 884768 | tf_op jit(solution)/shard_map/ppermute | solution.py:590
  690.0 4.2 collective-permute-start.23
  702.1 4.6 collective-permute-start.19
  719.6 7.1 collective-permute-start.29
  726.7 5.5 put_frames.1
  743.5 8.4 %collective-permute-done.24.got_ref = bf16[1,24,3072]{2,1,0:T(8,128)(2,1)S(1)} collective-permute-done((bf16[1,24,3072]{2,1,0:T(8,128)(2,1)S(1)}, bf16[1,24,3072]{2,1,0:T(8,128)(2,1)S(1)}, u32[]{:S(2)}, u32[]{:S(2)}) %collective-permute-start.24) | collective-permute-done | bytes 147488 | tf_op jit(solution)/shard_map/ppermute | solution.py:590
  757.4 3.8 copy.69
  761.2 4.0 reshape.464
  (336 shorter events, 148.4 us)
Async XLA Ops:
  7.2 190.2 %all-gather.3.cloned.1.call-start = ((), (), s32[]{:S(2)}) async-start(), calls=%async_computation.6 | async-start | bytes 3649536 | tf_op jit(solution)/shard_map/all_gather | solution.py:676
  13.0 239.8 %all-gather.5.cloned.1.call-start = ((), (), s32[]{:S(2)}) async-start(), calls=%async_computation.7 | async-start | bytes 9732096 | tf_op jit(solution)/shard_map/all_gather | solution.py:676
  19.6 14.4 %collective-permute-start = (bf16[1,24,3968]{2,1,0:T(8,128)(2,1)S(1)}, bf16[1,24,3968]{2,1,0:T(8,128)(2,1)S(1)}, u32[]{:S(2)}, u32[]{:S(2)}) collective-permute-start(bf16[1,24,3968]{2,1,0:T(8,128)(2,1)S(1)} %bitcast.145), channel_id=1, source_target_pairs={{0,4},{1,5},{2,6},{3,7},{4,0},{5,1},{6,2},{7,3},{8,12},{9,13},{10,... | collective-permute-start | bytes 571400 | tf_op jit(solution)/shard_map/ppermute | solution.py:590
  34.8 10.9 %collective-permute-start.1 = (bf16[2,24,3968]{2,1,0:T(8,128)(2,1)}, bf16[2,24,3968]{2,1,0:T(8,128)(2,1)S(1)}, u32[]{:S(2)}, u32[]{:S(2)}) collective-permute-start(bf16[2,24,3968]{2,1,0:T(8,128)(2,1)} %one_join.4.refs_0_), channel_id=1, source_target_pairs={{0,2},{1,3},{2,0},{3,1},{4,6},{5,7},{6,4},{7,5},{8,10},{9,11},{10,... | collective-permute-start | bytes 1142792 | tf_op jit(solution)/shard_map/ppermute | solution.py:590
  46.6 114.8 %all-to-all-start = ((bf16[8,256,768]{2,1,0:T(8,128)(2,1)}), bf16[8,256,768]{2,1,0:T(8,128)(2,1)S(1)}, u32[]{:S(2)}, u32[]{:S(2)}) async-start(bf16[8,256,768]{2,1,0:T(8,128)(2,1)} %pick_first.1), calls=%async_computation | async-start | bytes 6291456 | tf_op jit(solution)/shard_map/all_to_all | solution.py:843
  54.4 56.8 %collective-permute-start.2 = (bf16[4,24,3968]{2,1,0:T(8,128)(2,1)}, bf16[4,24,3968]{2,1,0:T(8,128)(2,1)S(1)}, u32[]{:S(2)}, u32[]{:S(2)}) collective-permute-start(bf16[4,24,3968]{2,1,0:T(8,128)(2,1)} %one_join.5.refs_0_), channel_id=1, source_target_pairs={{0,1},{1,0},{2,3},{3,2},{4,5},{5,4},{6,7},{7,6},{8,9},{9,8},{10,11... | collective-permute-start | bytes 2285576 | tf_op jit(solution)/shard_map/ppermute | solution.py:590
  113.5 35.3 %copy-start.24 = (bf16[16,64,768]{2,1,0:T(8,128)(2,1)S(1)}, bf16[16,64,768]{2,1,0:T(8,128)(2,1)}, u32[]{:S(2)}) copy-start(bf16[16,64,768]{2,1,0:T(8,128)(2,1)} %refs_1_.7) | copy-start | bytes 4718596
  113.5 32.2 %collective-permute-start.3 = (bf16[8,24,3968]{2,1,0:T(8,128)(2,1)}, bf16[8,24,3968]{2,1,0:T(8,128)(2,1)S(1)}, u32[]{:S(2)}, u32[]{:S(2)}) collective-permute-start(bf16[8,24,3968]{2,1,0:T(8,128)(2,1)} %one_join.6.refs_0_), channel_id=1, source_target_pairs={{0,16},{8,24},{16,0},{24,8},{1,17},{9,25},{17,1},{25,9},{2,18},{10... | collective-permute-start | bytes 4571144 | tf_op jit(solution)/shard_map/ppermute | solution.py:590
  148.7 10.1 %collective-permute-start.4 = (bf16[16,24,3968]{2,1,0:T(8,128)(2,1)}, bf16[16,24,3968]{2,1,0:T(8,128)(2,1)S(1)}, u32[]{:S(2)}, u32[]{:S(2)}) collective-permute-start(bf16[16,24,3968]{2,1,0:T(8,128)(2,1)} %one_join.7.refs_0_), channel_id=1, source_target_pairs={{0,8},{8,0},{16,24},{24,16},{1,9},{9,1},{17,25},{25,17},{2,10},{10... | collective-permute-start | bytes 9142280 | tf_op jit(solution)/shard_map/ppermute | solution.py:590
  161.5 35.9 %copy-start.5 = (bf16[8,256,768]{2,1,0:T(8,128)(2,1)}, bf16[8,256,768]{2,1,0:T(8,128)(2,1)S(1)}, u32[]{:S(2)}) copy-start(bf16[8,256,768]{2,1,0:T(8,128)(2,1)S(1)} %all-to-all-done.tok_ref.frm_ref.refs_7_.left0_ref) | copy-start | bytes 9437188
  161.5 73.5 %all-to-all-start.1 = ((bf16[8,128,768]{2,1,0:T(8,128)(2,1)}), bf16[8,128,768]{2,1,0:T(8,128)(2,1)}, u32[]{:S(2)}, u32[]{:S(2)}) async-start(bf16[8,128,768]{2,1,0:T(8,128)(2,1)} %pick_second.1), calls=%async_computation.1 | async-start | bytes 3145728 | tf_op jit(solution)/shard_map/all_to_all | solution.py:843
  172.7 80.1 %copy-start.51 = (f32[8,768]{1,0:T(8,128)}, f32[8,768]{1,0:T(8,128)S(1)}, u32[]{:S(2)}) copy-start(f32[8,768]{1,0:T(8,128)S(1)} %convert_bitcast_fusion.norm_ref.refs_9_) | copy-start | bytes 73732
  235.0 100.6 %all-to-all-start.2 = ((bf16[8,256,768]{2,1,0:T(8,128)(2,1)}), bf16[8,256,768]{2,1,0:T(8,128)(2,1)}, u32[]{:S(2)}, u32[]{:S(2)}) async-start(bf16[8,256,768]{2,1,0:T(8,128)(2,1)} %pick_third.1), calls=%async_computation.2 | async-start | bytes 6291456 | tf_op jit(solution)/shard_map/all_to_all | solution.py:843
  335.6 144.4 %all-to-all-start.3 = ((bf16[8,256,768]{2,1,0:T(8,128)(2,1)}), bf16[8,256,768]{2,1,0:T(8,128)(2,1)}, u32[]{:S(2)}, u32[]{:S(2)}) async-start(bf16[8,256,768]{2,1,0:T(8,128)(2,1)} %get-tuple-element.270), calls=%async_computation.3 | async-start | bytes 6291456 | tf_op jit(solution)/shard_map/all_to_all | solution.py:843
  391.3 23.3 %collective-permute-start.6 = (bf16[16,24,3072]{2,1,0:T(8,128)(2,1)}, bf16[16,24,3072]{2,1,0:T(8,128)(2,1)}, u32[]{:S(2)}, u32[]{:S(2)}) collective-permute-start(bf16[16,24,3072]{2,1,0:T(8,128)(2,1)} %bitcast.181), channel_id=1, source_target_pairs={{0,8},{8,0},{16,24},{24,16},{1,9},{9,1},{17,25},{25,17},{2,10},{10... | collective-permute-start | bytes 7077896 | tf_op jit(solution)/shard_map/ppermute | solution.py:590
  414.5 4.9 collective-permute-start.5
  422.2 32.8 %collective-permute-start.8 = (bf16[8,24,3072]{2,1,0:T(8,128)(2,1)}, bf16[8,24,3072]{2,1,0:T(8,128)(2,1)}, u32[]{:S(2)}, u32[]{:S(2)}) collective-permute-start(bf16[8,24,3072]{2,1,0:T(8,128)(2,1)} %bitcast.21), channel_id=1, source_target_pairs={{0,16},{8,24},{16,0},{24,8},{1,17},{9,25},{17,1},{25,9},{2,18},{10... | collective-permute-start | bytes 3538952 | tf_op jit(solution)/shard_map/ppermute | solution.py:590
  425.9 51.8 %collective-permute-start.7 = (bf16[8,24,3072]{2,1,0:T(8,128)(2,1)}, bf16[8,24,3072]{2,1,0:T(8,128)(2,1)S(1)}, u32[]{:S(2)}, u32[]{:S(2)}) collective-permute-start(bf16[8,24,3072]{2,1,0:T(8,128)(2,1)} %bitcast.16), channel_id=1, source_target_pairs={{0,16},{8,24},{16,0},{24,8},{1,17},{9,25},{17,1},{25,9},{2,18},{10... | collective-permute-start | bytes 3538952 | tf_op jit(solution)/shard_map/ppermute | solution.py:590
  479.9 29.9 %copy-start.6 = (bf16[8,256,768]{2,1,0:T(8,128)(2,1)S(1)}, bf16[8,256,768]{2,1,0:T(8,128)(2,1)}, u32[]{:S(2)}) copy-start(bf16[8,256,768]{2,1,0:T(8,128)(2,1)} %copy-done.5) | copy-start | bytes 9437188
  479.9 29.9 %copy-start.53 = (f32[8,768]{1,0:T(8,128)S(1)}, f32[8,768]{1,0:T(8,128)}, u32[]{:S(2)}) copy-start(f32[8,768]{1,0:T(8,128)} %copy-done.51) | copy-start | bytes 73732
  479.9 29.9 %copy-start.90 = (f32[6,4,256]{2,1,0:T(4,128)S(1)}, f32[6,4,256]{2,1,0:T(4,128)}, u32[]{:S(2)}) copy-start(f32[6,4,256]{2,1,0:T(4,128)} %get-tuple-element.353.refs_6_) | copy-start | bytes 73732
  479.9 154.0 %all-to-all-start.4 = ((bf16[8,256,768]{2,1,0:T(8,128)(2,1)}), bf16[8,256,768]{2,1,0:T(8,128)(2,1)}, u32[]{:S(2)}, u32[]{:S(2)}) async-start(bf16[8,256,768]{2,1,0:T(8,128)(2,1)} %get-tuple-element.348), calls=%async_computation.4 | async-start | bytes 6291456 | tf_op jit(solution)/shard_map/all_to_all | solution.py:843
  516.6 27.3 %copy-start.49 = (f32[512,768]{1,0:T(8,128)S(1)}, f32[512,768]{1,0:T(8,128)}, u32[]{:S(2)}) copy-start(f32[512,768]{1,0:T(8,128)} %get-tuple-element.359.grad_cross_ref) | copy-start | bytes 4718596
  516.6 27.3 %copy-start.91 = (f32[6,4,256]{2,1,0:T(4,128)S(1)}, f32[6,4,256]{2,1,0:T(4,128)}, u32[]{:S(2)}) copy-start(f32[6,4,256]{2,1,0:T(4,128)} %get-tuple-element.362.lse_ref) | copy-start | bytes 73732
  575.5 55.4 %collective-permute-start.9 = (bf16[16,24,3840]{2,1,0:T(8,128)(2,1)}, bf16[16,24,3840]{2,1,0:T(8,128)(2,1)}, u32[]{:S(2)}, u32[]{:S(2)}) collective-permute-start(bf16[16,24,3840]{2,1,0:T(8,128)(2,1)} %bitcast.168), channel_id=1, source_target_pairs={{0,8},{8,0},{16,24},{24,16},{1,9},{9,1},{17,25},{25,17},{2,10},{10... | collective-permute-start | bytes 8847368 | tf_op jit(solution)/shard_map/ppermute | solution.py:590
  596.5 31.7 %copy-start.18 = (bf16[2,192,2304]{2,1,0:T(8,128)(2,1)S(1)}, bf16[2,192,2304]{2,1,0:T(8,128)(2,1)}, u32[]{:S(2)}) copy-start(bf16[2,192,2304]{2,1,0:T(8,128)(2,1)} %get-tuple-element.386) | copy-start | bytes 5308420
  596.5 31.7 %collective-permute-start.10 = (bf16[16,24,2304]{2,1,0:T(8,128)(2,1)}, bf16[16,24,2304]{2,1,0:T(8,128)(2,1)S(1)}, u32[]{:S(2)}, u32[]{:S(2)}) collective-permute-start(bf16[16,24,2304]{2,1,0:T(8,128)(2,1)} %bitcast.171), channel_id=1, source_target_pairs={{0,8},{8,0},{16,24},{24,16},{1,9},{9,1},{17,25},{25,17},{2,10},{10... | collective-permute-start | bytes 5308424 | tf_op jit(solution)/shard_map/ppermute | solution.py:590
  596.8 16.5 %collective-permute-start.12 = (bf16[4,24,3072]{2,1,0:T(8,128)(2,1)}, bf16[4,24,3072]{2,1,0:T(8,128)(2,1)}, u32[]{:S(2)}, u32[]{:S(2)}) collective-permute-start(bf16[4,24,3072]{2,1,0:T(8,128)(2,1)} %bitcast.30), channel_id=1, source_target_pairs={{0,1},{1,0},{2,3},{3,2},{4,5},{5,4},{6,7},{7,6},{8,9},{9,8},{10,11... | collective-permute-start | bytes 1769480 | tf_op jit(solution)/shard_map/ppermute | solution.py:590
  598.5 26.8 %collective-permute-start.11 = (bf16[4,24,3072]{2,1,0:T(8,128)(2,1)}, bf16[4,24,3072]{2,1,0:T(8,128)(2,1)}, u32[]{:S(2)}, u32[]{:S(2)}) collective-permute-start(bf16[4,24,3072]{2,1,0:T(8,128)(2,1)} %bitcast.26), channel_id=1, source_target_pairs={{0,1},{1,0},{2,3},{3,2},{4,5},{5,4},{6,7},{7,6},{8,9},{9,8},{10,11... | collective-permute-start | bytes 1769480 | tf_op jit(solution)/shard_map/ppermute | solution.py:590
  633.9 35.5 %collective-permute-start.13 = (bf16[8,24,3840]{2,1,0:T(8,128)(2,1)}, bf16[8,24,3840]{2,1,0:T(8,128)(2,1)}, u32[]{:S(2)}, u32[]{:S(2)}) collective-permute-start(bf16[8,24,3840]{2,1,0:T(8,128)(2,1)} %bitcast.35), channel_id=1, source_target_pairs={{0,16},{8,24},{16,0},{24,8},{1,17},{9,25},{17,1},{25,9},{2,18},{10... | collective-permute-start | bytes 4423688 | tf_op jit(solution)/shard_map/ppermute | solution.py:590
  635.6 131.1 %all-to-all-start.5 = ((bf16[8,128,768]{2,1,0:T(8,128)(2,1)}), bf16[8,128,768]{2,1,0:T(8,128)(2,1)S(1)}, u32[]{:S(2)}, u32[]{:S(2)}) async-start(bf16[8,128,768]{2,1,0:T(8,128)(2,1)} %get-tuple-element.400), calls=%async_computation.5 | async-start | bytes 3145728 | tf_op jit(solution)/shard_map/all_to_all | solution.py:843
  650.3 36.6 %copy-start.55 = (bf16[1,8,24,2304]{3,2,1,0:T(8,128)(2,1)S(1)}, bf16[1,8,24,2304]{3,2,1,0:T(8,128)(2,1)}, u32[]{:S(2)}) copy-start(bf16[1,8,24,2304]{3,2,1,0:T(8,128)(2,1)} %copy-done.54) | copy-start | bytes 2654212
  650.3 36.5 %collective-permute-start.17 = (bf16[8,24,2304]{2,1,0:T(8,128)(2,1)}, bf16[8,24,2304]{2,1,0:T(8,128)(2,1)S(1)}, u32[]{:S(2)}, u32[]{:S(2)}) collective-permute-start(bf16[8,24,2304]{2,1,0:T(8,128)(2,1)} %bitcast.158), channel_id=1, source_target_pairs={{0,16},{8,24},{16,0},{24,8},{1,17},{9,25},{17,1},{25,9},{2,18},{10... | collective-permute-start | bytes 2654216 | tf_op jit(solution)/shard_map/ppermute | solution.py:590
  672.9 22.1 %collective-permute-start.14 = (bf16[4,24,3840]{2,1,0:T(8,128)(2,1)}, bf16[4,24,3840]{2,1,0:T(8,128)(2,1)S(1)}, u32[]{:S(2)}, u32[]{:S(2)}) collective-permute-start(bf16[4,24,3840]{2,1,0:T(8,128)(2,1)} %bitcast.54), channel_id=1, source_target_pairs={{0,1},{1,0},{2,3},{3,2},{4,5},{5,4},{6,7},{7,6},{8,9},{9,8},{10,11... | collective-permute-start | bytes 2211848 | tf_op jit(solution)/shard_map/ppermute | solution.py:590
  688.3 13.0 %collective-permute-start.18 = (bf16[4,24,2304]{2,1,0:T(8,128)(2,1)}, bf16[4,24,2304]{2,1,0:T(8,128)(2,1)S(1)}, u32[]{:S(2)}, u32[]{:S(2)}) collective-permute-start(bf16[4,24,2304]{2,1,0:T(8,128)(2,1)} %bitcast.66), channel_id=1, source_target_pairs={{0,1},{1,0},{2,3},{3,2},{4,5},{5,4},{6,7},{7,6},{8,9},{9,8},{10,11... | collective-permute-start | bytes 1327112 | tf_op jit(solution)/shard_map/ppermute | solution.py:590
  690.0 43.5 %collective-permute-start.23 = (bf16[2,24,3072]{2,1,0:T(8,128)(2,1)}, bf16[2,24,3072]{2,1,0:T(8,128)(2,1)}, u32[]{:S(2)}, u32[]{:S(2)}) collective-permute-start(bf16[2,24,3072]{2,1,0:T(8,128)(2,1)} %bitcast.45), channel_id=1, source_target_pairs={{0,2},{1,3},{2,0},{3,1},{4,6},{5,7},{6,4},{7,5},{8,10},{9,11},{10,... | collective-permute-start | bytes 884744 | tf_op jit(solution)/shard_map/ppermute | solution.py:590
  694.2 40.5 %collective-permute-start.21 = (bf16[2,24,3072]{2,1,0:T(8,128)(2,1)}, bf16[2,24,3072]{2,1,0:T(8,128)(2,1)S(1)}, u32[]{:S(2)}, u32[]{:S(2)}) collective-permute-start(bf16[2,24,3072]{2,1,0:T(8,128)(2,1)} %bitcast.159), channel_id=1, source_target_pairs={{0,2},{1,3},{2,0},{3,1},{4,6},{5,7},{6,4},{7,5},{8,10},{9,11},{10,... | collective-permute-start | bytes 884744 | tf_op jit(solution)/shard_map/ppermute | solution.py:590
  697.8 42.2 %collective-permute-start.15 = (bf16[2,24,3840]{2,1,0:T(8,128)(2,1)}, bf16[2,24,3840]{2,1,0:T(8,128)(2,1)S(1)}, u32[]{:S(2)}, u32[]{:S(2)}) collective-permute-start(bf16[2,24,3840]{2,1,0:T(8,128)(2,1)} %bitcast.57), channel_id=1, source_target_pairs={{0,2},{1,3},{2,0},{3,1},{4,6},{5,7},{6,4},{7,5},{8,10},{9,11},{10,... | collective-permute-start | bytes 1105928 | tf_op jit(solution)/shard_map/ppermute | solution.py:590
  702.1 36.1 %collective-permute-start.19 = (bf16[2,24,2304]{2,1,0:T(8,128)(2,1)}, bf16[2,24,2304]{2,1,0:T(8,128)(2,1)}, u32[]{:S(2)}, u32[]{:S(2)}) collective-permute-start(bf16[2,24,2304]{2,1,0:T(8,128)(2,1)} %bitcast.69), channel_id=1, source_target_pairs={{0,2},{1,3},{2,0},{3,1},{4,6},{5,7},{6,4},{7,5},{8,10},{9,11},{10,... | collective-permute-start | bytes 663560 | tf_op jit(solution)/shard_map/ppermute | solution.py:590
  707.1 1.2 collective-permute-start.25
  708.4 3.7 collective-permute-start.26
  712.2 3.7 collective-permute-start.27
  715.9 3.7 collective-permute-start.28
  719.6 12.6 %collective-permute-start.29 = (f32[1,1,192]{2,1,0:T(1,128)S(1)}, f32[1,1,192]{2,1,0:T(1,128)S(1)}, u32[]{:S(2)}, u32[]{:S(2)}) collective-permute-start(f32[1,1,192]{2,1,0:T(1,128)S(1)} %bitcast.166), channel_id=1, source_target_pairs={{0,4},{1,5},{2,6},{3,7},{4,0},{5,1},{6,2},{7,3},{8,12},{9,13},{10,... | collective-permute-start | bytes 2312 | tf_op jit(solution)/shard_map/ppermute | solution.py:590
  734.6 17.3 %collective-permute-start.24 = (bf16[1,24,3072]{2,1,0:T(8,128)(2,1)S(1)}, bf16[1,24,3072]{2,1,0:T(8,128)(2,1)S(1)}, u32[]{:S(2)}, u32[]{:S(2)}) collective-permute-start(bf16[1,24,3072]{2,1,0:T(8,128)(2,1)S(1)} %bitcast.161), channel_id=1, source_target_pairs={{0,4},{1,5},{2,6},{3,7},{4,0},{5,1},{6,2},{7,3},{8,12},{9,13},{10,... | collective-permute-start | bytes 442376 | tf_op jit(solution)/shard_map/ppermute | solution.py:590
  735.4 19.7 %collective-permute-start.22 = (bf16[1,24,3072]{2,1,0:T(8,128)(2,1)}, bf16[1,24,3072]{2,1,0:T(8,128)(2,1)S(1)}, u32[]{:S(2)}, u32[]{:S(2)}) collective-permute-start(bf16[1,24,3072]{2,1,0:T(8,128)(2,1)} %bitcast.78), channel_id=1, source_target_pairs={{0,4},{1,5},{2,6},{3,7},{4,0},{5,1},{6,2},{7,3},{8,12},{9,13},{10,... | collective-permute-start | bytes 442376 | tf_op jit(solution)/shard_map/ppermute | solution.py:590
  739.9 25.3 %collective-permute-start.20 = (bf16[1,24,2304]{2,1,0:T(8,128)(2,1)}, bf16[1,24,2304]{2,1,0:T(8,128)(2,1)S(1)}, u32[]{:S(2)}, u32[]{:S(2)}) collective-permute-start(bf16[1,24,2304]{2,1,0:T(8,128)(2,1)} %bitcast.72), channel_id=1, source_target_pairs={{0,4},{1,5},{2,6},{3,7},{4,0},{5,1},{6,2},{7,3},{8,12},{9,13},{10,... | collective-permute-start | bytes 331784 | tf_op jit(solution)/shard_map/ppermute | solution.py:590
  740.0 28.3 %collective-permute-start.16 = (bf16[1,24,3840]{2,1,0:T(8,128)(2,1)S(1)}, bf16[1,24,3840]{2,1,0:T(8,128)(2,1)S(1)}, u32[]{:S(2)}, u32[]{:S(2)}) collective-permute-start(bf16[1,24,3840]{2,1,0:T(8,128)(2,1)S(1)} %bitcast.160), channel_id=1, source_target_pairs={{0,4},{1,5},{2,6},{3,7},{4,0},{5,1},{6,2},{7,3},{8,12},{9,13},{10,... | collective-permute-start | bytes 552968 | tf_op jit(solution)/shard_map/ppermute | solution.py:590
  (88 other events, 628.0 us)
Sparse Core Ops, SparseCore 0:
  13.1 99.1 all-gather.2
  115.8 115.7 all-gather.4
